TPU v7x, 32 devices: a whole 2x2x4 slice. The times are simulated.
32 devices in a mesh: gx: 4 (over y, core), gy: 8 (over z, x).
Axes of the slice: x: 2, y: 2, z: 4, core: 2. Of those that a mesh axis runs over, the one named last changes fastest.
Arguments:
- source: float32 [256, 128, 128], P('gx', 'gy'), may hold values from -6 to 6
- diagonal: float32 [256, 128, 128], P('gx', 'gy'), may hold values from 6.05 to 7
- face_x: float32 [256, 128, 128], P('gx', 'gy'), may hold values from 0.1 to 1
- face_y: float32 [256, 128, 128], P('gx', 'gy'), may hold values from 0.1 to 1
- face_z: float32 [256, 128, 128], P('gx', 'gy'), may hold values from 0.1 to 1
- iterates: float32 [8, 256, 128, 128], P(None, 'gx', 'gy'), may hold values from -0.3 to 0.3
- labels: int32 [256, 128], P('gx', 'gy'), may hold values from 0 to 7
Outputs:
- new_iterates: float32 [8, 256, 128, 128], P(None, 'gx', 'gy')
- new_residual: float32 [256, 128, 128], P('gx', 'gy')
All inputs are finite; a program needn't handle non-finite values.
Results may differ from a plain program's by a relative error of at most 0.0003.
Values sent between devices are 32-bit elements; how exact they have to be, the bound alone decides.
No kernel may reach another device: no remote copies, remote signals or barrier semaphores. Data moves between devices by JAX's collectives and lax.ppermute only.
A program may use at most 128 MiB of HBM per device.

v0:
```python
import jax
import jax.numpy as jnp
from jax import lax
from jax.sharding import PartitionSpec as P

ENLARGE = 8


basis_shift = 6.5


def padded_2(block, sides, width):
    for axis, dim in sides:
        count = lax.axis_size(axis)
        forward = [(i, i + 1) for i in range(count - 1)]
        backward = [(target, source) for source, target in forward]
        low = lax.ppermute(
            lax.slice_in_dim(block, block.shape[dim] - width, None, axis=dim), axis, forward
        )
        high = lax.ppermute(lax.slice_in_dim(block, 0, width, axis=dim), axis, backward)
        block = jnp.concatenate([low, block, high], axis=dim)
    return block


def stencil(values, face_x, face_y, face_z, diagonal):
    centre = values[..., 1:-1, 1:-1, :]
    result = diagonal * centre
    result = (
        result
        - face_x[1:-1, 1:-1, :] * values[..., 2:, 1:-1, :]
        - face_x[:-2, 1:-1, :] * values[..., :-2, 1:-1, :]
    )
    result = (
        result
        - face_y[1:-1, 1:-1, :] * values[..., 1:-1, 2:, :]
        - face_y[1:-1, :-2, :] * values[..., 1:-1, :-2, :]
    )
    widths = [(0, 0)] * (centre.ndim - 1) + [(1, 1)]
    padded = jnp.pad(centre, widths)
    lower_face = jnp.pad(face_z[..., :-1], ((0, 0), (0, 0), (1, 0)))
    return result - face_z * padded[..., 2:] - lower_face * padded[..., :-2]


def finish(gram, project):
    highest = lax.Precision.HIGHEST
    lower = jnp.linalg.cholesky(gram)
    ident = jnp.eye(gram.shape[0], dtype=gram.dtype)
    inverse = lax.linalg.triangular_solve(lower, ident, left_side=True, lower=True)
    reduced = jnp.dot(jnp.dot(inverse, project, precision=highest), inverse.T, precision=highest)
    reduced = 0.5 * (reduced + reduced.T)
    target = jnp.dot(inverse, gram[:, :ENLARGE], precision=highest)
    factor = jnp.linalg.cholesky(reduced)
    middle = lax.linalg.triangular_solve(factor, target, left_side=True, lower=True)
    solved = lax.linalg.triangular_solve(
        factor, middle, left_side=True, lower=True, transpose_a=True
    )
    return jnp.dot(inverse.T, solved, precision=highest)


def shards(source, diagonal, face_x, face_y, face_z, iterates, labels):
    highest = lax.Precision.HIGHEST
    summed = jnp.sum(iterates, axis=0)
    columns = jnp.arange(ENLARGE, dtype=jnp.int32)
    near = (
        padded_2(summed, (("gx", 0), ("gy", 1)), 1),
        padded_2(face_x, (("gx", 0), ("gy", 1)), 1),
        padded_2(face_y, (("gx", 0), ("gy", 1)), 1),
    )
    near_sum, near_fx, near_fy = near
    residual = source - stencil(near_sum, near_fx, near_fy, face_z, diagonal)
    onehot = (labels[None] == columns[:, None, None]).astype(jnp.float32)
    blocks = residual[None] * onehot[..., None]
    blocks_wide = padded_2(blocks, (("gx", 1), ("gy", 2)), 1)
    applied = stencil(blocks_wide, near_fx, near_fy, face_z, diagonal)
    powered = applied - basis_shift * blocks
    powered_wide = padded_2(powered, (("gx", 1), ("gy", 2)), 1)
    second = stencil(powered_wide, near_fx, near_fy, face_z, diagonal)
    basis = jnp.concatenate([blocks, powered], axis=0)
    image = jnp.concatenate([applied, second], axis=0)
    gram_local = jnp.einsum("aijk,bijk->ab", basis, basis, precision=highest)
    project_local = jnp.einsum("aijk,bijk->ab", basis, image, precision=highest)
    gram = lax.psum(gram_local, ("gx", "gy"))
    project = lax.psum(project_local, ("gx", "gy"))
    coeffs = finish(gram, project)
    new_iterates = iterates + jnp.einsum("ab,aijk->bijk", coeffs, basis, precision=highest)
    carried = jnp.sum(coeffs, axis=1)
    new_residual = residual - jnp.einsum("a,aijk->ijk", carried, image, precision=highest)
    return (new_iterates, new_residual)


def solution(mesh):
    placed = (
        P("gx", "gy", None),
        P("gx", "gy", None),
        P("gx", "gy", None),
        P("gx", "gy", None),
        P("gx", "gy", None),
        P(None, "gx", "gy", None),
        P("gx", "gy"),
    )
    return jax.shard_map(
        shards,
        mesh=mesh,
        in_specs=placed,
        out_specs=(P(None, "gx", "gy", None), P("gx", "gy", None)),
        check_vma=False,
    )
```

profile of v0, /device:TPU:0, one launch (start us, length us, event | category | flops | bytes accessed | tf_op | source)
XLA Modules:
  0.0 177.3 jit_solution(15040397435094770270)
XLA Ops:
  0.7 2.7 %reduce_sum.18 = f32[64,16,128]{2,1,0:T(8,128)S(1)} reduce(f32[8,64,16,128]{3,2,1,0:T(8,128)} %param.13, f32[]{:T(128)} %constant.43.clone.1), dimensions={0}, to_apply=%region_0.0 | reduce | flops 917504 | bytes 4718596 | tf_op jit(solution)/shard_map/reduce_sum | solution.py:62
  4.7 3.0 %collective-permute-start.2 = (f32[1,16,128]{2,1,0:T(8,128)S(1)}, f32[1,16,128]{2,1,0:T(8,128)S(1)}, u32[]{:S(2)}, u32[]{:S(2)}) collective-permute-start(f32[1,16,128]{2,1,0:T(8,128)S(1)} %get-tuple-element.23), channel_id=1, source_target_pairs={{0,8},{8,16},{16,24},{1,9},{9,17},{17,25},{2,10},{10,18},{18,26},{... | collective-permute-start | bytes 24584 | tf_op jit(solution)/shard_map/ppermute | solution.py:17
  7.7 4.5 %collective-permute-start.4 = (f32[1,16,128]{2,1,0:T(8,128)S(1)}, f32[1,16,128]{2,1,0:T(8,128)S(1)}, u32[]{:S(2)}, u32[]{:S(2)}) collective-permute-start(f32[1,16,128]{2,1,0:T(8,128)S(1)} %get-tuple-element.22), channel_id=1, source_target_pairs={{0,8},{8,16},{16,24},{1,9},{9,17},{17,25},{2,10},{10,18},{18,26},{... | collective-permute-start | bytes 24584 | tf_op jit(solution)/shard_map/ppermute | solution.py:17
  13.6 3.0 %collective-permute-start.1 = (f32[1,16,128]{2,1,0:T(8,128)S(1)}, f32[1,16,128]{2,1,0:T(8,128)S(1)}, u32[]{:S(2)}, u32[]{:S(2)}) collective-permute-start(f32[1,16,128]{2,1,0:T(8,128)S(1)} %slice.156), channel_id=1, source_target_pairs={{0,8},{8,16},{16,24},{1,9},{9,17},{17,25},{2,10},{10,18},{18,26},{... | collective-permute-start | bytes 24584 | tf_op jit(solution)/shard_map/ppermute | solution.py:17
  18.1 4.5 %collective-permute-start.7 = (f32[66,1,128]{2,1,0:T(1,128)S(1)}, f32[66,1,128]{2,1,0:T(1,128)S(1)}, u32[]{:S(2)}, u32[]{:S(2)}) collective-permute-start(f32[66,1,128]{2,1,0:T(1,128)S(1)} %get-tuple-element.20), channel_id=1, source_target_pairs={{0,1},{1,2},{2,3},{3,4},{4,5},{5,6},{6,7},{8,9},{9,10},{10,11},{11... | collective-permute-start | bytes 101384 | tf_op jit(solution)/shard_map/ppermute | solution.py:17
  22.7 4.3 %collective-permute-start.6 = (f32[66,1,128]{2,1,0:T(1,128)S(1)}, f32[66,1,128]{2,1,0:T(1,128)S(1)}, u32[]{:S(2)}, u32[]{:S(2)}) collective-permute-start(f32[66,1,128]{2,1,0:T(1,128)S(1)} %slice.194), channel_id=1, source_target_pairs={{0,1},{1,2},{2,3},{3,4},{4,5},{5,6},{6,7},{8,9},{9,10},{10,11},{11... | collective-permute-start | bytes 101384 | tf_op jit(solution)/shard_map/ppermute | solution.py:17
  28.6 1.6 fusion.33
  32.8 3.0 %collective-permute-start.9 = (f32[8,1,16,128]{3,0,2,1:T(8,128)S(1)}, f32[8,1,16,128]{3,0,2,1:T(8,128)S(1)}, u32[]{:S(2)}, u32[]{:S(2)}) collective-permute-start(f32[8,1,16,128]{3,0,2,1:T(8,128)S(1)} %get-tuple-element.17), channel_id=1, source_target_pairs={{0,8},{8,16},{16,24},{1,9},{9,17},{17,25},{2,10},{10,18},{18,26},{... | collective-permute-start | bytes 196616 | tf_op jit(solution)/shard_map/ppermute | solution.py:17
  38.1 5.0 %collective-permute-start.11 = (f32[8,66,1,128]{3,0,2,1:T(8,128)S(1)}, f32[8,66,1,128]{3,0,2,1:T(8,128)S(1)}, u32[]{:S(2)}, u32[]{:S(2)}) collective-permute-start(f32[8,66,1,128]{3,0,2,1:T(8,128)S(1)} %get-tuple-element.14), channel_id=1, source_target_pairs={{0,1},{1,2},{2,3},{3,4},{4,5},{5,6},{6,7},{8,9},{9,10},{10,11},{11... | collective-permute-start | bytes 811016 | tf_op jit(solution)/shard_map/ppermute | solution.py:17
  43.4 4.0 %collective-permute-done.10 = f32[8,66,1,128]{3,0,2,1:T(8,128)S(1)} collective-permute-done((f32[8,66,1,128]{3,0,2,1:T(8,128)S(1)}, f32[8,66,1,128]{3,0,2,1:T(8,128)S(1)}, u32[]{:S(2)}, u32[]{:S(2)}) %collective-permute-start.10) | collective-permute-done | bytes 270368 | tf_op jit(solution)/shard_map/ppermute | solution.py:20
  47.4 7.2 %collective-permute-done.11 = f32[8,66,1,128]{3,0,2,1:T(8,128)S(1)} collective-permute-done((f32[8,66,1,128]{3,0,2,1:T(8,128)S(1)}, f32[8,66,1,128]{3,0,2,1:T(8,128)S(1)}, u32[]{:S(2)}, u32[]{:S(2)}) %collective-permute-start.11) | collective-permute-done | bytes 270368 | tf_op jit(solution)/shard_map/ppermute | solution.py:17
  54.6 7.5 %multiply_subtract_fusion = (f32[8,64,16,128]{3,0,2,1:T(8,128)S(1)}, f32[8,64,16,128]{3,0,2,1:T(8,128)S(1)}) fusion(f32[8,64,16]{0,2,1:T(8,128)S(1)} %fusion.43, f32[64,16,128]{2,1,0:T(8,128)S(1)} %get-tuple-element.9, f32[64,16,128]{2,1,0:T(8,128)S(1)} %pad.18, f32[8,64,16,128]{3,0,2,1:T(8,128)S(1)} %broadcast_multiply_fusion, ...), kind=kLoop, calls=%fused_computation.51 | loop fusion | flops 25165824 | bytes 17481728 | tf_op jit(solution)/shard_map/sub | solution.py:75
  63.4 3.0 %collective-permute-start.13 = (f32[8,1,16,128]{3,0,2,1:T(8,128)S(1)}, f32[8,1,16,128]{3,0,2,1:T(8,128)S(1)}, u32[]{:S(2)}, u32[]{:S(2)}) collective-permute-start(f32[8,1,16,128]{3,0,2,1:T(8,128)S(1)} %get-tuple-element.15), channel_id=1, source_target_pairs={{0,8},{8,16},{16,24},{1,9},{9,17},{17,25},{2,10},{10,18},{18,26},{... | collective-permute-start | bytes 196616 | tf_op jit(solution)/shard_map/ppermute | solution.py:17
  68.7 5.0 %collective-permute-start.15 = (f32[8,66,1,128]{3,0,2,1:T(8,128)S(1)}, f32[8,66,1,128]{3,0,2,1:T(8,128)S(1)}, u32[]{:S(2)}, u32[]{:S(2)}) collective-permute-start(f32[8,66,1,128]{3,0,2,1:T(8,128)S(1)} %get-tuple-element.12), channel_id=1, source_target_pairs={{0,1},{1,2},{2,3},{3,4},{4,5},{5,6},{6,7},{8,9},{9,10},{10,11},{11... | collective-permute-start | bytes 811016 | tf_op jit(solution)/shard_map/ppermute | solution.py:17
  73.7 11.2 %fusion.28 = f32[16,16]{0,1:T(8,128)S(1)} fusion(f32[8,64,16,128]{3,0,2,1:T(8,128)S(1)} %get-tuple-element.7, f32[8,64,16,128]{3,0,2,1:T(8,128)S(1)} %broadcast_multiply_fusion), kind=kOutput, calls=%fused_computation.55 | convolution fusion | flops 404750336 | bytes 8389632 | tf_op jit(solution)/shard_map/aijk,bijk->ab/dot_general | solution.py:80
  85.3 6.8 %fusion.10 = f32[8,64,16,128]{3,0,2,1:T(8,128)S(1)} fusion(f32[8,64,16,128]{3,0,2,1:T(8,128)S(1)} %get-tuple-element.7, f32[8,66,1,128]{3,0,2,1:T(8,128)S(1)} %collective-permute-done.15, f32[8,1,16,128]{3,0,2,1:T(8,128)S(1)} %collective-permute-done.12, f32[8,1,16,128]{3,0,2,1:T(8,128)S(1)} %collective-permute-done.13, ...), kind=kLoop, calls=%fused_computation.16 | loop fusion | flops 22020096 | bytes 12730368 | tf_op jit(solution)/shard_map/sub | solution.py:41
  92.1 1.9 %copy-done.5 = f32[8,64,16,128]{3,0,2,1:T(8,128)} copy-done((f32[8,64,16,128]{3,0,2,1:T(8,128)}, f32[8,64,16,128]{3,0,2,1:T(8,128)S(1)}, u32[]{:S(2)}) %copy-start.5) | copy-done | bytes 4194328
  94.1 10.4 %fusion.29 = f32[16,16]{1,0:T(8,128)S(1)} fusion(f32[8,64,16,128]{3,0,2,1:T(8,128)S(1)} %fusion.10, f32[8,64,16,128]{3,0,2,1:T(8,128)S(1)} %get-tuple-element.8, f32[8,64,16,128]{3,0,2,1:T(8,128)S(1)} %get-tuple-element.7, f32[8,64,16,128]{3,0,2,1:T(8,128)S(1)} %broadcast_multiply_fusion), kind=kOutput, calls=%fused_computation.56 | convolution fusion | flops 406847488 | bytes 16778240 | tf_op jit(solution)/shard_map/aijk,bijk->ab/dot_general | solution.py:81
  104.5 44.6 %all-reduce.4 = (f32[16,16]{0,1:T(8,128)S(1)}, f32[16,16]{1,0:T(8,128)S(1)}) all-reduce(f32[16,16]{0,1:T(8,128)S(1)} %fusion.28, f32[16,16]{1,0:T(8,128)S(1)} %fusion.29), channel_id=1, replica_groups=mesh['gx'=4,'gy'=8] {'gx','gy'}, use_global_device_ids=true, to_apply=%region_1.2 | all-reduce | flops 512 | bytes 4096 | tf_op jit(solution)/shard_map/psum | solution.py:82
  149.1 1.5 cholesky.44
  153.9 1.5 cholesky.55
  158.5 6.6 %fusion = f32[1,64,16,128]{3,0,2,1:T(1,128)S(1)} fusion(f32[8,64,16,128]{3,0,2,1:T(8,128)} %copy-done.5, f32[8,64,16,128]{3,0,2,1:T(8,128)} %copy-done.4, f32[16]{0:T(128)S(1)} %get-tuple-element.25), kind=kOutput, calls=%fused_computation.6 | convolution fusion | flops 27262976 | bytes 8912960 | tf_op jit(solution)/shard_map/a,aijk->ijk/dot_general | solution.py:87
  166.0 8.6 %copy_add_fusion = f32[8,64,16,128]{3,0,2,1:T(8,128)S(1)} fusion(f32[8,64,16,128]{3,2,1,0:T(8,128)} %param.13, f32[8,64,16,128]{3,0,2,1:T(8,128)S(1)} %copy-done.3, f32[8,64,16,128]{3,0,2,1:T(8,128)S(1)} %copy-done.1, f32[16,8]{0,1:T(8,128)S(1)} %get-tuple-element.26), kind=kOutput, calls=%fused_computation.50 | convolution fusion | flops 204472320 | bytes 16777728 | tf_op jit(solution)/shard_map/ab,aijk->bijk/dot_general | solution.py:85
  174.6 2.8 %copy.15 = f32[8,64,16,128]{3,2,1,0:T(8,128)} copy(f32[8,64,16,128]{3,0,2,1:T(8,128)S(1)} %copy_add_fusion) | data formatting | bytes 8388608
  (81 shorter events, 22.0 us)
Async XLA Ops:
  0.6 12.9 %copy-start.8 = (f32[64,16,128]{2,1,0:T(8,128)S(1)}, f32[64,16,128]{2,1,0:T(8,128)}, u32[]{:S(2)}) copy-start(f32[64,16,128]{2,1,0:T(8,128)} %param.10) | copy-start | bytes 1572868
  0.7 15.9 %copy-start.10 = (s32[64,16]{0,1:T(8,128)S(1)}, s32[64,16]{0,1:T(8,128)}, u32[]{:S(2)}) copy-start(s32[64,16]{0,1:T(8,128)} %param.14) | copy-start | bytes 12292
  0.7 28.0 %copy-start.6 = (f32[64,16,128]{2,1,0:T(8,128)S(1)}, f32[64,16,128]{2,1,0:T(8,128)}, u32[]{:S(2)}) copy-start(f32[64,16,128]{2,1,0:T(8,128)} %param.12) | copy-start | bytes 1572868
  0.7 28.0 %copy-start.9 = (f32[64,16,128]{2,1,0:T(8,128)S(1)}, f32[64,16,128]{2,1,0:T(8,128)}, u32[]{:S(2)}) copy-start(f32[64,16,128]{2,1,0:T(8,128)} %param.9) | copy-start | bytes 1572868
  3.4 13.3 %collective-permute-start = (f32[1,16,128]{2,1,0:T(8,128)S(1)}, f32[1,16,128]{2,1,0:T(8,128)S(1)}, u32[]{:S(2)}, u32[]{:S(2)}) collective-permute-start(f32[1,16,128]{2,1,0:T(8,128)S(1)} %get-tuple-element.24), channel_id=1, source_target_pairs={{8,0},{16,8},{24,16},{9,1},{17,9},{25,17},{10,2},{18,10},{26,18},{... | collective-permute-start | bytes 24584 | tf_op jit(solution)/shard_map/ppermute | solution.py:20
  4.7 12.0 %collective-permute-start.2 = (f32[1,16,128]{2,1,0:T(8,128)S(1)}, f32[1,16,128]{2,1,0:T(8,128)S(1)}, u32[]{:S(2)}, u32[]{:S(2)}) collective-permute-start(f32[1,16,128]{2,1,0:T(8,128)S(1)} %get-tuple-element.23), channel_id=1, source_target_pairs={{0,8},{8,16},{16,24},{1,9},{9,17},{17,25},{2,10},{10,18},{18,26},{... | collective-permute-start | bytes 24584 | tf_op jit(solution)/shard_map/ppermute | solution.py:17
  7.7 14.9 %collective-permute-start.4 = (f32[1,16,128]{2,1,0:T(8,128)S(1)}, f32[1,16,128]{2,1,0:T(8,128)S(1)}, u32[]{:S(2)}, u32[]{:S(2)}) collective-permute-start(f32[1,16,128]{2,1,0:T(8,128)S(1)} %get-tuple-element.22), channel_id=1, source_target_pairs={{0,8},{8,16},{16,24},{1,9},{9,17},{17,25},{2,10},{10,18},{18,26},{... | collective-permute-start | bytes 24584 | tf_op jit(solution)/shard_map/ppermute | solution.py:17
  12.2 10.4 %collective-permute-start.5 = (f32[1,16,128]{2,1,0:T(8,128)S(1)}, f32[1,16,128]{2,1,0:T(8,128)S(1)}, u32[]{:S(2)}, u32[]{:S(2)}) collective-permute-start(f32[1,16,128]{2,1,0:T(8,128)S(1)} %get-tuple-element.21), channel_id=1, source_target_pairs={{8,0},{16,8},{24,16},{9,1},{17,9},{25,17},{10,2},{18,10},{26,18},{... | collective-permute-start | bytes 24584 | tf_op jit(solution)/shard_map/ppermute | solution.py:20
  13.6 13.7 %collective-permute-start.1 = (f32[1,16,128]{2,1,0:T(8,128)S(1)}, f32[1,16,128]{2,1,0:T(8,128)S(1)}, u32[]{:S(2)}, u32[]{:S(2)}) collective-permute-start(f32[1,16,128]{2,1,0:T(8,128)S(1)} %slice.156), channel_id=1, source_target_pairs={{0,8},{8,16},{16,24},{1,9},{9,17},{17,25},{2,10},{10,18},{18,26},{... | collective-permute-start | bytes 24584 | tf_op jit(solution)/shard_map/ppermute | solution.py:17
  16.8 10.5 %collective-permute-start.3 = (f32[66,1,128]{2,1,0:T(1,128)S(1)}, f32[66,1,128]{2,1,0:T(1,128)S(1)}, u32[]{:S(2)}, u32[]{:S(2)}) collective-permute-start(f32[66,1,128]{2,1,0:T(1,128)S(1)} %get-tuple-element.19), channel_id=1, source_target_pairs={{1,0},{2,1},{3,2},{4,3},{5,4},{6,5},{7,6},{9,8},{10,9},{11,10},{12... | collective-permute-start | bytes 101384 | tf_op jit(solution)/shard_map/ppermute | solution.py:20
  18.1 9.2 %collective-permute-start.7 = (f32[66,1,128]{2,1,0:T(1,128)S(1)}, f32[66,1,128]{2,1,0:T(1,128)S(1)}, u32[]{:S(2)}, u32[]{:S(2)}) collective-permute-start(f32[66,1,128]{2,1,0:T(1,128)S(1)} %get-tuple-element.20), channel_id=1, source_target_pairs={{0,1},{1,2},{2,3},{3,4},{4,5},{5,6},{6,7},{8,9},{9,10},{10,11},{11... | collective-permute-start | bytes 101384 | tf_op jit(solution)/shard_map/ppermute | solution.py:17
  22.7 5.9 %collective-permute-start.6 = (f32[66,1,128]{2,1,0:T(1,128)S(1)}, f32[66,1,128]{2,1,0:T(1,128)S(1)}, u32[]{:S(2)}, u32[]{:S(2)}) collective-permute-start(f32[66,1,128]{2,1,0:T(1,128)S(1)} %slice.194), channel_id=1, source_target_pairs={{0,1},{1,2},{2,3},{3,4},{4,5},{5,6},{6,7},{8,9},{9,10},{10,11},{11... | collective-permute-start | bytes 101384 | tf_op jit(solution)/shard_map/ppermute | solution.py:17
  31.5 60.6 %copy-start = (f32[8,64,16,128]{3,0,2,1:T(8,128)}, f32[8,64,16,128]{3,0,2,1:T(8,128)S(1)}, u32[]{:S(2)}) copy-start(f32[8,64,16,128]{3,0,2,1:T(8,128)S(1)} %broadcast_multiply_fusion) | copy-start | bytes 12582916
  31.5 4.3 %collective-permute-start.8 = (f32[8,1,16,128]{3,0,2,1:T(8,128)S(1)}, f32[8,1,16,128]{3,0,2,1:T(8,128)S(1)}, u32[]{:S(2)}, u32[]{:S(2)}) collective-permute-start(f32[8,1,16,128]{3,0,2,1:T(8,128)S(1)} %get-tuple-element.18), channel_id=1, source_target_pairs={{8,0},{16,8},{24,16},{9,1},{17,9},{25,17},{10,2},{18,10},{26,18},{... | collective-permute-start | bytes 196616 | tf_op jit(solution)/shard_map/ppermute | solution.py:20
  32.8 3.9 %collective-permute-start.9 = (f32[8,1,16,128]{3,0,2,1:T(8,128)S(1)}, f32[8,1,16,128]{3,0,2,1:T(8,128)S(1)}, u32[]{:S(2)}, u32[]{:S(2)}) collective-permute-start(f32[8,1,16,128]{3,0,2,1:T(8,128)S(1)} %get-tuple-element.17), channel_id=1, source_target_pairs={{0,8},{8,16},{16,24},{1,9},{9,17},{17,25},{2,10},{10,18},{18,26},{... | collective-permute-start | bytes 196616 | tf_op jit(solution)/shard_map/ppermute | solution.py:17
  36.8 10.6 %collective-permute-start.10 = (f32[8,66,1,128]{3,0,2,1:T(8,128)S(1)}, f32[8,66,1,128]{3,0,2,1:T(8,128)S(1)}, u32[]{:S(2)}, u32[]{:S(2)}) collective-permute-start(f32[8,66,1,128]{3,0,2,1:T(8,128)S(1)} %get-tuple-element.13), channel_id=1, source_target_pairs={{1,0},{2,1},{3,2},{4,3},{5,4},{6,5},{7,6},{9,8},{10,9},{11,10},{12... | collective-permute-start | bytes 811016 | tf_op jit(solution)/shard_map/ppermute | solution.py:20
  38.1 16.6 %collective-permute-start.11 = (f32[8,66,1,128]{3,0,2,1:T(8,128)S(1)}, f32[8,66,1,128]{3,0,2,1:T(8,128)S(1)}, u32[]{:S(2)}, u32[]{:S(2)}) collective-permute-start(f32[8,66,1,128]{3,0,2,1:T(8,128)S(1)} %get-tuple-element.14), channel_id=1, source_target_pairs={{0,1},{1,2},{2,3},{3,4},{4,5},{5,6},{6,7},{8,9},{9,10},{10,11},{11... | collective-permute-start | bytes 811016 | tf_op jit(solution)/shard_map/ppermute | solution.py:17
  62.1 30.0 %copy-start.2 = (f32[8,64,16,128]{3,0,2,1:T(8,128)}, f32[8,64,16,128]{3,0,2,1:T(8,128)S(1)}, u32[]{:S(2)}) copy-start(f32[8,64,16,128]{3,0,2,1:T(8,128)S(1)} %get-tuple-element.7) | copy-start | bytes 12582916
  62.1 30.0 %copy-start.4 = (f32[8,64,16,128]{3,0,2,1:T(8,128)}, f32[8,64,16,128]{3,0,2,1:T(8,128)S(1)}, u32[]{:S(2)}) copy-start(f32[8,64,16,128]{3,0,2,1:T(8,128)S(1)} %get-tuple-element.8) | copy-start | bytes 12582916
  62.1 4.3 %collective-permute-start.12 = (f32[8,1,16,128]{3,0,2,1:T(8,128)S(1)}, f32[8,1,16,128]{3,0,2,1:T(8,128)S(1)}, u32[]{:S(2)}, u32[]{:S(2)}) collective-permute-start(f32[8,1,16,128]{3,0,2,1:T(8,128)S(1)} %get-tuple-element.16), channel_id=1, source_target_pairs={{8,0},{16,8},{24,16},{9,1},{17,9},{25,17},{10,2},{18,10},{26,18},{... | collective-permute-start | bytes 196616 | tf_op jit(solution)/shard_map/ppermute | solution.py:20
  63.4 3.9 %collective-permute-start.13 = (f32[8,1,16,128]{3,0,2,1:T(8,128)S(1)}, f32[8,1,16,128]{3,0,2,1:T(8,128)S(1)}, u32[]{:S(2)}, u32[]{:S(2)}) collective-permute-start(f32[8,1,16,128]{3,0,2,1:T(8,128)S(1)} %get-tuple-element.15), channel_id=1, source_target_pairs={{0,8},{8,16},{16,24},{1,9},{9,17},{17,25},{2,10},{10,18},{18,26},{... | collective-permute-start | bytes 196616 | tf_op jit(solution)/shard_map/ppermute | solution.py:17
  67.4 17.5 %collective-permute-start.14 = (f32[8,66,1,128]{3,0,2,1:T(8,128)S(1)}, f32[8,66,1,128]{3,0,2,1:T(8,128)S(1)}, u32[]{:S(2)}, u32[]{:S(2)}) collective-permute-start(f32[8,66,1,128]{3,0,2,1:T(8,128)S(1)} %get-tuple-element.11), channel_id=1, source_target_pairs={{1,0},{2,1},{3,2},{4,3},{5,4},{6,5},{7,6},{9,8},{10,9},{11,10},{12... | collective-permute-start | bytes 811016 | tf_op jit(solution)/shard_map/ppermute | solution.py:20
  68.7 16.6 %collective-permute-start.15 = (f32[8,66,1,128]{3,0,2,1:T(8,128)S(1)}, f32[8,66,1,128]{3,0,2,1:T(8,128)S(1)}, u32[]{:S(2)}, u32[]{:S(2)}) collective-permute-start(f32[8,66,1,128]{3,0,2,1:T(8,128)S(1)} %get-tuple-element.12), channel_id=1, source_target_pairs={{0,1},{1,2},{2,3},{3,4},{4,5},{5,6},{6,7},{8,9},{9,10},{10,11},{11... | collective-permute-start | bytes 811016 | tf_op jit(solution)/shard_map/ppermute | solution.py:17
  158.5 7.5 %copy-start.1 = (f32[8,64,16,128]{3,0,2,1:T(8,128)S(1)}, f32[8,64,16,128]{3,0,2,1:T(8,128)}, u32[]{:S(2)}) copy-start(f32[8,64,16,128]{3,0,2,1:T(8,128)} %copy-done) | copy-start | bytes 12582916
  (3 other events, 16.5 us)
where the time goes:
time: 178 us; the launch traced here: 177 us
  starting transfers between devices  44.6 us (25%)
  blocking collectives  44.6 us (25%)
  matrix products  37.9 us (21%)
  other arithmetic  29 us (16%)
  waiting for transfers between devices  14.8 us (8%)
  local copies, waits for them, and re-layouts  5.36 us (3%)
    psum x1, blocking collectives, shards(): gram = lax.psum(gram_local, ('gx', 'gy'))  44.6 us
    ppermute x9, starting transfers between devices, padded_2(): lax.ppermute(lax.slice_in_dim(block, block.shape[dim] - width, None, axis...  35.5 us
    dot_general x1, matrix products, shards(): gram_local = jnp.einsum('aijk,bijk->ab', basis, basis, precision=highest)  11.2 us
    ppermute x9, waiting for transfers between devices, padded_2(): lax.ppermute(lax.slice_in_dim(block, block.shape[dim] - width, None, axis...  10.7 us
    dot_general x1, matrix products, shards(): project_local = jnp.einsum('aijk,bijk->ab', basis, image, precision=highest)  10.4 us
    ppermute x7, starting transfers between devices, padded_2(): lax.ppermute(lax.slice_in_dim(block, 0, width, axis=dim), axis, backward)  9.04 us
    dot_general x1, matrix products, shards(): jnp.einsum('ab,aijk->bijk', coeffs, basis, precision=highest)  8.56 us
    sub x1, other arithmetic, shards(): powered = applied - basis_shift * blocks  7.45 us
  transfers between devices with their start and end apart: 16, of which 6 were waited for; matrix products, arithmetic and copies ran while one was open for 7% of the time, Pallas kernels for 0%

commit v1 on v0

v1 whole, which is shorter than its diff:
```python
import functools

import jax
import jax.numpy as jnp
from jax import lax
from jax.experimental import pallas as pl
from jax.experimental.pallas import tpu as pltpu
from jax.sharding import PartitionSpec as P

ENLARGE = 8
SHIFT = 6.5
F32 = jnp.float32
HIGHEST = lax.Precision.HIGHEST
PAIRS = [(j, k) for j in range(ENLARGE) for k in range(j, ENLARGE)]
GHOST = 2
XROWS = 16
VMEM_LIMIT = 40 * 1024 * 1024


def iota(shape, dim):
    return lax.broadcasted_iota(jnp.int32, shape, dim)


def even_pairs(count):
    return [(i, i ^ 1) for i in range(count) if (i ^ 1) < count]


def odd_pairs(count):
    return [(i, ((i - 1) ^ 1) + 1) for i in range(1, count) if ((i - 1) ^ 1) + 1 < count]


def whole(count):
    return [pl.BlockSpec(memory_space=pltpu.VMEM)] * count


def params():
    return pltpu.CompilerParams(vmem_limit_bytes=VMEM_LIMIT)


def sum_kernel(steps, it_ref, *refs):
    lows, highs = refs[0:6], refs[6:12]
    s_ref, even_ref, odd_ref = refs[12:]
    step = pl.program_id(0)
    total = it_ref[0]
    for j in range(1, ENLARGE):
        total = total + it_ref[j]
    s_ref[...] = total
    width = total.shape[0]

    def pack(ref, at, values):
        ref[at : at + values.shape[0]] = values

    def put(dest, low):
        src, dg, fx, fy, fz, lb = lows if low else highs
        if low:
            take = lambda a, n: a[0:n]
        else:
            take = lambda a, n: a[width - n : width]
        pack(dest, 0, take(total, 3))
        pack(dest, 3, take(fx, 3))
        at = 6
        for field in (src, dg, fy, fz, lb):
            pack(dest, at, take(field, 2))
            at += 2

    parity = lax.rem(lax.axis_index("gx"), 2)

    @pl.when(jnp.logical_and(step == 0, parity == 0))
    def _():
        put(odd_ref, True)

    @pl.when(jnp.logical_and(step == 0, parity == 1))
    def _():
        put(even_ref, True)

    @pl.when(jnp.logical_and(step == steps - 1, parity == 0))
    def _():
        put(even_ref, False)

    @pl.when(jnp.logical_and(step == steps - 1, parity == 1))
    def _():
        put(odd_ref, False)


def sum_and_edges(iterates, fields):
    _, nx, ny, nz = iterates.shape
    width = 8
    steps = nx // width
    block = (width, ny, nz)
    low = pl.BlockSpec(block, lambda i: (0, 0, 0))
    high = pl.BlockSpec(block, lambda i: (steps - 1, 0, 0))
    edge = jax.ShapeDtypeStruct((XROWS, ny, nz), F32)
    edge_spec = pl.BlockSpec((XROWS, ny, nz), lambda i: (0, 0, 0))
    return pl.pallas_call(
        functools.partial(sum_kernel, steps),
        grid=(steps,),
        in_specs=[pl.BlockSpec((ENLARGE,) + block, lambda i: (0, i, 0, 0))] + [low] * 6 + [high] * 6,
        out_specs=[pl.BlockSpec(block, lambda i: (i, 0, 0)), edge_spec, edge_spec],
        out_shape=[jax.ShapeDtypeStruct((nx, ny, nz), F32), edge, edge],
        compiler_params=params(),
        name="sum_and_edges",
    )(iterates, *fields, *fields)


def partial_kernel(
    nx, ny, xpad, gx, gy,
    s_in, src_in, dg_in, fx_in, fy_in, fz_in, lb_in, xe_ref, xo_ref,
    t_out, s_out, fx_out, fy_out, dg_out, fz_out, lb_out, ye_ref, yo_ref,
    src_ext,
):
    g = GHOST
    nz = s_in.shape[-1]
    lane = iota((ny, nz), 1)
    row = iota((ny, nz), 0)
    even_x = lax.rem(lax.axis_index("gx"), 2) == 0
    last_x = lax.axis_index("gx") == gx - 1
    last_y = lax.axis_index("gy") == gy - 1

    def rows(i):
        return pl.ds(pl.multiple_of(i * ny, ny), ny)

    def low(r):
        return jnp.where(even_x, xo_ref[r], xe_ref[r])

    def high(r):
        return jnp.where(even_x, xe_ref[r], xo_ref[r])

    top = jnp.logical_and(last_y, row == ny - 1)

    def fy_of(values):
        return jnp.where(top, 0.0, values)

    def fz_of(values):
        return jnp.where(lane == nz - 1, 0.0, values)

    s_low = [low(r) for r in range(3)]
    s_high = [high(r) for r in range(3)]
    fx_low = [low(3 + r) for r in range(3)]
    fx_high = [high(3 + r) for r in range(3)]
    for e in range(2):
        for side, at, pick in ((0, e, low), (1, g + nx + e, high)):
            s_out[rows(at)] = s_low[1 + e] if side == 0 else s_high[e]
            fx_out[rows(at)] = fx_low[1 + e] if side == 0 else fx_high[e]
            src_ext[rows(at)] = pick(6 + e)
            dg_out[rows(at)] = pick(8 + e)
            fy_out[rows(at)] = fy_of(pick(10 + e))
            fz_out[rows(at)] = fz_of(pick(12 + e))
            lb_out[rows(at)] = pick(14 + e)
    zero = jnp.zeros((ny, nz), F32)
    for at in range(nx + 2 * g, xpad):
        for ref in (t_out, s_out, fx_out, fy_out, dg_out, fz_out, lb_out):
            ref[rows(at)] = zero

    def copy(i, carry):
        at = rows(i + g)
        s_out[at] = s_in[i]
        fx_out[at] = fx_in[i]
        dg_out[at] = dg_in[i]
        fy_out[at] = fy_of(fy_in[i])
        fz_out[at] = fz_of(fz_in[i])
        lb_out[at] = lb_in[i]
        src_ext[at] = src_in[i]
        return carry

    lax.fori_loop(0, nx, copy, 0, unroll=4)

    @pl.when(last_x)
    def _():
        fx_out[rows(g + nx - 1)] = zero

    def partial(at, s, sp, sm, fxp, fxm):
        fy = fy_out[at]
        fz = fz_out[at]
        fys = fy * s
        ys = jnp.where(row == ny - 1, 0.0, fy * pltpu.roll(s, ny - 1, 0))
        ys = ys + jnp.where(row == 0, 0.0, pltpu.roll(fys, 1, 0))
        zs = fz * pltpu.roll(s, nz - 1, 1) + pltpu.roll(fz * s, 1, 1)
        return src_ext[at] - (dg_out[at] * s - fxp * sp - fxm * sm - ys - zs)

    def body(i, carry):
        at = rows(i)
        t_out[at] = partial(
            at, s_out[at], s_out[rows(i + 1)], s_out[rows(i - 1)], fx_out[at], fx_out[rows(i - 1)]
        )
        return carry

    at = rows(0)
    t_out[at] = partial(at, s_out[at], s_out[rows(1)], s_low[0], fx_out[at], fx_low[0])
    end = nx + 2 * g - 1
    at = rows(end)
    t_out[at] = partial(at, s_out[at], s_high[2], s_out[rows(end - 1)], fx_out[at], fx_out[rows(end - 1)])
    lax.fori_loop(1, end, body, 0, unroll=2)

    even_y = lax.rem(lax.axis_index("gy"), 2) == 0

    def pack(dest, is_high):
        first = jnp.where(is_high, ny - 1, 0)
        second = jnp.where(is_high, ny - 2, 1)
        between = jnp.where(is_high, ny - 2, 0)

        def line(ref, y):
            return ref[pl.ds(y, xpad, stride=ny), :]

        blocks = (
            line(t_out, first),
            line(s_out, first),
            line(fy_out, first),
            line(fx_out, first),
            line(fy_out, between) * line(t_out, second),
            line(dg_out, first),
            line(fz_out, first),
        )
        for b, values in enumerate(blocks):
            dest[b * xpad : (b + 1) * xpad] = values
        spot = iota((xpad, nz), 0) == iota((xpad, nz), 1)
        one = jnp.sum(jnp.where(spot, line(lb_out, first), 0.0), axis=0, keepdims=True)
        two = jnp.sum(jnp.where(spot, line(lb_out, second), 0.0), axis=0, keepdims=True)
        which = iota((8, nz), 0)
        dest[7 * xpad : 7 * xpad + 8] = jnp.where(which == 0, one, jnp.where(which == 1, two, 0.0))

    pack(ye_ref, even_y)
    pack(yo_ref, jnp.logical_not(even_y))


def partial_and_edges(total, fields, xe, xo, xpad, gx, gy):
    nx, ny, nz = total.shape
    ext = jax.ShapeDtypeStruct((xpad * ny, nz), F32)
    pack = jax.ShapeDtypeStruct((7 * xpad + 8, nz), F32)
    return pl.pallas_call(
        functools.partial(partial_kernel, nx, ny, xpad, gx, gy),
        in_specs=whole(9),
        out_specs=whole(9),
        out_shape=[ext] * 7 + [pack] * 2,
        scratch_shapes=[pltpu.VMEM((xpad * ny, nz), F32)],
        compiler_params=params(),
        name="partial_and_edges",
    )(total, *fields, xe, xo)


def powers_kernel(
    nx, ny, xpad, devices,
    t_ref, s_ref, fx_ref, fy_ref, dg_ref, fz_ref, lb_ref, ye_ref, yo_ref,
    p_out, q_out, r_out, gram_out,
    rex, fyx, lbx, pex, rhalo, rin, lab1, lab2, labin, accs,
):
    g = GHOST
    nz = t_ref.shape[-1]
    ext = nx + 2 * g
    pitch = ny + 16
    even_y = lax.rem(lax.axis_index("gy"), 2) == 0

    def at16(i):
        return pl.ds(pl.multiple_of(i * ny, ny), ny)

    def copy(i, carry):
        base = pl.multiple_of(i * pitch + 8, 8)
        rex[pl.ds(base, ny)] = t_ref[at16(i)]
        fyx[pl.ds(base, ny)] = fy_ref[at16(i)]
        lbx[pl.ds(base, ny)] = lb_ref[at16(i)]
        return carry

    lax.fori_loop(0, xpad, copy, 0, unroll=4)

    def packed(side, b, start=0, count=None):
        count = xpad if count is None else count
        span = slice(b * xpad + start, b * xpad + start + count)
        e, o = ye_ref[span], yo_ref[span]
        return jnp.where(even_y, o, e) if side == 0 else jnp.where(even_y, e, o)

    for side in range(2):
        inner = 0 if side == 0 else ny - 1
        outer_at = 7 if side == 0 else 8 + ny
        t1, s1 = packed(side, 0), packed(side, 1)
        face = packed(side, 2) if side == 0 else fy_ref[pl.ds(ny - 1, xpad, stride=ny), :]
        s_in = s_ref[pl.ds(inner, xpad, stride=ny), :]
        t_in = t_ref[pl.ds(inner, xpad, stride=ny), :]
        outer = t1 + face * s_in
        inner_r = t_in + face * s1
        rhalo[side * xpad : (side + 1) * xpad] = outer
        rin[side * xpad : (side + 1) * xpad] = -face * inner_r
        rex[pl.ds(outer_at, xpad, stride=pitch), :] = outer
        rex[pl.ds(8 + inner, xpad, stride=pitch), :] = inner_r
        if side == 0:
            fyx[pl.ds(outer_at, xpad, stride=pitch), :] = face
        labels = packed(side, 7, 0, 8)
        spot = iota((xpad, nz), 0) == iota((xpad, nz), 1)
        for r, dest in ((0, lab1), (1, lab2)):
            column = jnp.sum(jnp.where(spot, labels[r : r + 1], 0.0), axis=1, keepdims=True)
            dest[side * xpad : (side + 1) * xpad] = jnp.broadcast_to(column, (xpad, nz))
        lbx[pl.ds(outer_at, xpad, stride=pitch), :] = lab1[side * xpad : (side + 1) * xpad]
        labin[side * xpad : (side + 1) * xpad] = lb_ref[pl.ds(inner, xpad, stride=ny), :]

    def spread(parts):
        fields = []
        for j in range(ENLARGE):
            total = None
            for values, label in parts:
                term = jnp.where(label == float(j), values, 0.0)
                total = term if total is None else total + term
            fields.append(total)
        return fields

    def centre(dg, fz, r):
        return (dg - SHIFT) * r - fz * pltpu.roll(r, nz - 1, 1) - pltpu.roll(fz * r, 1, 1)

    def first(i, carry):
        for h in range(0, ny, 8):
            base = pl.multiple_of(i * pitch + 8 + h, 8)
            flat = pl.multiple_of(i * ny + h, 8)
            mid = pl.ds(base, 8)
            r = rex[mid]
            parts = [
                (centre(dg_ref[pl.ds(flat, 8)], fz_ref[pl.ds(flat, 8)], r), lbx[mid]),
                (-fx_ref[pl.ds(flat, 8)] * rex[pl.ds(base + pitch, 8)], lbx[pl.ds(base + pitch, 8)]),
                (-fx_ref[pl.ds(flat - ny, 8)] * rex[pl.ds(base - pitch, 8)], lbx[pl.ds(base - pitch, 8)]),
                (-fyx[mid] * rex[pl.ds(base + 1, 8)], lbx[pl.ds(base + 1, 8)]),
                (-fyx[pl.ds(base - 1, 8)] * rex[pl.ds(base - 1, 8)], lbx[pl.ds(base - 1, 8)]),
            ]
            for j, values in enumerate(spread(parts)):
                pex[j, mid] = values
        return carry

    lax.fori_loop(1, ext - 1, first, 0)

    for side in range(2):
        outer_at = 7 if side == 0 else 8 + ny
        for c in range(0, nx, 8):
            lo = g + c
            here = slice(side * xpad + lo, side * xpad + lo + 8)
            up = slice(side * xpad + lo + 1, side * xpad + lo + 9)
            down = slice(side * xpad + lo - 1, side * xpad + lo + 7)
            parts = [
                (centre(packed(side, 5, lo, 8), packed(side, 6, lo, 8), rhalo[here]), lab1[here]),
                (-packed(side, 3, lo, 8) * rhalo[up], lab1[up]),
                (-packed(side, 3, lo - 1, 8) * rhalo[down], lab1[down]),
                (-packed(side, 4, lo, 8), lab2[here]),
                (rin[here], labin[here]),
            ]
            for j, values in enumerate(spread(parts)):
                pex[j, pl.ds(lo * pitch + outer_at, 8, stride=pitch), :] = values

    def second(i, carry):
        for h in range(0, ny, 8):
            base = pl.multiple_of((i + g) * pitch + 8 + h, 8)
            flat = pl.multiple_of((i + g) * ny + h, 8)
            out = pl.ds(pl.multiple_of(i * ny + h, 8), 8)
            mid = pl.ds(base, 8)
            dg, fz = dg_ref[pl.ds(flat, 8)], fz_ref[pl.ds(flat, 8)]
            fxp, fxm = fx_ref[pl.ds(flat, 8)], fx_ref[pl.ds(flat - ny, 8)]
            fyp, fym = fyx[mid], fyx[pl.ds(base - 1, 8)]
            r_out[out] = rex[mid]
            for j in range(ENLARGE):
                p = pex[j, mid]
                q = dg * p
                q = q - fxp * pex[j, pl.ds(base + pitch, 8)] - fxm * pex[j, pl.ds(base - pitch, 8)]
                q = q - fyp * pex[j, pl.ds(base + 1, 8)] - fym * pex[j, pl.ds(base - 1, 8)]
                q = q - fz * pltpu.roll(p, nz - 1, 1) - pltpu.roll(fz * p, 1, 1)
                p_out[j, out] = p
                q_out[j, out] = q
        return carry

    lax.fori_loop(0, nx, second, 0)

    zeros = tuple(jnp.zeros((8, nz), F32) for _ in PAIRS)

    def dots_pp(i, sums):
        at = pl.ds(pl.multiple_of(i * 8, 8), 8)
        p = [p_out[j, at] for j in range(ENLARGE)]
        return tuple(t + p[j] * p[k] for t, (j, k) in zip(sums, PAIRS))

    def dots_pq(i, sums):
        at = pl.ds(pl.multiple_of(i * 8, 8), 8)
        p = [p_out[j, at] for j in range(ENLARGE)]
        q = [q_out[j, at] for j in range(ENLARGE)]
        return tuple(t + p[j] * q[k] for t, (j, k) in zip(sums, PAIRS))

    def dots_bp(i, sums):
        at = pl.ds(pl.multiple_of(i * 8, 8), 8)
        flat = pl.ds(pl.multiple_of(i * 8 + g * ny, 8), 8)
        r = r_out[at]
        label = lb_ref[flat]
        b = [jnp.where(label == float(j), r, 0.0) for j in range(ENLARGE)]
        p = [p_out[j, at] for j in range(ENLARGE)]
        own = tuple(t + v * v for t, v in zip(sums[len(PAIRS) :], b))
        return tuple(t + b[j] * p[k] for t, (j, k) in zip(sums, PAIRS)) + own

    count = nx * ny // 8
    bp = lax.fori_loop(0, count, dots_bp, zeros + zeros[:ENLARGE])
    put = lambda slot, values: accs.__setitem__(
        (slice(slot, slot + 1),), jnp.sum(values, axis=0, keepdims=True)
    )
    accs[...] = jnp.zeros_like(accs)
    span = ENLARGE * ENLARGE
    for which, sums in ((0, bp[: len(PAIRS)]),):
        for (j, k), values in zip(PAIRS, sums):
            put(which * span + j * ENLARGE + k, values)
            if j != k:
                put(which * span + k * ENLARGE + j, values)
    for j in range(ENLARGE):
        put(3 * span + j * ENLARGE + j, bp[len(PAIRS) + j])
    for which, dots in ((1, dots_pp), (2, dots_pq)):
        sums = lax.fori_loop(0, count, dots, zeros)
        for (j, k), values in zip(PAIRS, sums):
            put(which * span + j * ENLARGE + k, values)
            if j != k:
                put(which * span + k * ENLARGE + j, values)
    ones = jnp.ones((8, nz), F32)
    flat = lax.dot_general(ones, accs[...], (((1,), (1,)), ((), ())), precision=HIGHEST, preferred_element_type=F32)
    half = 2 * span
    pair = jnp.where(iota((2, half), 0) == 0, flat[0:2, 0:half], flat[0:2, half : 2 * half])
    for d in range(devices):
        gram_out[d] = pair


def powers(ext_fields, ye, yo, nx, ny, xpad, devices):
    nz = ye.shape[-1]
    pitch = ny + 16
    half = 2 * ENLARGE * ENLARGE
    field = jax.ShapeDtypeStruct((nx * ny, nz), F32)
    fields = jax.ShapeDtypeStruct((ENLARGE, nx * ny, nz), F32)
    padded = pltpu.VMEM((xpad * pitch, nz), F32)
    edge = pltpu.VMEM((2 * xpad, nz), F32)
    return pl.pallas_call(
        functools.partial(powers_kernel, nx, ny, xpad, devices),
        in_specs=whole(9),
        out_specs=whole(4),
        out_shape=[fields, fields, field, jax.ShapeDtypeStruct((devices, 2, half), F32)],
        scratch_shapes=[
            padded, padded, padded, pltpu.VMEM((ENLARGE, xpad * pitch, nz), F32),
            edge, edge, edge, edge, edge,
            pltpu.VMEM((2 * half, nz), F32),
        ],
        compiler_params=params(),
        name="powers",
    )(*ext_fields, ye, yo)


def solve_columns(parts):
    nz = parts.shape[-1]
    span = ENLARGE * ENLARGE
    v = jnp.sum(parts, axis=0)
    lhs = jnp.concatenate([jnp.broadcast_to(v[0:1], (8, nz)), jnp.broadcast_to(v[1:2], (8, nz))], axis=1)
    source = iota((8, 2 * nz), 1)
    lhs = jnp.where(iota((8, 2 * nz), 0) == lax.rem(source, span) // ENLARGE, lhs, 0.0)
    k = iota((2 * nz, nz), 0)
    n = iota((2 * nz, nz), 1)
    which = k // span
    column = lax.rem(k, ENLARGE)

    def place(block, offset, scale):
        return jnp.where(jnp.logical_and(which == block, n == column + offset), scale, 0.0)

    upper = place(0, 0, 1.0) + place(3, 0, SHIFT) + place(1, 8, 1.0) + place(0, 8, SHIFT) + place(3, 16, 1.0)
    lower = place(1, 0, 1.0) + place(0, 0, SHIFT) + place(2, 8, 1.0) + place(0, 16, 1.0)
    dot = functools.partial(jnp.dot, precision=HIGHEST, preferred_element_type=F32)
    m = jnp.concatenate([dot(lhs, upper), dot(lhs, lower)], axis=0)
    row = iota(m.shape, 0)
    for i in range(2 * ENLARGE):
        pivot = m[i : i + 1] / m[i : i + 1, i : i + 1]
        m = jnp.where(row == i, pivot, m - m[:, i : i + 1] * pivot)
    return m


def update_kernel(ny, parts_ref, p_ref, q_ref, r_ref, lb_ref, it_ref, it_out, r_out, table, weights):
    nz = r_ref.shape[-1]
    two = 2 * ENLARGE

    @pl.when(pl.program_id(0) == 0)
    def _():
        m = solve_columns(parts_ref[...])
        lane = iota(m.shape, 1)
        inside = jnp.logical_and(lane >= two, lane < two + ENLARGE)
        carried = jnp.sum(jnp.where(inside, m, 0.0), axis=1, keepdims=True)
        for j in range(ENLARGE):
            for k in range(ENLARGE):
                value = m[ENLARGE + k : ENLARGE + k + 1, two + j : two + j + 1]
                table[j * ENLARGE + k] = jnp.broadcast_to(value, (8, nz))
        for k in range(two):
            table[ENLARGE * ENLARGE + k] = jnp.broadcast_to(carried[k : k + 1], (8, nz))
        own = pltpu.roll(m[0:ENLARGE], nz - two, 1)
        lane = iota(own.shape, 1)
        own = jnp.where(lane < ENLARGE, own, jnp.where(lane == ENLARGE, carried[0:ENLARGE], 0.0))
        high = own.astype(jnp.bfloat16).astype(F32)
        mid = (own - high).astype(jnp.bfloat16).astype(F32)
        rest = own - high - mid
        weights[...] = jnp.zeros_like(weights)
        weights[0:8] = high
        weights[8:16] = mid
        weights[16:24] = rest

    count = r_ref.shape[0]
    lane = iota((count, nz), 1)
    chosen = jnp.logical_and(lane < 3 * ENLARGE, lax.rem(lane, ENLARGE).astype(F32) == lb_ref[...])
    onehot = jnp.where(chosen, 1.0, 0.0).astype(jnp.bfloat16)
    own = jnp.dot(onehot, weights[...].astype(jnp.bfloat16), preferred_element_type=F32)
    for at in range(0, count, 8):
        here = slice(at, at + 8)
        r = r_ref[here]
        mine = own[here]
        p = [p_ref[k, here] for k in range(ENLARGE)]
        for j in range(ENLARGE):
            total = it_ref[j, here] + mine[:, j : j + 1] * r
            for k in range(ENLARGE):
                total = total + table[j * ENLARGE + k] * p[k]
            it_out[j, here] = total
        base = ENLARGE * ENLARGE
        total = r - (SHIFT * mine[:, ENLARGE : ENLARGE + 1]) * r
        for k in range(ENLARGE):
            total = total - table[base + k] * p[k] - table[base + ENLARGE + k] * q_ref[k, here]
        r_out[here] = total


def update(parts, p, q, r, labels_ext, iterates, ny):
    _, rows, nz = p.shape
    block = 4 * ny
    assert rows % block == 0
    many = pl.BlockSpec((ENLARGE, block, nz), lambda i: (0, i, 0))
    one = pl.BlockSpec((block, nz), lambda i: (i, 0))
    return pl.pallas_call(
        functools.partial(update_kernel, ny),
        grid=(rows // block,),
        in_specs=[pl.BlockSpec(parts.shape, lambda i: (0, 0, 0)), many, many, one, one, many],
        out_specs=[many, one],
        out_shape=[jax.ShapeDtypeStruct((ENLARGE, rows, nz), F32), jax.ShapeDtypeStruct((rows, nz), F32)],
        scratch_shapes=[
            pltpu.VMEM((ENLARGE * ENLARGE + 2 * ENLARGE, 8, nz), F32),
            pltpu.VMEM((nz, nz), F32),
        ],
        compiler_params=params(),
        name="update",
    )(parts, p, q, r, labels_ext, iterates)


def shards(gx, gy, source, diagonal, face_x, face_y, face_z, iterates, labels):
    _, nx, ny, nz = iterates.shape
    xpad = -(-(nx + 2 * GHOST) // 8) * 8
    spread = jnp.broadcast_to(labels.astype(F32)[:, :, None], (nx, ny, nz))
    fields = (source, diagonal, face_x, face_y, face_z, spread)
    total, xe, xo = sum_and_edges(iterates, fields)
    xe = lax.ppermute(xe, "gx", even_pairs(gx))
    xo = lax.ppermute(xo, "gx", odd_pairs(gx))
    *ext, ye, yo = partial_and_edges(total, fields, xe, xo, xpad, gx, gy)
    ye = lax.ppermute(ye, "gy", even_pairs(gy))
    yo = lax.ppermute(yo, "gy", odd_pairs(gy))
    p, q, r, gram = powers(ext, ye, yo, nx, ny, xpad, gx * gy)
    parts = lax.all_to_all(gram, ("gx", "gy"), 0, 0, tiled=True)
    flat = iterates.reshape(ENLARGE, nx * ny, nz)
    new_iterates, new_residual = update(parts, p, q, r, spread.reshape(nx * ny, nz), flat, ny)
    return new_iterates.reshape(iterates.shape), new_residual.reshape(source.shape)


def solution(mesh):
    placed = (
        P("gx", "gy", None),
        P("gx", "gy", None),
        P("gx", "gy", None),
        P("gx", "gy", None),
        P("gx", "gy", None),
        P(None, "gx", "gy", None),
        P("gx", "gy"),
    )
    return jax.shard_map(
        functools.partial(shards, mesh.shape["gx"], mesh.shape["gy"]),
        mesh=mesh,
        in_specs=placed,
        out_specs=(P(None, "gx", "gy", None), P("gx", "gy", None)),
        check_vma=False,
    )
```

time: 178 us -> 91.6 us (0.51)
  blocking collectives: 44.6 us -> 0 us
  Pallas kernels: 0 us -> 40.6 us
  matrix products: 37.9 us -> 0 us
  other arithmetic: 29 us -> 0.7 us
  starting transfers between devices: 44.6 us -> 19.4 us
  local copies, waits for them, and re-layouts: 5.36 us -> 18.5 us
  waiting for transfers between devices: 14.8 us -> 11.1 us
    psum x1 -> x0, blocking collectives: 44.6 us -> none  [shards(): gram = lax.psum(gram_local, ('gx', 'gy'))]
    pallas_call x0 -> x4, Pallas kernels: none -> 40.6 us  [the longest x1 24.6 us: powers(): pl.pallas_call(functools.partial(powers_kernel, nx, ny, xpad, devices), i...]
    ppermute x16 -> x4, starting transfers between devices: 44.6 us -> 4.79 us  [the longest x1 2.91 us: shards(): ye = lax.ppermute(ye, 'gy', even_pairs(gy))]
    dot_general x8 -> x0, matrix products: 37.3 us -> none  [the longest x1 11.2 us: shards(): gram_local = jnp.einsum('aijk,bijk->ab', basis, basis, precision=highest)]
    sub x4 -> x0, other arithmetic: 16.7 us -> none  [the longest x1 7.45 us: shards(): powered = applied - basis_shift * blocks]
    all_to_all x0 -> x1, starting transfers between devices: none -> 14.7 us  [shards(): parts = lax.all_to_all(gram, ('gx', 'gy'), 0, 0, tiled=True)]
    unnamed x26 -> x32, local copies, waits for them, and re-layouts: 4.88 us -> 17.9 us
    ppermute x16 -> x4, waiting for transfers between devices: 14.8 us -> 4.01 us  [the longest x1 3.68 us: shards(): ye = lax.ppermute(ye, 'gy', even_pairs(gy))]
  transfers between devices with their start and end apart: 16 -> 5, of which waited for: 6 -> 3; matrix products, arithmetic and copies ran while one was open for 7% -> 0% of each run, Pallas kernels for 0% -> 0%
where the time goes in v1:
time: 91.6 us; the launch traced here: 91 us
  Pallas kernels  40.6 us (44%)
  starting transfers between devices  19.4 us (21%)
  local copies, waits for them, and re-layouts  18.5 us (20%)
  waiting for transfers between devices  11.1 us (12%)
    pallas_call x1, Pallas kernels, powers(): pl.pallas_call(functools.partial(powers_kernel, nx, ny, xpad, devices), i...  24.6 us
    unnamed x32, local copies, waits for them, and re-layouts  17.9 us
    all_to_all x1, starting transfers between devices, shards(): parts = lax.all_to_all(gram, ('gx', 'gy'), 0, 0, tiled=True)  14.7 us
    pallas_call x1, Pallas kernels, update(): pl.pallas_call(functools.partial(update_kernel, ny), grid=(rows // block,...  11.8 us
    all_to_all x1, waiting for transfers between devices, shards(): parts = lax.all_to_all(gram, ('gx', 'gy'), 0, 0, tiled=True)  7.11 us
    ppermute x1, waiting for transfers between devices, shards(): ye = lax.ppermute(ye, 'gy', even_pairs(gy))  3.68 us
    pallas_call x1, Pallas kernels, partial_and_edges(): pl.pallas_call(functools.partial(partial_kernel, nx, ny, xpad, gx, gy), i...  3.39 us
    ppermute x1, starting transfers between devices, shards(): ye = lax.ppermute(ye, 'gy', even_pairs(gy))  2.91 us
  transfers between devices with their start and end apart: 5, of which 3 were waited for; matrix products, arithmetic and copies ran while one was open for 0% of the time, Pallas kernels for 0%

profile of v1, /device:TPU:0, one launch (start us, length us, event | category | flops | bytes accessed | tf_op | source)
XLA Modules:
  0.0 91.0 jit_solution(12197325402861558052)
XLA Ops:
  0.6 0.7 convert_element_type.3
  1.6 2.2 %copy-done = f32[8,64,16,128]{3,2,1,0:T(8,128)S(1)} copy-done((f32[8,64,16,128]{3,2,1,0:T(8,128)S(1)}, f32[8,64,16,128]{3,2,1,0:T(8,128)}, u32[]{:S(2)}) %copy-start) | copy-done | bytes 4194328
  3.8 1.0 %copy-done.2 = f32[64,16,128]{2,1,0:T(8,128)S(1)} copy-done((f32[64,16,128]{2,1,0:T(8,128)S(1)}, f32[64,16,128]{2,1,0:T(8,128)}, u32[]{:S(2)}) %copy-start.2) | copy-done | bytes 524312
  4.9 1.0 %copy-done.4 = f32[64,16,128]{2,1,0:T(8,128)S(1)} copy-done((f32[64,16,128]{2,1,0:T(8,128)S(1)}, f32[64,16,128]{2,1,0:T(8,128)}, u32[]{:S(2)}) %copy-start.4) | copy-done | bytes 524312
  5.9 1.0 %copy-done.6 = f32[64,16,128]{2,1,0:T(8,128)S(1)} copy-done((f32[64,16,128]{2,1,0:T(8,128)S(1)}, f32[64,16,128]{2,1,0:T(8,128)}, u32[]{:S(2)}) %copy-start.6) | copy-done | bytes 524312
  6.9 1.0 %copy-done.8 = f32[64,16,128]{2,1,0:T(8,128)S(1)} copy-done((f32[64,16,128]{2,1,0:T(8,128)S(1)}, f32[64,16,128]{2,1,0:T(8,128)}, u32[]{:S(2)}) %copy-start.8) | copy-done | bytes 524312
  8.0 1.0 %copy-done.10 = f32[64,16,128]{2,1,0:T(8,128)S(1)} copy-done((f32[64,16,128]{2,1,0:T(8,128)S(1)}, f32[64,16,128]{2,1,0:T(8,128)}, u32[]{:S(2)}) %copy-start.10) | copy-done | bytes 524312
  9.0 0.8 sum_and_edges.1
  9.8 0.6 collective-permute-start
  10.4 0.7 collective-permute-start.1
  11.1 0.3 collective-permute-done.xe_ref
  11.4 3.4 %partial_and_edges.1 = (f32[1152,128]{1,0:T(8,128)S(1)}, f32[1152,128]{1,0:T(8,128)S(1)}, f32[1152,128]{1,0:T(8,128)S(1)}, f32[1152,128]{1,0:T(8,128)S(1)}, f32[...) custom-call(f32[64,16,128]{2,1,0:T(8,128)S(1)} %get-tuple-element.20, ...), custom_call_target="tpu_custom_call" | custom-call | tf_op jit(solution)/shard_map/partial_and_edges/pallas_call | solution.py:229
  14.8 2.9 %collective-permute-start.2 = (f32[512,128]{1,0:T(8,128)S(1)}, f32[512,128]{1,0:T(8,128)S(1)}, u32[]{:S(2)}, u32[]{:S(2)}) collective-permute-start(f32[512,128]{1,0:T(8,128)S(1)} %get-tuple-element.30), channel_id=1, source_target_pairs={{0,1},{1,0},{2,3},{3,2},{4,5},{5,4},{6,7},{7,6},{8,9},{9,8},{10,11... | collective-permute-start | bytes 786440 | tf_op jit(solution)/shard_map/ppermute | solution.py:543
  17.7 0.7 collective-permute-start.3
  18.4 3.7 %collective-permute-done.2.ye_ref = f32[512,128]{1,0:T(8,128)S(1)} collective-permute-done((f32[512,128]{1,0:T(8,128)S(1)}, f32[512,128]{1,0:T(8,128)S(1)}, u32[]{:S(2)}, u32[]{:S(2)}) %collective-permute-start.2) | collective-permute-done | bytes 262176 | tf_op jit(solution)/shard_map/ppermute | solution.py:543
  22.1 24.6 %powers.1 = (f32[8,1024,128]{2,1,0:T(8,128)S(1)}, f32[8,1024,128]{2,1,0:T(8,128)S(1)}, f32[1024,128]{1,0:T(8,128)S(1)}, f32[32,2,128]{2,1,0:T(2,128)}) custom-call(f32[1152,128]{1,0:T(8,128)S(1)} %get-tuple-element.23.t_ref, f32[1152,128]{1,0:T(8,128)S(1)} %get-tuple-element.24.s_ref, f32[1152,128]{1,0:T(8,128)S(1)} %get-tuple-element.25.fx_ref, ...), custom_call_target="tpu_custom_call" | custom-call | tf_op jit(solution)/shard_map/powers/pallas_call | solution.py:423
  46.7 2.0 %copy-done.12 = f32[8,1024,128]{2,1,0:T(8,128)} copy-done((f32[8,1024,128]{2,1,0:T(8,128)}, f32[8,1024,128]{2,1,0:T(8,128)S(1)}, u32[]{:S(2)}) %copy-start.12) | copy-done | bytes 4194328
  48.7 1.9 %copy-done.14 = f32[8,1024,128]{2,1,0:T(8,128)} copy-done((f32[8,1024,128]{2,1,0:T(8,128)}, f32[8,1024,128]{2,1,0:T(8,128)S(1)}, u32[]{:S(2)}) %copy-start.14) | copy-done | bytes 4194328
  50.6 14.7 %all-to-all-start = ((f32[32,2,128]{2,1,0:T(2,128)}), f32[32,2,128]{2,1,0:T(2,128)S(1)}, u32[]{:S(2)}, u32[]{:S(2)}) async-start(f32[32,2,128]{2,1,0:T(2,128)} %get-tuple-element.32), calls=%async_computation | async-start | bytes 65536 | tf_op jit(solution)/shard_map/all_to_all | solution.py:546
  65.4 7.1 %all-to-all-done.parts_ref = f32[32,2,128]{2,1,0:T(2,128)S(1)} async-done(((f32[32,2,128]{2,1,0:T(2,128)}), f32[32,2,128]{2,1,0:T(2,128)S(1)}, u32[]{:S(2)}, u32[]{:S(2)}) %all-to-all-start) | async-done | bytes 32800 | tf_op jit(solution)/shard_map/all_to_all | solution.py:546
  72.7 2.2 %copy-done.1 = f32[8,64,16,128]{3,2,1,0:T(8,128)S(1)} copy-done((f32[8,64,16,128]{3,2,1,0:T(8,128)S(1)}, f32[8,64,16,128]{3,2,1,0:T(8,128)}, u32[]{:S(2)}) %copy-start.1) | copy-done | bytes 4194328
  74.9 2.2 %copy-done.13 = f32[8,1024,128]{2,1,0:T(8,128)S(1)} copy-done((f32[8,1024,128]{2,1,0:T(8,128)S(1)}, f32[8,1024,128]{2,1,0:T(8,128)}, u32[]{:S(2)}) %copy-start.13) | copy-done | bytes 4194328
  77.1 2.2 %copy-done.15 = f32[8,1024,128]{2,1,0:T(8,128)S(1)} copy-done((f32[8,1024,128]{2,1,0:T(8,128)S(1)}, f32[8,1024,128]{2,1,0:T(8,128)}, u32[]{:S(2)}) %copy-start.15) | copy-done | bytes 4194328
  79.3 11.8 %update.1 = (f32[8,1024,128]{2,1,0:T(8,128)}, f32[1024,128]{1,0:T(8,128)}) custom-call(f32[32,2,128]{2,1,0:T(2,128)S(1)} %all-to-all-done.parts_ref, f32[8,1024,128]{2,1,0:T(8,128)S(1)} %copy-done.13, f32[8,1024,128]{2,1,0:T(8,128)S(1)} %copy-done.15, f32[1024,128]{1,0:T(8,128)S(1)} %get-tuple-element.35.r_ref, f32[1024,128]{1,0:T(8,128)S(1)} %broadcast_in_dim.12.lb_ref, ...), custom_call_target="tpu_custom_call" | custom-call | tf_op jit(solution)/shard_map/update/pallas_call | solution.py:519
  (27 shorter events, 0.6 us)
Async XLA Ops:
  1.6 2.2 %copy-start = (f32[8,64,16,128]{3,2,1,0:T(8,128)S(1)}, f32[8,64,16,128]{3,2,1,0:T(8,128)}, u32[]{:S(2)}) copy-start(f32[8,64,16,128]{3,2,1,0:T(8,128)} %it_ref.1) | copy-start | bytes 12582916
  3.8 1.0 %copy-start.2 = (f32[64,16,128]{2,1,0:T(8,128)S(1)}, f32[64,16,128]{2,1,0:T(8,128)}, u32[]{:S(2)}) copy-start(f32[64,16,128]{2,1,0:T(8,128)} %src_in.1) | copy-start | bytes 1572868
  4.8 1.0 %copy-start.4 = (f32[64,16,128]{2,1,0:T(8,128)S(1)}, f32[64,16,128]{2,1,0:T(8,128)}, u32[]{:S(2)}) copy-start(f32[64,16,128]{2,1,0:T(8,128)} %dg_in.1) | copy-start | bytes 1572868
  5.9 1.0 %copy-start.6 = (f32[64,16,128]{2,1,0:T(8,128)S(1)}, f32[64,16,128]{2,1,0:T(8,128)}, u32[]{:S(2)}) copy-start(f32[64,16,128]{2,1,0:T(8,128)} %fx_in.1) | copy-start | bytes 1572868
  6.9 1.0 %copy-start.8 = (f32[64,16,128]{2,1,0:T(8,128)S(1)}, f32[64,16,128]{2,1,0:T(8,128)}, u32[]{:S(2)}) copy-start(f32[64,16,128]{2,1,0:T(8,128)} %fy_in.1) | copy-start | bytes 1572868
  8.0 1.0 %copy-start.10 = (f32[64,16,128]{2,1,0:T(8,128)S(1)}, f32[64,16,128]{2,1,0:T(8,128)}, u32[]{:S(2)}) copy-start(f32[64,16,128]{2,1,0:T(8,128)} %fz_in.1) | copy-start | bytes 1572868
  9.0 2.4 %copy-start.3 = (f32[64,16,128]{2,1,0:T(8,128)S(1)}, f32[64,16,128]{2,1,0:T(8,128)}, u32[]{:S(2)}) copy-start(f32[64,16,128]{2,1,0:T(8,128)} %src_in.1) | copy-start | bytes 1572868
  9.0 2.4 %copy-start.5 = (f32[64,16,128]{2,1,0:T(8,128)S(1)}, f32[64,16,128]{2,1,0:T(8,128)}, u32[]{:S(2)}) copy-start(f32[64,16,128]{2,1,0:T(8,128)} %dg_in.1) | copy-start | bytes 1572868
  9.0 2.4 %copy-start.7 = (f32[64,16,128]{2,1,0:T(8,128)S(1)}, f32[64,16,128]{2,1,0:T(8,128)}, u32[]{:S(2)}) copy-start(f32[64,16,128]{2,1,0:T(8,128)} %fx_in.1) | copy-start | bytes 1572868
  9.0 2.4 %copy-start.9 = (f32[64,16,128]{2,1,0:T(8,128)S(1)}, f32[64,16,128]{2,1,0:T(8,128)}, u32[]{:S(2)}) copy-start(f32[64,16,128]{2,1,0:T(8,128)} %fy_in.1) | copy-start | bytes 1572868
  9.0 2.4 %copy-start.11 = (f32[64,16,128]{2,1,0:T(8,128)S(1)}, f32[64,16,128]{2,1,0:T(8,128)}, u32[]{:S(2)}) copy-start(f32[64,16,128]{2,1,0:T(8,128)} %fz_in.1) | copy-start | bytes 1572868
  9.8 1.5 %collective-permute-start = (f32[16,16,128]{2,1,0:T(8,128)S(1)}, f32[16,16,128]{2,1,0:T(8,128)S(1)}, u32[]{:S(2)}, u32[]{:S(2)}) collective-permute-start(f32[16,16,128]{2,1,0:T(8,128)S(1)} %get-tuple-element.21), channel_id=1, source_target_pairs={{0,8},{8,0},{16,24},{24,16},{1,9},{9,1},{17,25},{25,17},{2,10},{10... | collective-permute-start | bytes 393224 | tf_op jit(solution)/shard_map/ppermute | solution.py:540
  10.4 1.0 %collective-permute-start.1 = (f32[16,16,128]{2,1,0:T(8,128)S(1)}, f32[16,16,128]{2,1,0:T(8,128)S(1)}, u32[]{:S(2)}, u32[]{:S(2)}) collective-permute-start(f32[16,16,128]{2,1,0:T(8,128)S(1)} %get-tuple-element.22), channel_id=1, source_target_pairs={{8,16},{16,8},{9,17},{17,9},{10,18},{18,10},{11,19},{19,11},{12,20... | collective-permute-start | bytes 393224 | tf_op jit(solution)/shard_map/ppermute | solution.py:541
  14.8 7.3 %collective-permute-start.2 = (f32[512,128]{1,0:T(8,128)S(1)}, f32[512,128]{1,0:T(8,128)S(1)}, u32[]{:S(2)}, u32[]{:S(2)}) collective-permute-start(f32[512,128]{1,0:T(8,128)S(1)} %get-tuple-element.30), channel_id=1, source_target_pairs={{0,1},{1,0},{2,3},{3,2},{4,5},{5,4},{6,7},{7,6},{8,9},{9,8},{10,11... | collective-permute-start | bytes 786440 | tf_op jit(solution)/shard_map/ppermute | solution.py:543
  17.7 4.4 %collective-permute-start.3 = (f32[512,128]{1,0:T(8,128)S(1)}, f32[512,128]{1,0:T(8,128)S(1)}, u32[]{:S(2)}, u32[]{:S(2)}) collective-permute-start(f32[512,128]{1,0:T(8,128)S(1)} %get-tuple-element.31), channel_id=1, source_target_pairs={{1,2},{2,1},{3,4},{4,3},{5,6},{6,5},{9,10},{10,9},{11,12},{12,11},... | collective-permute-start | bytes 786440 | tf_op jit(solution)/shard_map/ppermute | solution.py:544
  46.7 2.0 %copy-start.12 = (f32[8,1024,128]{2,1,0:T(8,128)}, f32[8,1024,128]{2,1,0:T(8,128)S(1)}, u32[]{:S(2)}) copy-start(f32[8,1024,128]{2,1,0:T(8,128)S(1)} %get-tuple-element.33.p_ref) | copy-start | bytes 12582916
  48.7 1.9 %copy-start.14 = (f32[8,1024,128]{2,1,0:T(8,128)}, f32[8,1024,128]{2,1,0:T(8,128)S(1)}, u32[]{:S(2)}) copy-start(f32[8,1024,128]{2,1,0:T(8,128)S(1)} %get-tuple-element.34.q_ref) | copy-start | bytes 12582916
  50.6 21.9 %all-to-all-start = ((f32[32,2,128]{2,1,0:T(2,128)}), f32[32,2,128]{2,1,0:T(2,128)S(1)}, u32[]{:S(2)}, u32[]{:S(2)}) async-start(f32[32,2,128]{2,1,0:T(2,128)} %get-tuple-element.32), calls=%async_computation | async-start | bytes 65536 | tf_op jit(solution)/shard_map/all_to_all | solution.py:546
  72.7 2.2 %copy-start.1 = (f32[8,64,16,128]{3,2,1,0:T(8,128)S(1)}, f32[8,64,16,128]{3,2,1,0:T(8,128)}, u32[]{:S(2)}) copy-start(f32[8,64,16,128]{3,2,1,0:T(8,128)} %it_ref.1) | copy-start | bytes 12582916
  74.9 2.2 %copy-start.13 = (f32[8,1024,128]{2,1,0:T(8,128)S(1)}, f32[8,1024,128]{2,1,0:T(8,128)}, u32[]{:S(2)}) copy-start(f32[8,1024,128]{2,1,0:T(8,128)} %copy-done.12) | copy-start | bytes 12582916
  77.1 2.2 %copy-start.15 = (f32[8,1024,128]{2,1,0:T(8,128)S(1)}, f32[8,1024,128]{2,1,0:T(8,128)}, u32[]{:S(2)}) copy-start(f32[8,1024,128]{2,1,0:T(8,128)} %copy-done.14) | copy-start | bytes 12582916

commit v2 on v1

--- a/solution.py
+++ b/solution.py
@@ -241,14 +241,12 @@
     nx, ny, xpad, devices,
     t_ref, s_ref, fx_ref, fy_ref, dg_ref, fz_ref, lb_ref, ye_ref, yo_ref,
     p_out, q_out, r_out, gram_out,
-    rex, fyx, lbx, pex, rhalo, rin, lab1, lab2, labin, accs,
+    rex, fyx, lbx, pex, rhalo, rin, lab1, lab2, labin, accs, packs,
 ):
     g = GHOST
     nz = t_ref.shape[-1]
     ext = nx + 2 * g
     pitch = ny + 16
-    even_y = lax.rem(lax.axis_index("gy"), 2) == 0
-
     def at16(i):
         return pl.ds(pl.multiple_of(i * ny, ny), ny)
 
@@ -263,9 +261,11 @@
 
     def packed(side, b, start=0, count=None):
         count = xpad if count is None else count
-        span = slice(b * xpad + start, b * xpad + start + count)
-        e, o = ye_ref[span], yo_ref[span]
-        return jnp.where(even_y, o, e) if side == 0 else jnp.where(even_y, e, o)
+        return packs[side, b * xpad + start : b * xpad + start + count]
+
+    odd = lax.rem(lax.axis_index("gy"), 2)
+    packs[1 - odd] = ye_ref[...]
+    packs[odd] = yo_ref[...]
 
     for side in range(2):
         inner = 0 if side == 0 else ny - 1
@@ -359,7 +359,7 @@
                 q_out[j, out] = q
         return carry
 
-    lax.fori_loop(0, nx, second, 0)
+    lax.fori_loop(0, nx, second, 0, unroll=2)
 
     zeros = tuple(jnp.zeros((8, nz), F32) for _ in PAIRS)
 
@@ -385,7 +385,7 @@
         return tuple(t + b[j] * p[k] for t, (j, k) in zip(sums, PAIRS)) + own
 
     count = nx * ny // 8
-    bp = lax.fori_loop(0, count, dots_bp, zeros + zeros[:ENLARGE])
+    bp = lax.fori_loop(0, count, dots_bp, zeros + zeros[:ENLARGE], unroll=4)
     put = lambda slot, values: accs.__setitem__(
         (slice(slot, slot + 1),), jnp.sum(values, axis=0, keepdims=True)
     )
@@ -399,7 +399,7 @@
     for j in range(ENLARGE):
         put(3 * span + j * ENLARGE + j, bp[len(PAIRS) + j])
     for which, dots in ((1, dots_pp), (2, dots_pq)):
-        sums = lax.fori_loop(0, count, dots, zeros)
+        sums = lax.fori_loop(0, count, dots, zeros, unroll=4)
         for (j, k), values in zip(PAIRS, sums):
             put(which * span + j * ENLARGE + k, values)
             if j != k:
@@ -429,6 +429,7 @@
             padded, padded, padded, pltpu.VMEM((ENLARGE, xpad * pitch, nz), F32),
             edge, edge, edge, edge, edge,
             pltpu.VMEM((2 * half, nz), F32),
+            pltpu.VMEM((2,) + ye.shape, F32),
         ],
         compiler_params=params(),
         name="powers",
@@ -461,70 +462,114 @@
     return m
 
 
-def update_kernel(ny, parts_ref, p_ref, q_ref, r_ref, lb_ref, it_ref, it_out, r_out, table, weights):
-    nz = r_ref.shape[-1]
+def update_kernel(
+    offset, group, parts_ref, p_ref, q_ref, r_ref, lb_ref, it_hbm, it_out, r_out,
+    table, weights, onehot, own, work, r_work, sem_in, sem_out, sem_r,
+):
+    rows, nz = r_ref.shape
     two = 2 * ENLARGE
-
-    @pl.when(pl.program_id(0) == 0)
-    def _():
-        m = solve_columns(parts_ref[...])
-        lane = iota(m.shape, 1)
-        inside = jnp.logical_and(lane >= two, lane < two + ENLARGE)
-        carried = jnp.sum(jnp.where(inside, m, 0.0), axis=1, keepdims=True)
+    square = ENLARGE * ENLARGE
+    groups = rows // group
+
+    def span(c):
+        return pl.ds(pl.multiple_of(c * group, group), group)
+
+    def copy_in(c):
+        return pltpu.make_async_copy(it_hbm.at[:, span(c)], work.at[:, span(c)], sem_in.at[c])
+
+    def copy_out(c):
+        return pltpu.make_async_copy(work.at[:, span(c)], it_out.at[:, span(c)], sem_out.at[c])
+
+    def copy_r(c):
+        return pltpu.make_async_copy(r_work.at[span(c)], r_out.at[span(c)], sem_r.at[c])
+
+    def each(f):
+        def body(c, carry):
+            f(c)
+            return carry
+
+        lax.fori_loop(0, groups, body, 0)
+
+    each(lambda c: copy_in(c).start())
+
+    def mark(c):
+        lane = iota((group, nz), 1)
+        labels = lb_ref[pl.ds(pl.multiple_of(offset + c * group, 8), group)]
+        chosen = jnp.logical_and(lane < 3 * ENLARGE, lax.rem(lane, ENLARGE).astype(F32) == labels)
+        onehot[span(c)] = jnp.where(chosen, 1.0, 0.0).astype(jnp.bfloat16)
+
+    each(mark)
+
+    m = solve_columns(parts_ref[...])
+    lane = iota(m.shape, 1)
+    inside = jnp.logical_and(lane >= two, lane < two + ENLARGE)
+    carried = jnp.sum(jnp.where(inside, m, 0.0), axis=1, keepdims=True)
+    for j in range(ENLARGE):
+        for k in range(ENLARGE):
+            value = m[ENLARGE + k : ENLARGE + k + 1, two + j : two + j + 1]
+            table[j * ENLARGE + k] = jnp.broadcast_to(value, (8, nz))
+    for k in range(two):
+        table[square + k] = jnp.broadcast_to(carried[k : k + 1], (8, nz))
+    lane = iota((ENLARGE, nz), 1)
+    mine = pltpu.roll(m[0:ENLARGE], nz - two, 1)
+    mine = jnp.where(lane < ENLARGE, mine, jnp.where(lane == ENLARGE, carried[0:ENLARGE], 0.0))
+    high = mine.astype(jnp.bfloat16).astype(F32)
+    mid = (mine - high).astype(jnp.bfloat16).astype(F32)
+    weights[...] = jnp.zeros_like(weights)
+    weights[0:8] = high
+    weights[8:16] = mid
+    weights[16:24] = mine - high - mid
+    own[...] = jnp.dot(onehot[...], weights[...].astype(jnp.bfloat16), preferred_element_type=F32)
+
+    def body(c, carry):
+        copy_in(c).wait()
+        spots = [pl.ds(pl.multiple_of(c * group + h, 8), 8) for h in range(0, group, 8)]
+        r = [r_ref[at] for at in spots]
+        p = [[p_ref[k, at] for k in range(ENLARGE)] for at in spots]
+        mine = [own[at] for at in spots]
         for j in range(ENLARGE):
+            scale = [table[j * ENLARGE + k] for k in range(ENLARGE)]
+            for h, at in enumerate(spots):
+                total = work[j, at] + mine[h][:, j : j + 1] * r[h]
+                for k in range(ENLARGE):
+                    total = total + scale[k] * p[h][k]
+                work[j, at] = total
+        copy_out(c).start()
+        scale = [table[square + k] for k in range(two)]
+        for h, at in enumerate(spots):
+            total = r[h] - (SHIFT * mine[h][:, ENLARGE : ENLARGE + 1]) * r[h]
             for k in range(ENLARGE):
-                value = m[ENLARGE + k : ENLARGE + k + 1, two + j : two + j + 1]
-                table[j * ENLARGE + k] = jnp.broadcast_to(value, (8, nz))
-        for k in range(two):
-            table[ENLARGE * ENLARGE + k] = jnp.broadcast_to(carried[k : k + 1], (8, nz))
-        own = pltpu.roll(m[0:ENLARGE], nz - two, 1)
-        lane = iota(own.shape, 1)
-        own = jnp.where(lane < ENLARGE, own, jnp.where(lane == ENLARGE, carried[0:ENLARGE], 0.0))
-        high = own.astype(jnp.bfloat16).astype(F32)
-        mid = (own - high).astype(jnp.bfloat16).astype(F32)
-        rest = own - high - mid
-        weights[...] = jnp.zeros_like(weights)
-        weights[0:8] = high
-        weights[8:16] = mid
-        weights[16:24] = rest
-
-    count = r_ref.shape[0]
-    lane = iota((count, nz), 1)
-    chosen = jnp.logical_and(lane < 3 * ENLARGE, lax.rem(lane, ENLARGE).astype(F32) == lb_ref[...])
-    onehot = jnp.where(chosen, 1.0, 0.0).astype(jnp.bfloat16)
-    own = jnp.dot(onehot, weights[...].astype(jnp.bfloat16), preferred_element_type=F32)
-    for at in range(0, count, 8):
-        here = slice(at, at + 8)
-        r = r_ref[here]
-        mine = own[here]
-        p = [p_ref[k, here] for k in range(ENLARGE)]
-        for j in range(ENLARGE):
-            total = it_ref[j, here] + mine[:, j : j + 1] * r
-            for k in range(ENLARGE):
-                total = total + table[j * ENLARGE + k] * p[k]
-            it_out[j, here] = total
-        base = ENLARGE * ENLARGE
-        total = r - (SHIFT * mine[:, ENLARGE : ENLARGE + 1]) * r
-        for k in range(ENLARGE):
-            total = total - table[base + k] * p[k] - table[base + ENLARGE + k] * q_ref[k, here]
-        r_out[here] = total
+                total = total - scale[k] * p[h][k] - scale[ENLARGE + k] * q_ref[k, at]
+            r_work[at] = total
+        copy_r(c).start()
+        return carry
+
+    lax.fori_loop(0, groups, body, 0)
+    each(lambda c: copy_out(c).wait())
+    each(lambda c: copy_r(c).wait())
 
 
 def update(parts, p, q, r, labels_ext, iterates, ny):
     _, rows, nz = p.shape
-    block = 4 * ny
-    assert rows % block == 0
-    many = pl.BlockSpec((ENLARGE, block, nz), lambda i: (0, i, 0))
-    one = pl.BlockSpec((block, nz), lambda i: (i, 0))
+    group = 2 * ny
+    assert rows % group == 0
+    groups = rows // group
+    hbm = pl.BlockSpec(memory_space=pltpu.HBM)
     return pl.pallas_call(
-        functools.partial(update_kernel, ny),
-        grid=(rows // block,),
-        in_specs=[pl.BlockSpec(parts.shape, lambda i: (0, 0, 0)), many, many, one, one, many],
-        out_specs=[many, one],
+        functools.partial(update_kernel, GHOST * ny, group),
+        in_specs=whole(5) + [hbm],
+        out_specs=[hbm, hbm],
         out_shape=[jax.ShapeDtypeStruct((ENLARGE, rows, nz), F32), jax.ShapeDtypeStruct((rows, nz), F32)],
         scratch_shapes=[
             pltpu.VMEM((ENLARGE * ENLARGE + 2 * ENLARGE, 8, nz), F32),
             pltpu.VMEM((nz, nz), F32),
+            pltpu.VMEM((rows, nz), jnp.bfloat16),
+            pltpu.VMEM((rows, nz), F32),
+            pltpu.VMEM((ENLARGE, rows, nz), F32),
+            pltpu.VMEM((rows, nz), F32),
+            pltpu.SemaphoreType.DMA((groups,)),
+            pltpu.SemaphoreType.DMA((groups,)),
+            pltpu.SemaphoreType.DMA((groups,)),
         ],
         compiler_params=params(),
         name="update",
@@ -545,7 +590,7 @@
     p, q, r, gram = powers(ext, ye, yo, nx, ny, xpad, gx * gy)
     parts = lax.all_to_all(gram, ("gx", "gy"), 0, 0, tiled=True)
     flat = iterates.reshape(ENLARGE, nx * ny, nz)
-    new_iterates, new_residual = update(parts, p, q, r, spread.reshape(nx * ny, nz), flat, ny)
+    new_iterates, new_residual = update(parts, p, q, r, ext[-1], flat, ny)
     return new_iterates.reshape(iterates.shape), new_residual.reshape(source.shape)
 
 

time: 91.6 us -> 72.2 us (0.79)
  blocking collectives: 0 us -> 21.7 us
  starting transfers between devices: 19.4 us -> 4.79 us
  local copies, waits for them, and re-layouts: 18.5 us -> 7.69 us
  Pallas kernels: 40.6 us -> 32.1 us
  waiting for transfers between devices: 11.1 us -> 4.01 us
    all_to_all x0 -> x1, blocking collectives: none -> 21.7 us  [shards(): parts = lax.all_to_all(gram, ('gx', 'gy'), 0, 0, tiled=True)]
    all_to_all x1 -> x0, starting transfers between devices: 14.7 us -> none  [shards(): parts = lax.all_to_all(gram, ('gx', 'gy'), 0, 0, tiled=True)]
    unnamed x32 -> x24, local copies, waits for them, and re-layouts: 17.9 us -> 7.42 us
    all_to_all x1 -> x0, waiting for transfers between devices: 7.11 us -> none  [shards(): parts = lax.all_to_all(gram, ('gx', 'gy'), 0, 0, tiled=True)]
    pallas_call x1, Pallas kernels: 24.6 us -> 17.9 us  [powers(): pl.pallas_call(functools.partial(powers_kernel, nx, ny, xpad, devices), i...]
    pallas_call x1, Pallas kernels: 11.8 us -> 10 us  [update(): pl.pallas_call(functools.partial(update_kernel, GHOST * ny, group), in_sp...]
  transfers between devices with their start and end apart: 5 -> 4, of which waited for: 3 -> 2; matrix products, arithmetic and copies ran while one was open for 0% -> 0% of each run, Pallas kernels for 0% -> 0%
where the time goes in v2:
time: 72.2 us; the launch traced here: 71.7 us
  Pallas kernels  32.1 us (44%)
  blocking collectives  21.7 us (30%)
  local copies, waits for them, and re-layouts  7.69 us (11%)
  starting transfers between devices  4.79 us (7%)
  waiting for transfers between devices  4.01 us (6%)
  between operations  0.73 us (1%)
    all_to_all x1, blocking collectives, shards(): parts = lax.all_to_all(gram, ('gx', 'gy'), 0, 0, tiled=True)  21.7 us
    pallas_call x1, Pallas kernels, powers(): pl.pallas_call(functools.partial(powers_kernel, nx, ny, xpad, devices), i...  17.9 us
    pallas_call x1, Pallas kernels, update(): pl.pallas_call(functools.partial(update_kernel, GHOST * ny, group), in_sp...  10 us
    unnamed x24, local copies, waits for them, and re-layouts  7.42 us
    ppermute x1, waiting for transfers between devices, shards(): ye = lax.ppermute(ye, 'gy', even_pairs(gy))  3.68 us
    pallas_call x1, Pallas kernels, partial_and_edges(): pl.pallas_call(functools.partial(partial_kernel, nx, ny, xpad, gx, gy), i...  3.39 us
    ppermute x1, starting transfers between devices, shards(): ye = lax.ppermute(ye, 'gy', even_pairs(gy))  2.91 us
  transfers between devices with their start and end apart: 4, of which 2 were waited for; matrix products, arithmetic and copies ran while one was open for 0% of the time, Pallas kernels for 0%

profile of v2, /device:TPU:0, one launch (start us, length us, event | category | flops | bytes accessed | tf_op | source)
XLA Modules:
  0.0 71.7 jit_solution(10565462183328444888)
XLA Ops:
  0.6 0.7 convert_element_type.3
  1.3 0.1 copy.9
  1.4 0.2 broadcast_in_dim.2.refs_5_.refs_11_.lb_in
  1.6 0.0 copy-start
  1.6 2.2 %copy-done = f32[8,64,16,128]{3,2,1,0:T(8,128)S(1)} copy-done((f32[8,64,16,128]{3,2,1,0:T(8,128)S(1)}, f32[8,64,16,128]{3,2,1,0:T(8,128)}, u32[]{:S(2)}) %copy-start) | copy-done | bytes 4194328
  3.8 1.0 %copy-done.2 = f32[64,16,128]{2,1,0:T(8,128)S(1)} copy-done((f32[64,16,128]{2,1,0:T(8,128)S(1)}, f32[64,16,128]{2,1,0:T(8,128)}, u32[]{:S(2)}) %copy-start.2) | copy-done | bytes 524312
  4.9 1.0 %copy-done.4 = f32[64,16,128]{2,1,0:T(8,128)S(1)} copy-done((f32[64,16,128]{2,1,0:T(8,128)S(1)}, f32[64,16,128]{2,1,0:T(8,128)}, u32[]{:S(2)}) %copy-start.4) | copy-done | bytes 524312
  5.9 1.0 %copy-done.6 = f32[64,16,128]{2,1,0:T(8,128)S(1)} copy-done((f32[64,16,128]{2,1,0:T(8,128)S(1)}, f32[64,16,128]{2,1,0:T(8,128)}, u32[]{:S(2)}) %copy-start.6) | copy-done | bytes 524312
  6.9 1.0 %copy-done.8 = f32[64,16,128]{2,1,0:T(8,128)S(1)} copy-done((f32[64,16,128]{2,1,0:T(8,128)S(1)}, f32[64,16,128]{2,1,0:T(8,128)}, u32[]{:S(2)}) %copy-start.8) | copy-done | bytes 524312
  8.0 1.0 %copy-done.10 = f32[64,16,128]{2,1,0:T(8,128)S(1)} copy-done((f32[64,16,128]{2,1,0:T(8,128)S(1)}, f32[64,16,128]{2,1,0:T(8,128)}, u32[]{:S(2)}) %copy-start.10) | copy-done | bytes 524312
  9.0 0.8 %sum_and_edges.1 = (f32[64,16,128]{2,1,0:T(8,128)S(1)}, f32[16,16,128]{2,1,0:T(8,128)S(1)}, f32[16,16,128]{2,1,0:T(8,128)S(1)}) custom-call(f32[8,64,16,128]{3,2,1,0:T(8,128)S(1)} %copy-done, f32[64,16,128]{2,1,0:T(8,128)S(1)} %copy-done.2, f32[64,16,128]{2,1,0:T(8,128)S(1)} %copy-done.4, f32[64,16,128]{2,1,0:T(8,128)S(1)} %copy-done.6, ...), custom_call_target="tpu_custom_call" | custom-call | tf_op jit(solution)/shard_map/sum_and_edges/pallas_call | solution.py:94
  9.8 0.6 collective-permute-start
  10.4 0.7 collective-permute-start.1
  11.1 0.3 collective-permute-done.xe_ref
  11.4 0.0 collective-permute-done.1.xo_ref
  11.4 0.0 copy-start.1
  11.4 3.4 %partial_and_edges.1 = (f32[1152,128]{1,0:T(8,128)S(1)}, f32[1152,128]{1,0:T(8,128)S(1)}, f32[1152,128]{1,0:T(8,128)S(1)}, f32[1152,128]{1,0:T(8,128)S(1)}, f32[...) custom-call(f32[64,16,128]{2,1,0:T(8,128)S(1)} %get-tuple-element.20, ...), custom_call_target="tpu_custom_call" | custom-call | tf_op jit(solution)/shard_map/partial_and_edges/pallas_call | solution.py:229
  14.8 2.9 %collective-permute-start.2 = (f32[512,128]{1,0:T(8,128)S(1)}, f32[512,128]{1,0:T(8,128)S(1)}, u32[]{:S(2)}, u32[]{:S(2)}) collective-permute-start(f32[512,128]{1,0:T(8,128)S(1)} %get-tuple-element.30), channel_id=1, source_target_pairs={{0,1},{1,0},{2,3},{3,2},{4,5},{5,4},{6,7},{7,6},{8,9},{9,8},{10,11... | collective-permute-start | bytes 786440 | tf_op jit(solution)/shard_map/ppermute | solution.py:588
  17.7 0.7 collective-permute-start.3
  18.4 3.7 %collective-permute-done.2.ye_ref = f32[512,128]{1,0:T(8,128)S(1)} collective-permute-done((f32[512,128]{1,0:T(8,128)S(1)}, f32[512,128]{1,0:T(8,128)S(1)}, u32[]{:S(2)}, u32[]{:S(2)}) %collective-permute-start.2) | collective-permute-done | bytes 262176 | tf_op jit(solution)/shard_map/ppermute | solution.py:588
  22.1 0.0 collective-permute-done.3.yo_ref
  22.1 17.9 %powers.1 = (f32[8,1024,128]{2,1,0:T(8,128)S(1)}, f32[8,1024,128]{2,1,0:T(8,128)S(1)}, f32[1024,128]{1,0:T(8,128)S(1)}, f32[32,2,128]{2,1,0:T(2,128)S(1)}) custom-call(f32[1152,128]{1,0:T(8,128)S(1)} %get-tuple-element.23.t_ref, f32[1152,128]{1,0:T(8,128)S(1)} %get-tuple-element.24.s_ref, f32[1152,128]{1,0:T(8,128)S(1)} %get-tuple-element.25.fx_ref, ...), custom_call_target="tpu_custom_call" | custom-call | tf_op jit(solution)/shard_map/powers/pallas_call | solution.py:423
  40.0 21.7 %all_to_all.5.parts_ref = f32[32,2,128]{2,1,0:T(2,128)S(1)} all-to-all(f32[32,2,128]{2,1,0:T(2,128)S(1)} %get-tuple-element.32), channel_id=1, replica_groups=mesh['gx'=4,'gy'=8] {'gx','gy'}, dimensions={0} | all-to-all | bytes 65536 | tf_op jit(solution)/shard_map/all_to_all | solution.py:591
  61.7 10.0 %update.1 = (f32[8,1024,128]{2,1,0:T(8,128)}, f32[1024,128]{1,0:T(8,128)}) custom-call(f32[32,2,128]{2,1,0:T(2,128)S(1)} %all_to_all.5.parts_ref, f32[8,1024,128]{2,1,0:T(8,128)S(1)} %get-tuple-element.33.p_ref, f32[8,1024,128]{2,1,0:T(8,128)S(1)} %get-tuple-element.34.q_ref, f32[1024,128]{1,0:T(8,128)S(1)} %get-tuple-element.35.r_ref, ...), custom_call_target="tpu_custom_call" | custom-call | tf_op jit(solution)/shard_map/update/pallas_call | solution.py:558
  (16 shorter events, 0.0 us)
Async XLA Ops:
  1.6 2.2 %copy-start = (f32[8,64,16,128]{3,2,1,0:T(8,128)S(1)}, f32[8,64,16,128]{3,2,1,0:T(8,128)}, u32[]{:S(2)}) copy-start(f32[8,64,16,128]{3,2,1,0:T(8,128)} %it_ref.1) | copy-start | bytes 12582916
  3.8 1.0 %copy-start.2 = (f32[64,16,128]{2,1,0:T(8,128)S(1)}, f32[64,16,128]{2,1,0:T(8,128)}, u32[]{:S(2)}) copy-start(f32[64,16,128]{2,1,0:T(8,128)} %src_in.1) | copy-start | bytes 1572868
  4.8 1.0 %copy-start.4 = (f32[64,16,128]{2,1,0:T(8,128)S(1)}, f32[64,16,128]{2,1,0:T(8,128)}, u32[]{:S(2)}) copy-start(f32[64,16,128]{2,1,0:T(8,128)} %dg_in.1) | copy-start | bytes 1572868
  5.9 1.0 %copy-start.6 = (f32[64,16,128]{2,1,0:T(8,128)S(1)}, f32[64,16,128]{2,1,0:T(8,128)}, u32[]{:S(2)}) copy-start(f32[64,16,128]{2,1,0:T(8,128)} %fx_in.1) | copy-start | bytes 1572868
  6.9 1.0 %copy-start.8 = (f32[64,16,128]{2,1,0:T(8,128)S(1)}, f32[64,16,128]{2,1,0:T(8,128)}, u32[]{:S(2)}) copy-start(f32[64,16,128]{2,1,0:T(8,128)} %fy_in.1) | copy-start | bytes 1572868
  8.0 1.0 %copy-start.10 = (f32[64,16,128]{2,1,0:T(8,128)S(1)}, f32[64,16,128]{2,1,0:T(8,128)}, u32[]{:S(2)}) copy-start(f32[64,16,128]{2,1,0:T(8,128)} %fz_in.1) | copy-start | bytes 1572868
  9.0 2.4 %copy-start.3 = (f32[64,16,128]{2,1,0:T(8,128)S(1)}, f32[64,16,128]{2,1,0:T(8,128)}, u32[]{:S(2)}) copy-start(f32[64,16,128]{2,1,0:T(8,128)} %src_in.1) | copy-start | bytes 1572868
  9.0 2.4 %copy-start.5 = (f32[64,16,128]{2,1,0:T(8,128)S(1)}, f32[64,16,128]{2,1,0:T(8,128)}, u32[]{:S(2)}) copy-start(f32[64,16,128]{2,1,0:T(8,128)} %dg_in.1) | copy-start | bytes 1572868
  9.0 2.4 %copy-start.7 = (f32[64,16,128]{2,1,0:T(8,128)S(1)}, f32[64,16,128]{2,1,0:T(8,128)}, u32[]{:S(2)}) copy-start(f32[64,16,128]{2,1,0:T(8,128)} %fx_in.1) | copy-start | bytes 1572868
  9.0 2.4 %copy-start.9 = (f32[64,16,128]{2,1,0:T(8,128)S(1)}, f32[64,16,128]{2,1,0:T(8,128)}, u32[]{:S(2)}) copy-start(f32[64,16,128]{2,1,0:T(8,128)} %fy_in.1) | copy-start | bytes 1572868
  9.0 2.4 %copy-start.11 = (f32[64,16,128]{2,1,0:T(8,128)S(1)}, f32[64,16,128]{2,1,0:T(8,128)}, u32[]{:S(2)}) copy-start(f32[64,16,128]{2,1,0:T(8,128)} %fz_in.1) | copy-start | bytes 1572868
  9.8 1.5 %collective-permute-start = (f32[16,16,128]{2,1,0:T(8,128)S(1)}, f32[16,16,128]{2,1,0:T(8,128)S(1)}, u32[]{:S(2)}, u32[]{:S(2)}) collective-permute-start(f32[16,16,128]{2,1,0:T(8,128)S(1)} %get-tuple-element.21), channel_id=1, source_target_pairs={{0,8},{8,0},{16,24},{24,16},{1,9},{9,1},{17,25},{25,17},{2,10},{10... | collective-permute-start | bytes 393224 | tf_op jit(solution)/shard_map/ppermute | solution.py:585
  10.4 1.0 %collective-permute-start.1 = (f32[16,16,128]{2,1,0:T(8,128)S(1)}, f32[16,16,128]{2,1,0:T(8,128)S(1)}, u32[]{:S(2)}, u32[]{:S(2)}) collective-permute-start(f32[16,16,128]{2,1,0:T(8,128)S(1)} %get-tuple-element.22), channel_id=1, source_target_pairs={{8,16},{16,8},{9,17},{17,9},{10,18},{18,10},{11,19},{19,11},{12,20... | collective-permute-start | bytes 393224 | tf_op jit(solution)/shard_map/ppermute | solution.py:586
  11.4 50.3 %copy-start.1 = (f32[8,64,16,128]{3,2,1,0:T(8,128)S(1)}, f32[8,64,16,128]{3,2,1,0:T(8,128)}, u32[]{:S(2)}) copy-start(f32[8,64,16,128]{3,2,1,0:T(8,128)} %it_ref.1) | copy-start | bytes 12582916
  14.8 7.3 %collective-permute-start.2 = (f32[512,128]{1,0:T(8,128)S(1)}, f32[512,128]{1,0:T(8,128)S(1)}, u32[]{:S(2)}, u32[]{:S(2)}) collective-permute-start(f32[512,128]{1,0:T(8,128)S(1)} %get-tuple-element.30), channel_id=1, source_target_pairs={{0,1},{1,0},{2,3},{3,2},{4,5},{5,4},{6,7},{7,6},{8,9},{9,8},{10,11... | collective-permute-start | bytes 786440 | tf_op jit(solution)/shard_map/ppermute | solution.py:588
  17.7 4.4 %collective-permute-start.3 = (f32[512,128]{1,0:T(8,128)S(1)}, f32[512,128]{1,0:T(8,128)S(1)}, u32[]{:S(2)}, u32[]{:S(2)}) collective-permute-start(f32[512,128]{1,0:T(8,128)S(1)} %get-tuple-element.31), channel_id=1, source_target_pairs={{1,2},{2,1},{3,4},{4,3},{5,6},{6,5},{9,10},{10,9},{11,12},{12,11},... | collective-permute-start | bytes 786440 | tf_op jit(solution)/shard_map/ppermute | solution.py:589

commit v3 on v0

v3 whole, which is shorter than its diff:
```python
import functools

import jax
import jax.numpy as jnp
from jax import lax
from jax.experimental import pallas as pl
from jax.experimental.pallas import tpu as pltpu
from jax.sharding import PartitionSpec as P

ENLARGE = 8
SHIFT = 6.5
F32 = jnp.float32
HIGHEST = lax.Precision.HIGHEST
PAIRS = [(j, k) for j in range(ENLARGE) for k in range(j, ENLARGE)]
VMEM_LIMIT = 40 * 1024 * 1024
PAD = 8
SENT = 2


def iota(shape, dim):
    return lax.broadcasted_iota(jnp.int32, shape, dim)


def even_pairs(count):
    return [(i, i ^ 1) for i in range(count) if (i ^ 1) < count]


def odd_pairs(count):
    return [(i, ((i - 1) ^ 1) + 1) for i in range(1, count) if ((i - 1) ^ 1) + 1 < count]


def vmem(count):
    return [pl.BlockSpec(memory_space=pltpu.VMEM)] * count


def hbm(count):
    return [pl.BlockSpec(memory_space=pltpu.HBM)] * count


def pinned(value):
    return pltpu.with_memory_space_constraint(value, pltpu.HBM)


def array(*shape):
    return jax.ShapeDtypeStruct(shape, F32)


def params():
    return pltpu.CompilerParams(vmem_limit_bytes=VMEM_LIMIT)


def aligned(value):
    return value if isinstance(value, int) else pl.multiple_of(value, 8)


def eight(start):
    return pl.ds(aligned(start), 8)


def near(start):
    return pl.ds(start, 8)


def loop(count, body, **kw):
    def wrapped(i, carry):
        body(i)
        return carry

    lax.fori_loop(0, count, wrapped, 0, **kw)


def load_kernel(
    it_hbm, src_hbm, dg_hbm, fx_hbm, fy_hbm, fz_hbm, label_ref,
    s_out, src_out, dg_out, fx_out, fy_out, fz_out, lb_out, even_out, odd_out,
    work, sem_it, sem_field,
):
    ny, nx, nz = s_out.shape
    pairs = list(zip((src_hbm, dg_hbm, fx_hbm, fy_hbm, fz_hbm), (src_out, dg_out, fx_out, fy_out, fz_out)))

    def copy_it(y):
        return pltpu.make_async_copy(it_hbm.at[:, :, y], work.at[:, y], sem_it.at[y])

    def copy_field(f, y):
        return pltpu.make_async_copy(pairs[f][0].at[:, y], pairs[f][1].at[y], sem_field.at[f, y])

    def start(y):
        copy_it(y).start()
        for f in range(len(pairs)):
            copy_field(f, y).start()

    loop(ny, start)

    spot = iota((nx, nx), 0) == iota((nx, nx), 1)
    ones = jnp.ones((nx, nz), jnp.bfloat16)
    labels = label_ref[...].astype(F32)
    for y in range(ny):
        row = jnp.where(spot, labels[y : y + 1], 0.0).astype(jnp.bfloat16)
        lb_out[y] = jnp.dot(row, ones, preferred_element_type=F32)

    def add(y):
        copy_it(y).wait()
        for r in range(0, nx, 8):
            total = work[0, y, r : r + 8]
            for j in range(1, ENLARGE):
                total = total + work[j, y, r : r + 8]
            s_out[y, r : r + 8] = total

    loop(ny, add)

    def finish(y):
        for f in range(len(pairs)):
            copy_field(f, y).wait()

    loop(ny, finish)
    even = lax.rem(lax.axis_index("gx"), 2) == 0
    sub = iota((8, nz), 0)

    def pack(y):
        hi = slice(nx - 8, nx)
        lo = slice(0, 8)
        roll = lambda v, n: pltpu.roll(v, n, 0)
        high1 = jnp.where(sub >= 5, s_out[y, hi], jnp.where(sub < 2, roll(lb_out[y, hi], 2), roll(fx_out[y, hi], 5)))
        low1 = jnp.where(sub < 3, s_out[y, lo], jnp.where(sub >= 6, roll(lb_out[y, lo], 6), roll(fx_out[y, lo], 3)))

        def second(at, first):
            values = src_out[y, at]
            for n, ref in enumerate((dg_out, fy_out, fz_out)):
                begin = (first + 2 * n + 2) % 8
                inside = jnp.logical_or(sub == begin, sub == begin + 1)
                values = jnp.where(inside, roll(ref[y, at], 2 * n + 2), values)
            return values

        high2 = second(hi, 6)
        low2 = second(lo, 0)
        for part, high, low in ((0, high1, low1), (1, high2, low2)):
            even_out[part, y] = jnp.where(even, high, low)
            odd_out[part, y] = jnp.where(even, low, high)

    loop(ny, pack)


def load(iterates, fields, labels):
    _, nx, ny, nz = iterates.shape
    field = array(ny, nx, nz)
    edge = array(2, ny, 8, nz)
    return pl.pallas_call(
        load_kernel,
        in_specs=hbm(6) + vmem(1),
        out_specs=vmem(9),
        out_shape=[field] * 7 + [edge] * 2,
        scratch_shapes=[
            pltpu.VMEM((ENLARGE, ny, nx, nz), F32),
            pltpu.SemaphoreType.DMA((ny,)),
            pltpu.SemaphoreType.DMA((5, ny)),
        ],
        compiler_params=params(),
        name="load",
    )(*[pinned(a) for a in (iterates, *fields)], labels.T)


def blocks_of(nx):
    wide = nx + PAD
    sizes = (wide, wide, wide, wide, nx, nx, nx, 8)
    starts = [sum(sizes[:i]) for i in range(len(sizes) + 1)]
    return wide, starts


def partial_kernel(
    gx, gy,
    s_in, src_in, dg_in, fx_in, fy_in, fz_in, lb_in, xe_ref, xo_ref,
    t_out, s_out, fx_out, fy_out, dg_out, fz_out, lb_out, ye_ref, yo_ref,
    src_ext,
):
    ny, nx, nz = s_in.shape
    pitch = nx + 2 * PAD
    lane = iota((8, nz), 1)
    even_x = lax.rem(lax.axis_index("gx"), 2) == 0
    last_x = lax.axis_index("gx") == gx - 1
    last_y = lax.axis_index("gy") == gy - 1
    last_row = jnp.logical_and(iota((8, nz), 0) == 7, last_x)

    def fill(y):
        top = jnp.logical_and(last_y, y == ny - 1)
        fy_of = lambda v: jnp.where(top, 0.0, v)
        fz_of = lambda v: jnp.where(lane == nz - 1, 0.0, v)
        base = y * pitch
        roll = lambda v, n: pltpu.roll(v, n, 0)
        for at, is_low in ((0, True), (PAD + nx, False)):
            one, two = [
                jnp.where(even_x == is_low, xo_ref[part, y], xe_ref[part, y]) for part in range(2)
            ]
            here = eight(base + at)
            s_out[here] = one
            fx_out[here] = roll(one, 3 if is_low else 5)
            lb_out[here] = roll(one, 6 if is_low else 2)
            src_ext[here] = two
            dg_out[here] = roll(two, 6)
            fy_out[here] = fy_of(roll(two, 4))
            fz_out[here] = fz_of(roll(two, 2))
        for r in range(0, nx, 8):
            here = eight(base + PAD + r)
            span = slice(r, r + 8)
            s_out[here] = s_in[y, span]
            face = fx_in[y, span]
            fx_out[here] = jnp.where(last_row, 0.0, face) if r == nx - 8 else face
            lb_out[here] = lb_in[y, span]
            src_ext[here] = src_in[y, span]
            dg_out[here] = dg_in[y, span]
            fy_out[here] = fy_of(fy_in[y, span])
            fz_out[here] = fz_of(fz_in[y, span])

    loop(ny, fill)

    def layer(y, down=True, up=True):
        base = y * pitch
        for r in range(0, pitch, 8):
            at = base + r
            here = eight(at)
            s, fx, fz = s_out[here], fx_out[here], fz_out[here]
            if r == 0:
                sm, fxm = pltpu.roll(s, 1, 0), pltpu.roll(fx, 1, 0)
            else:
                sm, fxm = s_out[near(at - 1)], fx_out[near(at - 1)]
            sp = pltpu.roll(s, 7, 0) if r == pitch - 8 else s_out[near(at + 1)]
            total = dg_out[here] * s - fx * sp - fxm * sm
            if up:
                total = total - fy_out[here] * s_out[eight(at + pitch)]
            if down:
                total = total - fy_out[eight(at - pitch)] * s_out[eight(at - pitch)]
            total = total - fz * pltpu.roll(s, nz - 1, 1) - pltpu.roll(fz * s, 1, 1)
            t_out[here] = src_ext[here] - total

    layer(0, down=False)
    layer(ny - 1, up=False)
    loop(ny - 2, lambda i: layer(i + 1))

    even_y = lax.rem(lax.axis_index("gy"), 2) == 0
    wide, starts = blocks_of(nx)

    def pack(dest, is_high):
        first = jnp.where(is_high, ny - 1, 0) * pitch
        second = jnp.where(is_high, ny - 2, 1) * pitch
        between = jnp.where(is_high, ny - 2, 0) * pitch

        def line(ref, base):
            return ref[pl.ds(base + (PAD - SENT), wide)]

        def inner(ref, base):
            return ref[pl.ds(pl.multiple_of(base + PAD, 8), nx)]

        parts = (
            line(t_out, first),
            line(s_out, first),
            line(fy_out, first),
            line(fx_out, first),
            inner(fy_out, between) * inner(t_out, second),
            inner(dg_out, first),
            inner(fz_out, first),
        )
        for b, values in enumerate(parts):
            dest[starts[b] : starts[b + 1]] = values
        spot = iota((wide, nz), 0) == iota((wide, nz), 1)
        one = jnp.sum(jnp.where(spot, line(lb_out, first), 0.0), axis=0, keepdims=True)
        two = jnp.sum(jnp.where(spot, line(lb_out, second), 0.0), axis=0, keepdims=True)
        which = iota((8, nz), 0)
        dest[starts[7] : starts[8]] = jnp.where(which == 0, one, jnp.where(which == 1, two, 0.0))

    pack(ye_ref, even_y)
    pack(yo_ref, jnp.logical_not(even_y))


def partial_residual(fields, xe, xo, gx, gy):
    ny, nx, nz = fields[0].shape
    rows = ny * (nx + 2 * PAD)
    ext = array(rows, nz)
    pack = array(blocks_of(nx)[1][-1], nz)
    return pl.pallas_call(
        functools.partial(partial_kernel, gx, gy),
        in_specs=vmem(9),
        out_specs=vmem(9),
        out_shape=[ext] * 7 + [pack] * 2,
        scratch_shapes=[pltpu.VMEM((rows, nz), F32)],
        compiler_params=params(),
        name="partial_residual",
    )(*fields, xe, xo)


def spread(parts):
    fields = []
    for j in range(ENLARGE):
        total = None
        for values, label in parts:
            term = jnp.where(label == float(j), values, 0.0)
            total = term if total is None else total + term
        fields.append(total)
    return fields


def along_z(fz, values):
    nz = values.shape[-1]
    return fz * pltpu.roll(values, nz - 1, 1) + pltpu.roll(fz * values, 1, 1)


def edge_near(ref, at, shift, last):
    if last == shift:
        return pltpu.roll(ref[eight(at)], 1 if shift < 0 else 7, 0)
    return ref[near(at + shift)]


def zeros_like_pairs(nz, count):
    return tuple(jnp.zeros((8, nz), F32) for _ in range(count))


def dot_own(sums, r, label, p):
    b = [jnp.where(label == float(j), r, 0.0) for j in range(ENLARGE)]
    n = len(PAIRS)
    own = tuple(t + v * v for t, v in zip(sums[n:], b))
    return tuple(t + b[j] * p[k] for t, (j, k) in zip(sums, PAIRS)) + own


def dot_pairs(sums, p, q):
    return tuple(t + p[j] * q[k] for t, (j, k) in zip(sums, PAIRS))


def clean_kernel(
    ny, nx,
    t_ref, fx_ref, fy_ref, dg_ref, fz_ref, lb_ref,
    p_out, q_out, acc_out,
):
    nz = t_ref.shape[-1]
    pitch = nx + 2 * PAD
    chunks = nx // 8

    def first(i):
        layer = (i + 2) * pitch
        for r in range(0, pitch, 8):
            at = layer + r
            last = -1 if r == 0 else (1 if r == pitch - 8 else 0)
            here = eight(at)
            value = t_ref[here]
            below, above = eight(at - pitch), eight(at + pitch)
            parts = [
                ((dg_ref[here] - SHIFT) * value - along_z(fz_ref[here], value), lb_ref[here]),
                (-fx_ref[here] * edge_near(t_ref, at, 1, last), edge_near(lb_ref, at, 1, last)),
                (-edge_near(fx_ref, at, -1, last) * edge_near(t_ref, at, -1, last), edge_near(lb_ref, at, -1, last)),
                (-fy_ref[here] * t_ref[above], lb_ref[above]),
                (-fy_ref[below] * t_ref[below], lb_ref[below]),
            ]
            for j, values in enumerate(spread(parts)):
                p_out[j, eight(i * pitch + r)] = values

    loop(ny - 4, first)

    def second(n):
        i, c = n // (chunks // 2), lax.rem(n, chunks // 2)
        for h in range(2):
            r = c * 16 + h * 8
            at = (i + 3) * pitch + PAD + r
            own = (i + 1) * pitch + PAD + r
            here = eight(at)
            dg, fz, fxp, fxm = dg_ref[here], fz_ref[here], fx_ref[here], fx_ref[near(at - 1)]
            fyp, fym = fy_ref[here], fy_ref[eight(at - pitch)]
            for j in range(ENLARGE):
                p = p_out[j, eight(own)]
                q = dg * p - fxp * p_out[j, near(own + 1)] - fxm * p_out[j, near(own - 1)]
                q = q - fyp * p_out[j, eight(own + pitch)] - fym * p_out[j, eight(own - pitch)]
                q_out[j, eight(i * nx + r)] = q - along_z(fz, p)

    loop((ny - 6) * chunks // 2, second)

    def fields_at(ref, at):
        return [ref[j, eight(at)] for j in range(ENLARGE)]

    def own_dots(n, sums):
        row = (n // chunks) * pitch + PAD + lax.rem(n, chunks) * 8
        shifted = eight(row + 2 * pitch)
        return dot_own(sums, t_ref[shifted], lb_ref[shifted], fields_at(p_out, row))

    def p_dots(n, sums):
        row = (n // chunks) * pitch + PAD + lax.rem(n, chunks) * 8
        p = fields_at(p_out, row)
        return dot_pairs(sums, p, p)

    def q_dots(n, sums):
        row = (n // chunks + 1) * pitch + PAD + lax.rem(n, chunks) * 8
        return dot_pairs(sums, fields_at(p_out, row), fields_at(q_out, n * 8))

    slot = 0
    for dots, layers, count in (
        (own_dots, ny - 4, len(PAIRS) + ENLARGE), (p_dots, ny - 4, len(PAIRS)), (q_dots, ny - 6, len(PAIRS)),
    ):
        sums = lax.fori_loop(0, layers * chunks, dots, zeros_like_pairs(nz, count), unroll=4)
        for values in sums:
            acc_out[slot] = values
            slot += 1


def clean_powers(ext, ny, nx):
    t, _, fx, fy, dg, fz, lb = ext
    nz = t.shape[-1]
    pitch = nx + 2 * PAD
    return pl.pallas_call(
        functools.partial(clean_kernel, ny, nx),
        in_specs=vmem(6),
        out_specs=vmem(3),
        out_shape=[
            array(ENLARGE, (ny - 4) * pitch, nz),
            array(ENLARGE, (ny - 6) * nx, nz),
            array(3 * len(PAIRS) + ENLARGE, 8, nz),
        ],
        compiler_params=params(),
        cost_estimate=pl.CostEstimate(flops=60_000_000, bytes_accessed=12_000_000, transcendentals=0),
        name="clean_powers",
    )(t, fx, fy, dg, fz, lb)


def edge_kernel(
    ny, nx, devices,
    t_ref, s_ref, fx_ref, fy_ref, dg_ref, fz_ref, lb_ref, pc_ref, acc_ref, ye_ref, yo_ref,
    p_out, q_out, r_out, gram_out,
    packs, face_g, fx_g, lb_g, lb_g2, rows_acc,
):
    nz = t_ref.shape[-1]
    pitch = nx + 2 * PAD
    chunks = nx // 8
    wide, starts = blocks_of(nx)
    odd = lax.rem(lax.axis_index("gy"), 2)
    packs[1 - odd] = ye_ref[...]
    packs[odd] = yo_ref[...]
    p_layers = (-1, 0, 1, ny - 2, ny - 1, ny)
    q_layers = (0, 1, 2, ny - 3, ny - 2, ny - 1)
    r_layers = (-1, 0, ny - 1, ny)
    left = PAD - SENT

    def packed(side, b):
        return packs[side, starts[b] : starts[b + 1]]

    for side in range(2):
        inner, outer = (0, -1) if side == 0 else (ny - 1, ny)
        base = pl.ds(inner * pitch + left, wide)
        face = packed(side, 2) if side == 0 else fy_ref[base]
        at = lambda y: pl.ds(r_layers.index(y) * pitch + left, wide)
        r_out[at(outer)] = packed(side, 0) + face * s_ref[base]
        r_out[at(inner)] = t_ref[base] + face * packed(side, 1)
        if side == 0:
            face_g[pl.ds(left, wide)] = face
        ghost = pl.ds(side * pitch + left, wide)
        fx_g[ghost] = packed(side, 3)
        labels = packed(side, 7)
        spot = iota((wide, nz), 0) == iota((wide, nz), 1)
        for r, dest in ((0, lb_g), (1, lb_g2)):
            column = jnp.sum(jnp.where(spot, labels[r : r + 1], 0.0), axis=1, keepdims=True)
            dest[ghost] = jnp.broadcast_to(column, (wide, nz))

    def r_at(y):
        return (r_out, r_layers.index(y) * pitch) if y in r_layers else (t_ref, y * pitch)

    def label_at(y):
        if 0 <= y < ny:
            return lb_ref, y * pitch
        return lb_g, (0 if y < 0 else pitch)

    def face_at(y):
        return (face_g, 0) if y < 0 else (fy_ref, y * pitch)

    def p_at(y):
        return (p_out, p_layers.index(y) * pitch) if y in p_layers else (pc_ref, (y - 2) * pitch)

    def first(y, r, last=0):
        ref, base = r_at(y)
        labels, label_base = label_at(y)
        at = base + r
        mark = label_base + r
        value = ref[eight(at)]
        if 0 <= y < ny:
            dg, fz = dg_ref[eight(y * pitch + r)], fz_ref[eight(y * pitch + r)]
            fxs, fx_base = fx_ref, y * pitch
        else:
            side = 0 if y < 0 else 1
            dg, fz = [packs[side, eight(starts[b] + r - PAD)] for b in (5, 6)]
            fxs, fx_base = fx_g, side * pitch
        fx_row = fx_base + r
        parts = [
            ((dg - SHIFT) * value - along_z(fz, value), labels[eight(mark)]),
            (-fxs[eight(fx_row)] * edge_near(ref, at, 1, last), edge_near(labels, mark, 1, last)),
            (-edge_near(fxs, fx_row, -1, last) * edge_near(ref, at, -1, last), edge_near(labels, mark, -1, last)),
        ]
        for step in (-1, 1):
            if not -1 <= y + step <= ny:
                side = 0 if y < 0 else 1
                parts.append((-packs[side, eight(starts[4] + r - PAD)], lb_g2[eight(side * pitch + r)]))
                continue
            ref2, base2 = r_at(y + step)
            labels2, label_base2 = label_at(y + step)
            face, face_base = face_at(min(y, y + step))
            parts.append((-face[eight(face_base + r)] * ref2[eight(base2 + r)], labels2[eight(label_base2 + r)]))
        for j, values in enumerate(spread(parts)):
            p_out[j, eight(p_layers.index(y) * pitch + r)] = values

    for y in p_layers:
        if 0 <= y < ny:
            first(y, 0, -1)
            first(y, pitch - 8, 1)
        loop(chunks, lambda c, y=y: first(y, aligned(PAD + c * 8)), unroll=2)

    def second(y, c):
        r = aligned(PAD + c * 8)
        row = y * pitch + r
        here = eight(row)
        dg, fz, fxp, fxm = dg_ref[here], fz_ref[here], fx_ref[here], fx_ref[near(row - 1)]
        face, face_base = face_at(y - 1)
        fyp, fym = fy_ref[here], face[eight(face_base + r)]
        (mid, mid_base), (low, low_base), (high, high_base) = p_at(y), p_at(y - 1), p_at(y + 1)
        for j in range(ENLARGE):
            p = mid[j, eight(mid_base + r)]
            q = dg * p - fxp * mid[j, near(mid_base + r + 1)] - fxm * mid[j, near(mid_base + r - 1)]
            q = q - fyp * high[j, eight(high_base + r)] - fym * low[j, eight(low_base + r)]
            q_out[j, eight(q_layers.index(y) * nx + c * 8)] = q - along_z(fz, p)

    for y in q_layers:
        loop(chunks, lambda c, y=y: second(y, c), unroll=2)

    def fields_at(ref, at):
        return [ref[j, eight(at)] for j in range(ENLARGE)]

    n = len(PAIRS)
    stored = [acc_ref[i] for i in range(n + ENLARGE)]
    sums = tuple(stored)
    for y in (0, 1, ny - 2, ny - 1):

        def body(c, sums, y=y):
            r = PAD + c * 8
            ref, base = r_at(y)
            own = fields_at(p_out, p_layers.index(y) * pitch + r)
            return dot_own(sums, ref[eight(base + r)], lb_ref[eight(y * pitch + r)], own)

        sums = lax.fori_loop(0, chunks, body, sums, unroll=4)
    rows_acc[...] = jnp.zeros_like(rows_acc)
    span = ENLARGE * ENLARGE

    def put(slot, values):
        rows_acc[slot : slot + 1] = jnp.sum(values, axis=0, keepdims=True)

    def put_pairs(which, sums):
        for (j, k), values in zip(PAIRS, sums):
            put(which * span + j * ENLARGE + k, values)
            if j != k:
                put(which * span + k * ENLARGE + j, values)

    put_pairs(0, sums)
    for j in range(ENLARGE):
        put(3 * span + j * ENLARGE + j, sums[n + j])
    begin = n + ENLARGE
    for which, layers in ((1, (0, 1, ny - 2, ny - 1)), (2, q_layers)):
        sums = tuple(acc_ref[begin + i] for i in range(n))
        begin += n
        for y in layers:

            def body(c, sums, y=y, which=which):
                ref, base = p_at(y)
                p = fields_at(ref, base + PAD + c * 8)
                q = p if which == 1 else fields_at(q_out, q_layers.index(y) * nx + c * 8)
                return dot_pairs(sums, p, q)

            sums = lax.fori_loop(0, chunks, body, sums, unroll=4)
        put_pairs(which, sums)
    ones = jnp.ones((8, nz), F32)
    flat = lax.dot_general(
        ones, rows_acc[...], (((1,), (1,)), ((), ())), precision=HIGHEST, preferred_element_type=F32
    )
    half = 2 * span
    pair = jnp.where(iota((2, half), 0) == 0, flat[0:2, 0:half], flat[0:2, half : 2 * half])
    for d in range(devices):
        gram_out[d] = pair


def edge_powers(ext, pc, acc, ye, yo, ny, nx, devices):
    nz = pc.shape[-1]
    pitch = nx + 2 * PAD
    half = 2 * ENLARGE * ENLARGE
    return pl.pallas_call(
        functools.partial(edge_kernel, ny, nx, devices),
        in_specs=vmem(11),
        out_specs=vmem(4),
        out_shape=[
            array(ENLARGE, 6 * pitch, nz), array(ENLARGE, 6 * nx, nz), array(4 * pitch, nz), array(devices, 2, half),
        ],
        scratch_shapes=[
            pltpu.VMEM((2,) + ye.shape, F32),
            pltpu.VMEM((pitch, nz), F32),
            pltpu.VMEM((2 * pitch, nz), F32),
            pltpu.VMEM((2 * pitch, nz), F32),
            pltpu.VMEM((2 * pitch, nz), F32),
            pltpu.VMEM((2 * half, nz), F32),
        ],
        compiler_params=params(),
        name="edge_powers",
    )(*ext, pc, acc, ye, yo)


def solve_columns(parts):
    nz = parts.shape[-1]
    span = ENLARGE * ENLARGE
    v = jnp.sum(parts, axis=0)
    lhs = jnp.concatenate([jnp.broadcast_to(v[0:1], (8, nz)), jnp.broadcast_to(v[1:2], (8, nz))], axis=1)
    source = iota((8, 2 * nz), 1)
    lhs = jnp.where(iota((8, 2 * nz), 0) == lax.rem(source, span) // ENLARGE, lhs, 0.0)
    k = iota((2 * nz, nz), 0)
    n = iota((2 * nz, nz), 1)
    which = k // span
    column = lax.rem(k, ENLARGE)

    def place(block, offset, scale):
        return jnp.where(jnp.logical_and(which == block, n == column + offset), scale, 0.0)

    upper = place(0, 0, 1.0) + place(3, 0, SHIFT) + place(1, 8, 1.0) + place(0, 8, SHIFT) + place(3, 16, 1.0)
    lower = place(1, 0, 1.0) + place(0, 0, SHIFT) + place(2, 8, 1.0) + place(0, 16, 1.0)
    dot = functools.partial(jnp.dot, precision=HIGHEST, preferred_element_type=F32)
    m = jnp.concatenate([dot(lhs, upper), dot(lhs, lower)], axis=0)
    row = iota(m.shape, 0)
    for i in range(2 * ENLARGE):
        pivot = m[i : i + 1] / m[i : i + 1, i : i + 1]
        m = jnp.where(row == i, pivot, m - m[:, i : i + 1] * pivot)
    return m


def update_kernel(
    ny, nx, parts_ref, pc_ref, qc_ref, pd_ref, qd_ref, t_ref, rd_ref, lb_ref, it_hbm,
    it_out, r_out,
    table, weights, onehot, own, work, r_work, sem_in, sem_out, sem_r,
):
    nz = t_ref.shape[-1]
    pitch = nx + 2 * PAD
    two = 2 * ENLARGE
    square = ENLARGE * ENLARGE

    def copy_in(y):
        return pltpu.make_async_copy(it_hbm.at[:, :, y], work.at[:, y], sem_in.at[y])

    def copy_out(y):
        return pltpu.make_async_copy(work.at[:, y], it_out.at[:, :, y], sem_out.at[y])

    def copy_r(y):
        return pltpu.make_async_copy(r_work.at[y], r_out.at[:, y], sem_r.at[y])

    loop(ny, lambda y: copy_in(y).start())

    def mark(y):
        lane = iota((nx, nz), 1)
        labels = lb_ref[pl.ds(pl.multiple_of(y * pitch + PAD, 8), nx)]
        chosen = jnp.logical_and(lane < 3 * ENLARGE, lax.rem(lane, ENLARGE).astype(F32) == labels)
        onehot[pl.ds(pl.multiple_of(y * nx, nx), nx)] = jnp.where(chosen, 1.0, 0.0).astype(jnp.bfloat16)

    loop(ny, mark)

    m = solve_columns(parts_ref[...])
    lane = iota(m.shape, 1)
    inside = jnp.logical_and(lane >= two, lane < two + ENLARGE)
    carried = jnp.sum(jnp.where(inside, m, 0.0), axis=1, keepdims=True)
    for j in range(ENLARGE):
        for k in range(ENLARGE):
            value = m[ENLARGE + k : ENLARGE + k + 1, two + j : two + j + 1]
            table[j * ENLARGE + k] = jnp.broadcast_to(value, (8, nz))
    for k in range(two):
        table[square + k] = jnp.broadcast_to(carried[k : k + 1], (8, nz))
    lane = iota((ENLARGE, nz), 1)
    mine = pltpu.roll(m[0:ENLARGE], nz - two, 1)
    mine = jnp.where(lane < ENLARGE, mine, jnp.where(lane == ENLARGE, carried[0:ENLARGE], 0.0))
    high = mine.astype(jnp.bfloat16).astype(F32)
    mid = (mine - high).astype(jnp.bfloat16).astype(F32)
    weights[...] = jnp.zeros_like(weights)
    weights[0:8] = high
    weights[8:16] = mid
    weights[16:24] = mine - high - mid
    own[...] = jnp.dot(onehot[...], weights[...].astype(jnp.bfloat16), preferred_element_type=F32)

    def layer(y, p_ref, p_base, q_ref, q_base, r_ref, r_base):
        copy_in(y).wait()

        def body(c):
            x = [c * 16, c * 16 + 8]
            at = [eight(v) for v in x]
            r = [r_ref[eight(r_base + v)] for v in x]
            p = [[p_ref[k, eight(p_base + v)] for k in range(ENLARGE)] for v in x]
            mine = [own[eight(y * nx + v)] for v in x]
            for j in range(ENLARGE):
                scale = [table[j * ENLARGE + k] for k in range(ENLARGE)]
                for h in range(2):
                    total = work[j, y, at[h]] + mine[h][:, j : j + 1] * r[h]
                    for k in range(ENLARGE):
                        total = total + scale[k] * p[h][k]
                    work[j, y, at[h]] = total
            scale = [table[square + k] for k in range(two)]
            for h in range(2):
                total = r[h] - (SHIFT * mine[h][:, ENLARGE : ENLARGE + 1]) * r[h]
                for k in range(ENLARGE):
                    q = q_ref[k, eight(q_base + x[h])]
                    total = total - scale[k] * p[h][k] - scale[ENLARGE + k] * q
                r_work[y, at[h]] = total

        loop(nx // 16, body)
        copy_out(y).start()
        copy_r(y).start()

    def clean(i):
        y = i + 3
        layer(y, pc_ref, (i + 1) * pitch + PAD, qc_ref, i * nx, t_ref, y * pitch + PAD)

    loop(ny - 6, clean)
    p_layers = (-1, 0, 1, ny - 2, ny - 1, ny)
    q_layers = (0, 1, 2, ny - 3, ny - 2, ny - 1)
    r_layers = (-1, 0, ny - 1, ny)
    for i, y in enumerate(q_layers):
        p = (pd_ref, p_layers.index(y) * pitch + PAD) if y in p_layers else (pc_ref, (y - 2) * pitch + PAD)
        r = (rd_ref, r_layers.index(y) * pitch + PAD) if y in r_layers else (t_ref, y * pitch + PAD)
        layer(y, *p, qd_ref, i * nx, *r)
    loop(ny, lambda y: copy_out(y).wait())
    loop(ny, lambda y: copy_r(y).wait())


def update(parts, pc, qc, pd, qd, t, rd, labels, iterates):
    _, nx, ny, nz = iterates.shape
    return pl.pallas_call(
        functools.partial(update_kernel, ny, nx),
        in_specs=vmem(8) + hbm(1),
        out_specs=hbm(2),
        out_shape=[array(ENLARGE, nx, ny, nz), array(nx, ny, nz)],
        scratch_shapes=[
            pltpu.VMEM((ENLARGE * ENLARGE + 2 * ENLARGE, 8, nz), F32),
            pltpu.VMEM((nz, nz), F32),
            pltpu.VMEM((ny * nx, nz), jnp.bfloat16),
            pltpu.VMEM((ny * nx, nz), F32),
            pltpu.VMEM((ENLARGE, ny, nx, nz), F32),
            pltpu.VMEM((ny, nx, nz), F32),
            pltpu.SemaphoreType.DMA((ny,)),
            pltpu.SemaphoreType.DMA((ny,)),
            pltpu.SemaphoreType.DMA((ny,)),
        ],
        compiler_params=params(),
        name="update",
    )(parts, pc, qc, pd, qd, t, rd, labels, pinned(iterates))


def shards(gx, gy, source, diagonal, face_x, face_y, face_z, iterates, labels):
    _, nx, ny, nz = iterates.shape
    *fields, xe, xo = load(iterates, (source, diagonal, face_x, face_y, face_z), labels)
    xe = lax.ppermute(xe, "gx", even_pairs(gx))
    xo = lax.ppermute(xo, "gx", odd_pairs(gx))
    *ext, ye, yo = partial_residual(fields, xe, xo, gx, gy)
    ye = lax.ppermute(ye, "gy", even_pairs(gy))
    yo = lax.ppermute(yo, "gy", odd_pairs(gy))
    pc, qc, acc = clean_powers(ext, ny, nx)
    pd, qd, rd, gram = edge_powers(ext, pc, acc, ye, yo, ny, nx, gx * gy)
    parts = lax.all_to_all(gram, ("gx", "gy"), 0, 0, tiled=True)
    return update(parts, pc, qc, pd, qd, ext[0], rd, ext[-1], iterates)


def solution(mesh):
    placed = (
        P("gx", "gy", None),
        P("gx", "gy", None),
        P("gx", "gy", None),
        P("gx", "gy", None),
        P("gx", "gy", None),
        P(None, "gx", "gy", None),
        P("gx", "gy"),
    )
    return jax.shard_map(
        functools.partial(shards, mesh.shape["gx"], mesh.shape["gy"]),
        mesh=mesh,
        in_specs=placed,
        out_specs=(P(None, "gx", "gy", None), P("gx", "gy", None)),
        check_vma=False,
    )
```

time: 178 us -> 61.8 us (0.35)
  starting transfers between devices: 44.6 us -> 4.78 us
  matrix products: 37.9 us -> 0 us
  Pallas kernels: 0 us -> 35.5 us
  other arithmetic: 29 us -> 0 us
  blocking collectives: 44.6 us -> 19.6 us
  waiting for transfers between devices: 14.8 us -> 0.33 us
  local copies, waits for them, and re-layouts: 5.36 us -> 0.69 us
    psum x1 -> x0, blocking collectives: 44.6 us -> none  [shards(): gram = lax.psum(gram_local, ('gx', 'gy'))]
    ppermute x16 -> x4, starting transfers between devices: 44.6 us -> 4.78 us  [the longest x1 2.9 us: shards(): ye = lax.ppermute(ye, 'gy', even_pairs(gy))]
    dot_general x8 -> x0, matrix products: 37.3 us -> none  [the longest x1 11.2 us: shards(): gram_local = jnp.einsum('aijk,bijk->ab', basis, basis, precision=highest)]
    pallas_call x0 -> x5, Pallas kernels: none -> 35.5 us  [the longest x1 11.2 us: clean_powers(): pl.pallas_call(functools.partial(clean_kernel, ny, nx), in_specs=vmem(6),...]
    all_to_all x0 -> x1, blocking collectives: none -> 19.6 us  [shards(): parts = lax.all_to_all(gram, ('gx', 'gy'), 0, 0, tiled=True)]
    sub x4 -> x0, other arithmetic: 16.7 us -> none  [the longest x1 7.45 us: shards(): powered = applied - basis_shift * blocks]
    ppermute x16 -> x4, waiting for transfers between devices: 14.8 us -> 0.33 us  [the longest x1 0.32 us: shards(): xe = lax.ppermute(xe, 'gx', even_pairs(gx))]
    another operation x10 -> x0, other arithmetic: 8.03 us -> none  [the longest x3 2.15 us: finish(): factor = jnp.linalg.cholesky(reduced)]
  transfers between devices with their start and end apart: 16 -> 4, of which waited for: 6 -> 1; matrix products, arithmetic and copies ran while one was open for 7% -> 0% of each run, Pallas kernels for 0% -> 18%
where the time goes in v3:
time: 61.8 us; the launch traced here: 61.5 us
  Pallas kernels  35.5 us (57%)
  blocking collectives  19.6 us (32%)
  starting transfers between devices  4.78 us (8%)
  between operations  0.7 us (1%)
  local copies, waits for them, and re-layouts  0.69 us (1%)
    all_to_all x1, blocking collectives, shards(): parts = lax.all_to_all(gram, ('gx', 'gy'), 0, 0, tiled=True)  19.6 us
    pallas_call x1, Pallas kernels, clean_powers(): pl.pallas_call(functools.partial(clean_kernel, ny, nx), in_specs=vmem(6),...  11.2 us
    pallas_call x1, Pallas kernels, update(): pl.pallas_call(functools.partial(update_kernel, ny, nx), in_specs=vmem(8)...  10.3 us
    pallas_call x1, Pallas kernels, edge_powers(): pl.pallas_call(functools.partial(edge_kernel, ny, nx, devices), in_specs=...  7.24 us
    pallas_call x1, Pallas kernels, load(): pl.pallas_call(load_kernel, in_specs=hbm(6) + vmem(1), out_specs=vmem(9),...  4.75 us
    ppermute x1, starting transfers between devices, shards(): ye = lax.ppermute(ye, 'gy', even_pairs(gy))  2.9 us
    pallas_call x1, Pallas kernels, partial_residual(): pl.pallas_call(functools.partial(partial_kernel, gx, gy), in_specs=vmem(9...  1.97 us
  transfers between devices with their start and end apart: 4, of which 1 were waited for; matrix products, arithmetic and copies ran while one was open for 0% of the time, Pallas kernels for 18%

profile of v3, /device:TPU:0, one launch (start us, length us, event | category | flops | bytes accessed | tf_op | source)
XLA Modules:
  0.0 61.5 jit_solution(13935555795187759334)
XLA Ops:
  0.6 0.0 copy-start
  0.6 0.7 %copy-done = s32[64,16]{0,1:T(8,128)S(1)} copy-done((s32[64,16]{0,1:T(8,128)S(1)}, s32[64,16]{0,1:T(8,128)}, u32[]{:S(2)}) %copy-start) | copy-done | bytes 4120
  1.3 4.8 %load.1 = (f32[16,64,128]{2,1,0:T(8,128)S(1)}, f32[16,64,128]{2,1,0:T(8,128)S(1)}, f32[16,64,128]{2,1,0:T(8,128)S(1)}, f32[16,64,128]{2,1,0:T(8,128)S(1)}, f32[1...) custom-call(f32[8,64,16,128]{3,2,1,0:T(8,128)} %it_hbm.3, ...), custom_call_target="tpu_custom_call" | custom-call | tf_op jit(solution)/shard_map/load/pallas_call | solution.py:146
  6.1 0.6 collective-permute-start
  6.6 0.7 %collective-permute-start.1 = (f32[2,16,8,128]{3,2,1,0:T(8,128)S(1)}, f32[2,16,8,128]{3,2,1,0:T(8,128)S(1)}, u32[]{:S(2)}, u32[]{:S(2)}) collective-permute-start(f32[2,16,8,128]{3,2,1,0:T(8,128)S(1)} %get-tuple-element.35), channel_id=1, source_target_pairs={{8,16},{16,8},{9,17},{17,9},{10,18},{18,10},{11,19},{19,11},{12,20... | collective-permute-start | bytes 393224 | tf_op jit(solution)/shard_map/ppermute | solution.py:748
  7.3 0.3 collective-permute-done.xe_ref
  7.6 0.0 collective-permute-done.1.xo_ref
  7.6 2.0 %partial_residual.1 = (f32[1280,128]{1,0:T(8,128)S(1)}, f32[1280,128]{1,0:T(8,128)S(1)}, f32[1280,128]{1,0:T(8,128)S(1)}, f32[1280,128]{1,0:T(8,128)S(1)}, f32[1...) custom-call(f32[16,64,128]{2,1,0:T(8,128)S(1)} %get-tuple-element.27, ...), custom_call_target="tpu_custom_call" | custom-call | tf_op jit(solution)/shard_map/partial_residual/pallas_call | solution.py:277
  9.6 2.9 %collective-permute-start.2 = (f32[488,128]{1,0:T(8,128)S(1)}, f32[488,128]{1,0:T(8,128)S(1)}, u32[]{:S(2)}, u32[]{:S(2)}) collective-permute-start(f32[488,128]{1,0:T(8,128)S(1)} %get-tuple-element.45), channel_id=1, source_target_pairs={{0,1},{1,0},{2,3},{3,2},{4,5},{5,4},{6,7},{7,6},{8,9},{9,8},{10,11... | collective-permute-start | bytes 749576 | tf_op jit(solution)/shard_map/ppermute | solution.py:750
  12.5 0.7 %collective-permute-start.3 = (f32[488,128]{1,0:T(8,128)S(1)}, f32[488,128]{1,0:T(8,128)S(1)}, u32[]{:S(2)}, u32[]{:S(2)}) collective-permute-start(f32[488,128]{1,0:T(8,128)S(1)} %get-tuple-element.46), channel_id=1, source_target_pairs={{1,2},{2,1},{3,4},{4,3},{5,6},{6,5},{9,10},{10,9},{11,12},{12,11},... | collective-permute-start | bytes 749576 | tf_op jit(solution)/shard_map/ppermute | solution.py:751
  13.2 11.2 %clean_powers.1 = (f32[8,960,128]{2,1,0:T(8,128)S(1)}, f32[8,640,128]{2,1,0:T(8,128)S(1)}, f32[116,8,128]{2,1,0:T(8,128)S(1)}) custom-call(f32[1280,128]{1,0:T(8,128)S(1)} %get-tuple-element.36.t_ref, f32[1280,128]{1,0:T(8,128)S(1)} %get-tuple-element.38.fx_ref, f32[1280,128]{1,0:T(8,128)S(1)} %get-tuple-element.39.fy_ref, ...), custom_call_target="tpu_custom_call" | custom-call | flops 60000000 | bytes 12000000 | tf_op jit(solution)/shard_map/clean_powers/pallas_call | solution.py:402
  24.4 0.0 collective-permute-done.2.ye_ref
  24.4 0.0 collective-permute-done.3.yo_ref
  24.4 7.2 %edge_powers.1 = (f32[8,480,128]{2,1,0:T(8,128)S(1)}, f32[8,384,128]{2,1,0:T(8,128)S(1)}, f32[320,128]{1,0:T(8,128)S(1)}, f32[32,2,128]{2,1,0:T(2,128)S(1)}) custom-call(f32[1280,128]{1,0:T(8,128)S(1)} %get-tuple-element.36.t_ref, f32[1280,128]{1,0:T(8,128)S(1)} %get-tuple-element.37.s_ref, f32[1280,128]{1,0:T(8,128)S(1)} %get-tuple-element.38.fx_ref, ...), custom_call_target="tpu_custom_call" | custom-call | tf_op jit(solution)/shard_map/edge_powers/pallas_call | solution.py:581
  31.6 19.6 %all_to_all.5.parts_ref = f32[32,2,128]{2,1,0:T(2,128)S(1)} all-to-all(f32[32,2,128]{2,1,0:T(2,128)S(1)} %get-tuple-element.47), channel_id=1, replica_groups=mesh['gx'=4,'gy'=8] {'gx','gy'}, dimensions={0} | all-to-all | bytes 65536 | tf_op jit(solution)/shard_map/all_to_all | solution.py:754
  51.2 10.3 %update.1 = (f32[8,64,16,128]{3,2,1,0:T(8,128)}, f32[64,16,128]{2,1,0:T(8,128)}) custom-call(f32[32,2,128]{2,1,0:T(2,128)S(1)} %all_to_all.5.parts_ref, f32[8,960,128]{2,1,0:T(8,128)S(1)} %get-tuple-element.43.pc_ref, f32[8,640,128]{2,1,0:T(8,128)S(1)} %get-tuple-element.48.qc_ref, f32[8,480,128]{2,1,0:T(8,128)S(1)} %get-tuple-element.49.pd_ref, ...), custom_call_target="tpu_custom_call" | custom-call | tf_op jit(solution)/shard_map/update/pallas_call | solution.py:723
Async XLA Ops:
  0.6 0.7 %copy-start = (s32[64,16]{0,1:T(8,128)S(1)}, s32[64,16]{0,1:T(8,128)}, u32[]{:S(2)}) copy-start(s32[64,16]{0,1:T(8,128)} %param.13) | copy-start | bytes 12292
  6.1 1.5 %collective-permute-start = (f32[2,16,8,128]{3,2,1,0:T(8,128)S(1)}, f32[2,16,8,128]{3,2,1,0:T(8,128)S(1)}, u32[]{:S(2)}, u32[]{:S(2)}) collective-permute-start(f32[2,16,8,128]{3,2,1,0:T(8,128)S(1)} %get-tuple-element.34), channel_id=1, source_target_pairs={{0,8},{8,0},{16,24},{24,16},{1,9},{9,1},{17,25},{25,17},{2,10},{10... | collective-permute-start | bytes 393224 | tf_op jit(solution)/shard_map/ppermute | solution.py:747
  6.6 1.0 %collective-permute-start.1 = (f32[2,16,8,128]{3,2,1,0:T(8,128)S(1)}, f32[2,16,8,128]{3,2,1,0:T(8,128)S(1)}, u32[]{:S(2)}, u32[]{:S(2)}) collective-permute-start(f32[2,16,8,128]{3,2,1,0:T(8,128)S(1)} %get-tuple-element.35), channel_id=1, source_target_pairs={{8,16},{16,8},{9,17},{17,9},{10,18},{18,10},{11,19},{19,11},{12,20... | collective-permute-start | bytes 393224 | tf_op jit(solution)/shard_map/ppermute | solution.py:748
  9.6 14.8 %collective-permute-start.2 = (f32[488,128]{1,0:T(8,128)S(1)}, f32[488,128]{1,0:T(8,128)S(1)}, u32[]{:S(2)}, u32[]{:S(2)}) collective-permute-start(f32[488,128]{1,0:T(8,128)S(1)} %get-tuple-element.45), channel_id=1, source_target_pairs={{0,1},{1,0},{2,3},{3,2},{4,5},{5,4},{6,7},{7,6},{8,9},{9,8},{10,11... | collective-permute-start | bytes 749576 | tf_op jit(solution)/shard_map/ppermute | solution.py:750
  12.5 11.9 %collective-permute-start.3 = (f32[488,128]{1,0:T(8,128)S(1)}, f32[488,128]{1,0:T(8,128)S(1)}, u32[]{:S(2)}, u32[]{:S(2)}) collective-permute-start(f32[488,128]{1,0:T(8,128)S(1)} %get-tuple-element.46), channel_id=1, source_target_pairs={{1,2},{2,1},{3,4},{4,3},{5,6},{6,5},{9,10},{10,9},{11,12},{12,11},... | collective-permute-start | bytes 749576 | tf_op jit(solution)/shard_map/ppermute | solution.py:751

commit v4 on v3

v4 whole, which is shorter than its diff:
```python
import functools

import jax
import jax.numpy as jnp
from jax import lax
from jax.experimental import pallas as pl
from jax.experimental.pallas import tpu as pltpu
from jax.sharding import PartitionSpec as P

ENLARGE = 8
SHIFT = 6.5
F32 = jnp.float32
HIGHEST = lax.Precision.HIGHEST
PAIRS = [(j, k) for j in range(ENLARGE) for k in range(j, ENLARGE)]
VMEM_LIMIT = 20 * 1024 * 1024
PAD = 8
SENT = 2


def iota(shape, dim):
    return lax.broadcasted_iota(jnp.int32, shape, dim)


def even_pairs(count):
    return [(i, i ^ 1) for i in range(count) if (i ^ 1) < count]


def odd_pairs(count):
    return [(i, ((i - 1) ^ 1) + 1) for i in range(1, count) if ((i - 1) ^ 1) + 1 < count]


def vmem(count):
    return [pl.BlockSpec(memory_space=pltpu.VMEM)] * count


def hbm(count):
    return [pl.BlockSpec(memory_space=pltpu.HBM)] * count


def pinned(value):
    return pltpu.with_memory_space_constraint(value, pltpu.HBM)


def array(*shape):
    return jax.ShapeDtypeStruct(shape, F32)


def params():
    return pltpu.CompilerParams(vmem_limit_bytes=VMEM_LIMIT)


def aligned(value):
    return value if isinstance(value, int) else pl.multiple_of(value, 8)


def eight(start):
    return pl.ds(aligned(start), 8)


def near(start):
    return pl.ds(start, 8)


def loop(count, body, **kw):
    def wrapped(i, carry):
        body(i)
        return carry

    lax.fori_loop(0, count, wrapped, 0, **kw)


def edges_kernel(
    it_hbm, src_hbm, dg_hbm, fx_hbm, fy_hbm, fz_hbm, label_hbm,
    even_out, odd_out,
    work, fields, labels, sem_it, sem_field, sem_label,
):
    _, nx, ny, nz = it_hbm.shape
    sources = (src_hbm, dg_hbm, fx_hbm, fy_hbm, fz_hbm)
    lines = [(x, x) for x in range(3)] + [(nx - 3 + x, 13 + x) for x in range(3)]
    copies = [pltpu.make_async_copy(label_hbm, labels, sem_label)]
    for n, (x, row) in enumerate(lines):
        copies.append(pltpu.make_async_copy(it_hbm.at[:, x], work.at[:, :, row], sem_it.at[n]))
        for f, ref in enumerate(sources):
            copies.append(pltpu.make_async_copy(ref.at[x], fields.at[f, :, row], sem_field.at[f, n]))
    for copy in copies:
        copy.start()
    copies[0].wait()
    spread_rows = iota((16, nx), 0)
    spot = jnp.where(spread_rows < 8, spread_rows, spread_rows + nx - 16) == iota((16, nx), 1)
    ones = jnp.ones((nx, nz), jnp.bfloat16)
    marks = labels[...].astype(F32)
    for copy in copies[1:]:
        copy.wait()
    even = lax.rem(lax.axis_index("gx"), 2) == 0
    sub = iota((8, nz), 0)
    roll = lambda v, n: pltpu.roll(v, n, 0)
    for y in range(ny):
        row = jnp.where(spot, marks[y : y + 1], 0.0).astype(jnp.bfloat16)
        lb = jnp.dot(row, ones, preferred_element_type=F32)
        total = work[0, y]
        for j in range(1, ENLARGE):
            total = total + work[j, y]
        src, dg, fx, fy, fz = [fields[f, y] for f in range(5)]

        def first(at, is_low):
            if is_low:
                return jnp.where(sub < 3, total[at], jnp.where(sub >= 6, roll(lb[at], 6), roll(fx[at], 3)))
            return jnp.where(sub >= 5, total[at], jnp.where(sub < 2, roll(lb[at], 2), roll(fx[at], 5)))

        def second(at, start):
            values = src[at]
            for n, field in enumerate((dg, fy, fz)):
                begin = (start + 2 * n + 2) % 8
                inside = jnp.logical_or(sub == begin, sub == begin + 1)
                values = jnp.where(inside, roll(field[at], 2 * n + 2), values)
            return values

        lo, hi = slice(0, 8), slice(8, 16)
        for part, high, low in ((0, first(hi, False), first(lo, True)), (1, second(hi, 6), second(lo, 0))):
            even_out[part, y] = jnp.where(even, high, low)
            odd_out[part, y] = jnp.where(even, low, high)


def x_edges(arrays):
    _, nx, ny, nz = arrays[0].shape
    edge = array(2, ny, 8, nz)
    return pl.pallas_call(
        edges_kernel,
        in_specs=hbm(7),
        out_specs=vmem(2),
        out_shape=[edge] * 2,
        scratch_shapes=[
            pltpu.VMEM((ENLARGE, ny, 16, nz), F32),
            pltpu.VMEM((5, ny, 16, nz), F32),
            pltpu.VMEM((ny, nx), jnp.int32),
            pltpu.SemaphoreType.DMA((6,)),
            pltpu.SemaphoreType.DMA((5, 6)),
            pltpu.SemaphoreType.DMA,
        ],
        compiler_params=params(),
        name="x_edges",
    )(*arrays)


def load_kernel(
    it_hbm, src_hbm, dg_hbm, fx_hbm, fy_hbm, fz_hbm, label_hbm,
    s_out, src_out, dg_out, fx_out, fy_out, fz_out, lb_out, work,
    label_ref, sem_it, sem_field, sem_label,
):
    ny, nx, nz = s_out.shape
    pairs = list(zip((src_hbm, dg_hbm, fx_hbm, fy_hbm, fz_hbm), (src_out, dg_out, fx_out, fy_out, fz_out)))
    label_copy = pltpu.make_async_copy(label_hbm, label_ref, sem_label)

    def copy_it(y):
        return pltpu.make_async_copy(it_hbm.at[:, :, y], work.at[:, y], sem_it.at[y])

    def copy_field(f, y):
        return pltpu.make_async_copy(pairs[f][0].at[:, y], pairs[f][1].at[y], sem_field.at[f, y])

    def start(y):
        copy_it(y).start()
        for f in range(len(pairs)):
            copy_field(f, y).start()

    label_copy.start()
    loop(ny, start)
    label_copy.wait()

    spot = iota((nx, nx), 0) == iota((nx, nx), 1)
    ones = jnp.ones((nx, nz), jnp.bfloat16)
    labels = label_ref[...].astype(F32)
    for y in range(ny):
        row = jnp.where(spot, labels[y : y + 1], 0.0).astype(jnp.bfloat16)
        lb_out[y] = jnp.dot(row, ones, preferred_element_type=F32)

    def add(y):
        copy_it(y).wait()
        for r in range(0, nx, 8):
            total = work[0, y, r : r + 8]
            for j in range(1, ENLARGE):
                total = total + work[j, y, r : r + 8]
            s_out[y, r : r + 8] = total

    loop(ny, add)

    def finish(y):
        for f in range(len(pairs)):
            copy_field(f, y).wait()

    loop(ny, finish)


def load(arrays):
    _, nx, ny, nz = arrays[0].shape
    field = array(ny, nx, nz)
    return pl.pallas_call(
        load_kernel,
        in_specs=hbm(7),
        out_specs=vmem(8),
        out_shape=[field] * 7 + [array(ENLARGE, ny, nx, nz)],
        scratch_shapes=[
            pltpu.VMEM((ny, nx), jnp.int32),
            pltpu.SemaphoreType.DMA((ny,)),
            pltpu.SemaphoreType.DMA((5, ny)),
            pltpu.SemaphoreType.DMA,
        ],
        compiler_params=params(),
        cost_estimate=pl.CostEstimate(flops=2_000_000, bytes_accessed=16_000_000, transcendentals=0),
        name="load",
    )(*arrays)


def blocks_of(nx):
    wide = nx + PAD
    sizes = (wide, wide, wide, wide, nx, nx, nx, 8)
    starts = [sum(sizes[:i]) for i in range(len(sizes) + 1)]
    return wide, starts


def pack_y_edge(ny, nx, dest, is_high, t, s, fy, fx, dg, fz, lb):
    pitch = nx + 2 * PAD
    nz = t.shape[-1]
    wide, starts = blocks_of(nx)
    first = jnp.where(is_high, ny - 1, 0) * pitch
    second = jnp.where(is_high, ny - 2, 1) * pitch
    between = jnp.where(is_high, ny - 2, 0) * pitch

    def line(ref, base):
        return ref[pl.ds(base + (PAD - SENT), wide)]

    def inner(ref, base):
        return ref[pl.ds(pl.multiple_of(base + PAD, 8), nx)]

    parts = (
        line(t, first),
        line(s, first),
        line(fy, first),
        line(fx, first),
        inner(fy, between) * inner(t, second),
        inner(dg, first),
        inner(fz, first),
    )
    for b, values in enumerate(parts):
        dest[starts[b] : starts[b + 1]] = values
    spot = iota((wide, nz), 0) == iota((wide, nz), 1)
    one = jnp.sum(jnp.where(spot, line(lb, first), 0.0), axis=0, keepdims=True)
    two = jnp.sum(jnp.where(spot, line(lb, second), 0.0), axis=0, keepdims=True)
    which = iota((8, nz), 0)
    dest[starts[7] : starts[8]] = jnp.where(which == 0, one, jnp.where(which == 1, two, 0.0))


def partial_kernel(
    gx, gy,
    s_in, src_in, dg_in, fx_in, fy_in, fz_in, lb_in, xe_ref, xo_ref,
    t_out, s_out, fx_out, fy_out, dg_out, fz_out, lb_out, ye_ref,
    src_ext,
):
    ny, nx, nz = s_in.shape
    pitch = nx + 2 * PAD
    lane = iota((8, nz), 1)
    even_x = lax.rem(lax.axis_index("gx"), 2) == 0
    last_x = lax.axis_index("gx") == gx - 1
    last_y = lax.axis_index("gy") == gy - 1
    last_row = jnp.logical_and(iota((8, nz), 0) == 7, last_x)

    def fill(y):
        top = jnp.logical_and(last_y, y == ny - 1)
        fy_of = lambda v: jnp.where(top, 0.0, v)
        fz_of = lambda v: jnp.where(lane == nz - 1, 0.0, v)
        base = y * pitch
        roll = lambda v, n: pltpu.roll(v, n, 0)
        for at, is_low in ((0, True), (PAD + nx, False)):
            one, two = [
                jnp.where(even_x == is_low, xo_ref[part, y], xe_ref[part, y]) for part in range(2)
            ]
            here = eight(base + at)
            s_out[here] = one
            fx_out[here] = roll(one, 3 if is_low else 5)
            lb_out[here] = roll(one, 6 if is_low else 2)
            src_ext[here] = two
            dg_out[here] = roll(two, 6)
            fy_out[here] = fy_of(roll(two, 4))
            fz_out[here] = fz_of(roll(two, 2))
        for r in range(0, nx, 8):
            here = eight(base + PAD + r)
            span = slice(r, r + 8)
            s_out[here] = s_in[y, span]
            face = fx_in[y, span]
            fx_out[here] = jnp.where(last_row, 0.0, face) if r == nx - 8 else face
            lb_out[here] = lb_in[y, span]
            src_ext[here] = src_in[y, span]
            dg_out[here] = dg_in[y, span]
            fy_out[here] = fy_of(fy_in[y, span])
            fz_out[here] = fz_of(fz_in[y, span])

    loop(ny, fill)

    def layer(y, down=True, up=True):
        base = y * pitch
        for r in range(0, pitch, 8):
            at = base + r
            here = eight(at)
            s, fx, fz = s_out[here], fx_out[here], fz_out[here]
            if r == 0:
                sm, fxm = pltpu.roll(s, 1, 0), pltpu.roll(fx, 1, 0)
            else:
                sm, fxm = s_out[near(at - 1)], fx_out[near(at - 1)]
            sp = pltpu.roll(s, 7, 0) if r == pitch - 8 else s_out[near(at + 1)]
            total = dg_out[here] * s - fx * sp - fxm * sm
            if up:
                total = total - fy_out[here] * s_out[eight(at + pitch)]
            if down:
                total = total - fy_out[eight(at - pitch)] * s_out[eight(at - pitch)]
            total = total - fz * pltpu.roll(s, nz - 1, 1) - pltpu.roll(fz * s, 1, 1)
            t_out[here] = src_ext[here] - total

    layer(0, down=False)
    layer(ny - 1, up=False)
    loop(ny - 2, lambda i: layer(i + 1))

    even_y = lax.rem(lax.axis_index("gy"), 2) == 0
    pack_y_edge(ny, nx, ye_ref, even_y, t_out, s_out, fy_out, fx_out, dg_out, fz_out, lb_out)


def partial_residual(fields, xe, xo, gx, gy):
    ny, nx, nz = fields[0].shape
    rows = ny * (nx + 2 * PAD)
    ext = array(rows, nz)
    pack = array(blocks_of(nx)[1][-1], nz)
    return pl.pallas_call(
        functools.partial(partial_kernel, gx, gy),
        in_specs=vmem(9),
        out_specs=vmem(8),
        out_shape=[ext] * 7 + [pack],
        scratch_shapes=[pltpu.VMEM((rows, nz), F32)],
        compiler_params=params(),
        name="partial_residual",
    )(*fields, xe, xo)


def spread(parts):
    fields = []
    for j in range(ENLARGE):
        total = None
        for values, label in parts:
            term = jnp.where(label == float(j), values, 0.0)
            total = term if total is None else total + term
        fields.append(total)
    return fields


def along_z(fz, values):
    nz = values.shape[-1]
    return fz * pltpu.roll(values, nz - 1, 1) + pltpu.roll(fz * values, 1, 1)


def edge_near(ref, at, shift, last):
    if last == shift:
        return pltpu.roll(ref[eight(at)], 1 if shift < 0 else 7, 0)
    return ref[near(at + shift)]


def zeros_like_pairs(nz, count):
    return tuple(jnp.zeros((8, nz), F32) for _ in range(count))


def dot_own(sums, r, label, p):
    b = [jnp.where(label == float(j), r, 0.0) for j in range(ENLARGE)]
    n = len(PAIRS)
    own = tuple(t + v * v for t, v in zip(sums[n:], b))
    return tuple(t + b[j] * p[k] for t, (j, k) in zip(sums, PAIRS)) + own


def dot_pairs(sums, p, q):
    return tuple(t + p[j] * q[k] for t, (j, k) in zip(sums, PAIRS))


def clean_first_kernel(
    ny, nx,
    t_ref, s_ref, fx_ref, fy_ref, dg_ref, fz_ref, lb_ref,
    p_out, yo_ref,
):
    pitch = nx + 2 * PAD

    def first(i):
        layer = (i + 2) * pitch
        for r in range(0, pitch, 8):
            at = layer + r
            last = -1 if r == 0 else (1 if r == pitch - 8 else 0)
            here = eight(at)
            value = t_ref[here]
            below, above = eight(at - pitch), eight(at + pitch)
            parts = [
                ((dg_ref[here] - SHIFT) * value - along_z(fz_ref[here], value), lb_ref[here]),
                (-fx_ref[here] * edge_near(t_ref, at, 1, last), edge_near(lb_ref, at, 1, last)),
                (-edge_near(fx_ref, at, -1, last) * edge_near(t_ref, at, -1, last), edge_near(lb_ref, at, -1, last)),
                (-fy_ref[here] * t_ref[above], lb_ref[above]),
                (-fy_ref[below] * t_ref[below], lb_ref[below]),
            ]
            for j, values in enumerate(spread(parts)):
                p_out[j, eight(i * pitch + r)] = values

    loop(ny - 4, first)
    odd_y = lax.rem(lax.axis_index("gy"), 2) == 1
    pack_y_edge(ny, nx, yo_ref, odd_y, t_ref, s_ref, fy_ref, fx_ref, dg_ref, fz_ref, lb_ref)


def clean_second_kernel(
    ny, nx,
    t_ref, fx_ref, fy_ref, dg_ref, fz_ref, lb_ref, p_out,
    q_out, acc_out,
):
    nz = t_ref.shape[-1]
    pitch = nx + 2 * PAD
    chunks = nx // 8

    def second(i):
        for c in range(chunks):
            at = (i + 3) * pitch + PAD + c * 8
            own = (i + 1) * pitch + PAD + c * 8
            here = eight(at)
            dg, fz, fxp, fxm = dg_ref[here], fz_ref[here], fx_ref[here], fx_ref[near(at - 1)]
            fyp, fym = fy_ref[here], fy_ref[eight(at - pitch)]
            for j in range(ENLARGE):
                p = p_out[j, eight(own)]
                q = dg * p - fxp * p_out[j, near(own + 1)] - fxm * p_out[j, near(own - 1)]
                q = q - fyp * p_out[j, eight(own + pitch)] - fym * p_out[j, eight(own - pitch)]
                q_out[j, eight(i * nx + c * 8)] = q - along_z(fz, p)

    loop(ny - 6, second)

    def fields_at(ref, at):
        return [ref[j, eight(at)] for j in range(ENLARGE)]

    def own_dots(i, sums):
        for c in range(chunks):
            row = i * pitch + PAD + c * 8
            shifted = eight(row + 2 * pitch)
            sums = dot_own(sums, t_ref[shifted], lb_ref[shifted], fields_at(p_out, row))
        return sums

    def p_dots(i, sums):
        for c in range(chunks):
            p = fields_at(p_out, i * pitch + PAD + c * 8)
            sums = dot_pairs(sums, p, p)
        return sums

    def q_dots(i, sums):
        for c in range(chunks):
            p = fields_at(p_out, (i + 1) * pitch + PAD + c * 8)
            sums = dot_pairs(sums, p, fields_at(q_out, i * nx + c * 8))
        return sums

    slot = 0
    for dots, layers, count in (
        (own_dots, ny - 4, len(PAIRS) + ENLARGE), (p_dots, ny - 4, len(PAIRS)), (q_dots, ny - 6, len(PAIRS)),
    ):
        sums = lax.fori_loop(0, layers, dots, zeros_like_pairs(nz, count))
        for values in sums:
            acc_out[slot] = values
            slot += 1


def clean_first(ext, ny, nx):
    nz = ext[0].shape[-1]
    return pl.pallas_call(
        functools.partial(clean_first_kernel, ny, nx),
        in_specs=vmem(7),
        out_specs=vmem(2),
        out_shape=[array(ENLARGE, (ny - 4) * (nx + 2 * PAD), nz), array(blocks_of(nx)[1][-1], nz)],
        compiler_params=params(),
        cost_estimate=pl.CostEstimate(flops=20_000_000, bytes_accessed=8_000_000, transcendentals=0),
        name="clean_first",
    )(*ext)


def clean_second(ext, pc, ny, nx):
    t, _, fx, fy, dg, fz, lb = ext
    nz = t.shape[-1]
    return pl.pallas_call(
        functools.partial(clean_second_kernel, ny, nx),
        in_specs=vmem(7),
        out_specs=vmem(2),
        out_shape=[array(ENLARGE, (ny - 6) * nx, nz), array(3 * len(PAIRS) + ENLARGE, 8, nz)],
        compiler_params=params(),
        cost_estimate=pl.CostEstimate(flops=40_000_000, bytes_accessed=12_000_000, transcendentals=0),
        name="clean_second",
    )(t, fx, fy, dg, fz, lb, pc)


def edge_slot(y, ny):
    return y + 2 if y < 4 else y - (ny - 4) + 6


def edge_kernel(
    ny, nx, devices,
    t_ref, s_ref, fx_ref, fy_ref, dg_ref, fz_ref, lb_ref, pc_ref, acc_ref, ye_ref, yo_ref,
    p_out, q_out, r_out, lb_out, gram_out,
    packs, fx, fy, dg, fz, rows_acc,
):
    nz = t_ref.shape[-1]
    pitch = nx + 2 * PAD
    chunks = nx // 8
    wide, starts = blocks_of(nx)
    left = PAD - SENT
    odd = lax.rem(lax.axis_index("gy"), 2)
    packs[1 - odd] = ye_ref[...]
    packs[odd] = yo_ref[...]

    def packed(side, b):
        return packs[side, starts[b] : starts[b + 1]]

    for side in range(2):
        for i in range(4):
            source = ((side * (ny - 4)) + i) * pitch
            dest = (side * 4 + i + 2) * pitch
            for ref, out in ((t_ref, r_out), (lb_ref, lb_out), (fx_ref, fx), (fy_ref, fy), (dg_ref, dg), (fz_ref, fz)):
                out[dest : dest + pitch] = ref[source : source + pitch]
        for i in range(2):
            source = (side * (ny - 6) + i) * pitch
            dest = (side * 2 + i + 4) * pitch
            p_out[:, dest : dest + pitch] = pc_ref[:, source : source + pitch]
    for side in range(2):
        inner, ghost, far = (0, -1, -2) if side == 0 else (ny - 1, ny, ny + 1)
        at = lambda y, start=left, size=wide: pl.ds(edge_slot(y, ny) * pitch + start, size)
        base = pl.ds(inner * pitch + left, wide)
        face = packed(side, 2) if side == 0 else fy_ref[base]
        r_out[at(ghost)] = packed(side, 0) + face * s_ref[base]
        r_out[at(inner)] = t_ref[base] + face * packed(side, 1)
        if side == 0:
            fy[at(ghost)] = face
        fy[at(far if side == 0 else ghost)] = jnp.ones((wide, nz), F32)
        r_out[at(far, PAD, nx)] = packed(side, 4)
        fx[at(ghost)] = packed(side, 3)
        dg[at(ghost, PAD, nx)] = packed(side, 5)
        fz[at(ghost, PAD, nx)] = packed(side, 6)
        labels = packed(side, 7)
        spot = iota((wide, nz), 0) == iota((wide, nz), 1)
        for r, y in ((0, ghost), (1, far)):
            column = jnp.sum(jnp.where(spot, labels[r : r + 1], 0.0), axis=1, keepdims=True)
            lb_out[at(y)] = jnp.broadcast_to(column, (wide, nz))

    def first(i):
        base = (i + 1 + jnp.where(i >= 3, 4, 0)) * pitch
        for r in range(0, pitch, 8):
            at = base + r
            here, below, above = eight(at), eight(at - pitch), eight(at + pitch)
            value = r_out[here]
            parts = [
                ((dg[here] - SHIFT) * value - along_z(fz[here], value), lb_out[here]),
                (-fx[here] * r_out[near(at + 1)], lb_out[near(at + 1)]),
                (-fx[near(at - 1)] * r_out[near(at - 1)], lb_out[near(at - 1)]),
                (-fy[here] * r_out[above], lb_out[above]),
                (-fy[below] * r_out[below], lb_out[below]),
            ]
            for j, values in enumerate(spread(parts)):
                p_out[j, here] = values

    loop(6, first)

    def q_slot(i):
        return i + 2 + jnp.where(i >= 3, 2, 0)

    def second(i):
        for c in range(chunks):
            at = q_slot(i) * pitch + PAD + c * 8
            here, below, above = eight(at), eight(at - pitch), eight(at + pitch)
            d, z, fxp, fxm, fyp, fym = dg[here], fz[here], fx[here], fx[near(at - 1)], fy[here], fy[below]
            for j in range(ENLARGE):
                p = p_out[j, here]
                q = d * p - fxp * p_out[j, near(at + 1)] - fxm * p_out[j, near(at - 1)]
                q = q - fyp * p_out[j, above] - fym * p_out[j, below]
                q_out[j, eight(i * nx + c * 8)] = q - along_z(z, p)

    loop(6, second)

    def fields_at(ref, at):
        return [ref[j, eight(at)] for j in range(ENLARGE)]

    def own_dots(i, sums):
        base = (i + 2 + jnp.where(i >= 2, 4, 0)) * pitch + PAD
        for c in range(chunks):
            at = base + c * 8
            sums = dot_own(sums, r_out[eight(at)], lb_out[eight(at)], fields_at(p_out, at))
        return sums

    def p_dots(i, sums):
        base = (i + 2 + jnp.where(i >= 2, 4, 0)) * pitch + PAD
        for c in range(chunks):
            p = fields_at(p_out, base + c * 8)
            sums = dot_pairs(sums, p, p)
        return sums

    def q_dots(i, sums):
        base = q_slot(i) * pitch + PAD
        for c in range(chunks):
            sums = dot_pairs(sums, fields_at(p_out, base + c * 8), fields_at(q_out, i * nx + c * 8))
        return sums

    rows_acc[...] = jnp.zeros_like(rows_acc)
    span = ENLARGE * ENLARGE

    def put(slot, values):
        rows_acc[slot : slot + 1] = jnp.sum(values, axis=0, keepdims=True)

    pairs = len(PAIRS)
    begin = 0
    for which, dots, layers, count in (
        (0, own_dots, 4, pairs + ENLARGE), (1, p_dots, 4, pairs), (2, q_dots, 6, pairs),
    ):
        sums = tuple(acc_ref[begin + i] for i in range(count))
        begin += count
        sums = lax.fori_loop(0, layers, dots, sums)
        for (j, k), values in zip(PAIRS, sums):
            put(which * span + j * ENLARGE + k, values)
            if j != k:
                put(which * span + k * ENLARGE + j, values)
        for j, values in enumerate(sums[pairs:]):
            put(3 * span + j * ENLARGE + j, values)
    ones = jnp.ones((8, nz), F32)
    flat = lax.dot_general(
        ones, rows_acc[...], (((1,), (1,)), ((), ())), precision=HIGHEST, preferred_element_type=F32
    )
    half = 2 * span
    pair = jnp.where(iota((2, half), 0) == 0, flat[0:2, 0:half], flat[0:2, half : 2 * half])
    for d in range(devices):
        gram_out[d] = pair


def edge_powers(ext, pc, acc, ye, yo, ny, nx, devices):
    nz = pc.shape[-1]
    rows = 12 * (nx + 2 * PAD)
    half = 2 * ENLARGE * ENLARGE
    return pl.pallas_call(
        functools.partial(edge_kernel, ny, nx, devices),
        in_specs=vmem(11),
        out_specs=vmem(5),
        out_shape=[
            array(ENLARGE, rows, nz), array(ENLARGE, 6 * nx, nz), array(rows, nz), array(rows, nz),
            array(devices, 2, half),
        ],
        scratch_shapes=[
            pltpu.VMEM((2,) + ye.shape, F32),
            pltpu.VMEM((rows, nz), F32),
            pltpu.VMEM((rows, nz), F32),
            pltpu.VMEM((rows, nz), F32),
            pltpu.VMEM((rows, nz), F32),
            pltpu.VMEM((2 * half, nz), F32),
        ],
        compiler_params=params(),
        name="edge_powers",
    )(*ext, pc, acc, ye, yo)


def solve_columns(parts):
    nz = parts.shape[-1]
    span = ENLARGE * ENLARGE
    v = jnp.sum(parts, axis=0)
    lhs = jnp.concatenate([jnp.broadcast_to(v[0:1], (8, nz)), jnp.broadcast_to(v[1:2], (8, nz))], axis=1)
    source = iota((8, 2 * nz), 1)
    lhs = jnp.where(iota((8, 2 * nz), 0) == lax.rem(source, span) // ENLARGE, lhs, 0.0)
    k = iota((2 * nz, nz), 0)
    n = iota((2 * nz, nz), 1)
    which = k // span
    column = lax.rem(k, ENLARGE)

    def place(block, offset, scale):
        return jnp.where(jnp.logical_and(which == block, n == column + offset), scale, 0.0)

    upper = place(0, 0, 1.0) + place(3, 0, SHIFT) + place(1, 8, 1.0) + place(0, 8, SHIFT) + place(3, 16, 1.0)
    lower = place(1, 0, 1.0) + place(0, 0, SHIFT) + place(2, 8, 1.0) + place(0, 16, 1.0)
    dot = functools.partial(jnp.dot, precision=HIGHEST, preferred_element_type=F32)
    m = jnp.concatenate([dot(lhs, upper), dot(lhs, lower)], axis=0)
    row = iota(m.shape, 0)
    for i in range(2 * ENLARGE):
        pivot = m[i : i + 1] / m[i : i + 1, i : i + 1]
        m = jnp.where(row == i, pivot, m - m[:, i : i + 1] * pivot)
    return m


def update_kernel(
    parts_ref, pc_ref, qc_ref, pd_ref, qd_ref, t_ref, rd_ref, lb_ref, it_ref,
    it_out, r_out,
    table, weights, onehot, own, work, r_work, sem_out, sem_r,
):
    _, ny, nx, nz = it_ref.shape
    pitch = nx + 2 * PAD
    two = 2 * ENLARGE
    square = ENLARGE * ENLARGE
    chunks = nx // 8

    def copy_out(half, c):
        span, rows = pl.ds(half * 4, 4), pl.ds(pl.multiple_of(c * 8 * ny, 8 * ny), 8 * ny)
        return pltpu.make_async_copy(work.at[span, rows], it_out.at[span, rows], sem_out.at[half, c])

    def copy_r(c):
        rows = pl.ds(pl.multiple_of(c * 8 * ny, 8 * ny), 8 * ny)
        return pltpu.make_async_copy(r_work.at[rows], r_out.at[rows], sem_r.at[c])

    def mark(y):
        lane = iota((nx, nz), 1)
        labels = lb_ref[pl.ds(pl.multiple_of(y * pitch + PAD, 8), nx)]
        chosen = jnp.logical_and(lane < 3 * ENLARGE, lax.rem(lane, ENLARGE).astype(F32) == labels)
        onehot[pl.ds(pl.multiple_of(y * nx, nx), nx)] = jnp.where(chosen, 1.0, 0.0).astype(jnp.bfloat16)

    loop(ny, mark)

    m = solve_columns(parts_ref[...])
    columns = [jnp.broadcast_to(m[:, two + j : two + j + 1], (two, nz)) for j in range(ENLARGE)]
    carried = columns[0]
    for column in columns[1:]:
        carried = carried + column
    weights[...] = jnp.zeros_like(weights)
    for j, column in enumerate(columns + [carried]):
        for k in range(two):
            if j < ENLARGE and k < ENLARGE:
                continue
            slot = j * ENLARGE + k - ENLARGE if j < ENLARGE else square + k
            table[slot] = jnp.broadcast_to(column[k : k + 1], (8, nz))
        mine = column[0:ENLARGE]
        high = mine.astype(jnp.bfloat16).astype(F32)
        mid = (mine - high).astype(jnp.bfloat16).astype(F32)
        at = slice(j * nz, (j + 1) * nz)
        weights[0:8, at] = high
        weights[8:16, at] = mid
        weights[16:24, at] = mine - high - mid
    spread_weights = weights[...].astype(jnp.bfloat16)

    def coefficients(n):
        here = pl.ds(pl.multiple_of(n * 128, 128), 128)
        own[here] = jnp.dot(onehot[here], spread_weights, preferred_element_type=F32)

    loop(ny * nx // 128, coefficients, unroll=2)

    def spots(c, visit):
        def clean(i):
            x = PAD + c * 8
            visit(i + 3, pc_ref, (i + 1) * pitch + x, qc_ref, i * nx + c * 8, t_ref, (i + 3) * pitch + x)

        loop(ny - 6, clean, unroll=2)

        def edge(i):
            at = (i + 2 + jnp.where(i >= 3, 2, 0)) * pitch + PAD + c * 8
            y = i + jnp.where(i >= 3, ny - 6, 0)
            visit(y, pd_ref, at, qd_ref, i * nx + c * 8, rd_ref, at)

        loop(6, edge, unroll=2)

    def place(c, y):
        return pl.ds(c * 8 * ny + y, 8, stride=ny)

    def updates(half):
        js = range(half * 4, half * 4 + 4)
        scales = [[table[j * ENLARGE + k] for k in range(ENLARGE)] for j in js]

        def block(c):
            def visit(y, p_ref, p_at, q_ref, q_at, r_ref, r_at):
                r = r_ref[eight(r_at)]
                at = eight(y * nx + c * 8)
                totals = [it_ref[j, y, eight(c * 8)] + own[at, j * nz : (j + 1) * nz] * r for j in js]
                for k in range(ENLARGE):
                    p = p_ref[k, eight(p_at)]
                    totals = [t + scale[k] * p for t, scale in zip(totals, scales)]
                for j, t in zip(js, totals):
                    work[j, place(c, y), :] = t

            spots(c, visit)
            copy_out(half, c).start()

        loop(chunks, block)

    def residuals():
        scales = [table[square + k] for k in range(two)]

        def block(c):
            def visit(y, p_ref, p_at, q_ref, q_at, r_ref, r_at):
                r = r_ref[eight(r_at)]
                total = r - (SHIFT * own[eight(y * nx + c * 8), ENLARGE * nz : (ENLARGE + 1) * nz]) * r
                for k in range(ENLARGE):
                    total = total - scales[k] * p_ref[k, eight(p_at)]
                    total = total - scales[ENLARGE + k] * q_ref[k, eight(q_at)]
                r_work[place(c, y), :] = total

            spots(c, visit)
            copy_r(c).start()

        loop(chunks, block)

    updates(0)
    updates(1)
    residuals()
    for half in range(2):
        loop(chunks, lambda c, half=half: copy_out(half, c).wait())
    loop(chunks, lambda c: copy_r(c).wait())


def update(parts, pc, qc, pd, qd, t, rd, labels, held):
    _, ny, nx, nz = held.shape
    rows = nx * ny
    return pl.pallas_call(
        update_kernel,
        in_specs=vmem(9),
        out_specs=hbm(2),
        out_shape=[array(ENLARGE, rows, nz), array(rows, nz)],
        scratch_shapes=[
            pltpu.VMEM((ENLARGE * ENLARGE + 2 * ENLARGE, 8, nz), F32),
            pltpu.VMEM((nz, (ENLARGE + 1) * nz), F32),
            pltpu.VMEM((rows, nz), jnp.bfloat16),
            pltpu.VMEM((rows, (ENLARGE + 1) * nz), F32),
            pltpu.VMEM((ENLARGE, rows, nz), F32),
            pltpu.VMEM((rows, nz), F32),
            pltpu.SemaphoreType.DMA((2, nx // 8)),
            pltpu.SemaphoreType.DMA((nx // 8,)),
        ],
        compiler_params=params(),
        name="update",
    )(parts, pc, qc, pd, qd, t, rd, labels, held)


def shards(gx, gy, source, diagonal, face_x, face_y, face_z, iterates, labels):
    _, nx, ny, nz = iterates.shape
    arrays = [pinned(a) for a in (iterates, source, diagonal, face_x, face_y, face_z, labels.T)]
    xe, xo = x_edges(arrays)
    xo = lax.ppermute(xo, "gx", odd_pairs(gx))
    xe = lax.ppermute(xe, "gx", even_pairs(gx))
    *fields, held = load(arrays)
    *ext, ye = partial_residual(fields, xe, xo, gx, gy)
    ye = lax.ppermute(ye, "gy", even_pairs(gy))
    pc, yo = clean_first(ext, ny, nx)
    yo = lax.ppermute(yo, "gy", odd_pairs(gy))
    qc, acc = clean_second(ext, pc, ny, nx)
    pd, qd, rd, _, gram = edge_powers(ext, pc, acc, ye, yo, ny, nx, gx * gy)
    parts = lax.all_to_all(gram, ("gx", "gy"), 0, 0, tiled=True)
    new_iterates, new_residual = update(parts, pc, qc, pd, qd, ext[0], rd, ext[-1], held)
    return new_iterates.reshape(iterates.shape), new_residual.reshape(source.shape)


def solution(mesh):
    placed = (
        P("gx", "gy", None),
        P("gx", "gy", None),
        P("gx", "gy", None),
        P("gx", "gy", None),
        P("gx", "gy", None),
        P(None, "gx", "gy", None),
        P("gx", "gy"),
    )
    return jax.shard_map(
        functools.partial(shards, mesh.shape["gx"], mesh.shape["gy"]),
        mesh=mesh,
        in_specs=placed,
        out_specs=(P(None, "gx", "gy", None), P("gx", "gy", None)),
        check_vma=False,
    )
```

time: 61.8 us -> 53.4 us (0.86)
  Pallas kernels: 35.5 us -> 31.2 us
  blocking collectives: 19.6 us -> 16.7 us
  local copies, waits for them, and re-layouts: 0.69 us -> 0 us
    all_to_all x1, blocking collectives: 19.6 us -> 16.7 us  [shards(): parts = lax.all_to_all(gram, ('gx', 'gy'), 0, 0, tiled=True)]
    pallas_call x1, Pallas kernels: 7.24 us -> 4.91 us  [edge_powers(): pl.pallas_call(functools.partial(edge_kernel, ny, nx, devices), in_specs=...]
    pallas_call x3 -> x5, Pallas kernels: 26.2 us -> 24.5 us  [the longest x1 10.4 us: update(): pl.pallas_call(update_kernel, in_specs=vmem(9), out_specs=hbm(2), out_sha...]
    unnamed x2 -> x0, local copies, waits for them, and re-layouts: 0.69 us -> none
  transfers between devices with their start and end apart: 4 -> 4, of which waited for: 1 -> 0; matrix products, arithmetic and copies ran while one was open for 0% -> 0% of each run, Pallas kernels for 18% -> 23%
where the time goes in v4:
time: 53.4 us; the launch traced here: 53.1 us
  Pallas kernels  31.2 us (58%)
  blocking collectives  16.7 us (31%)
  starting transfers between devices  4.45 us (8%)
  between operations  0.7 us (1%)
    all_to_all x1, blocking collectives, shards(): parts = lax.all_to_all(gram, ('gx', 'gy'), 0, 0, tiled=True)  16.7 us
    pallas_call x1, Pallas kernels, update(): pl.pallas_call(update_kernel, in_specs=vmem(9), out_specs=hbm(2), out_sha...  10.4 us
    pallas_call x1, Pallas kernels, clean_second(): pl.pallas_call(functools.partial(clean_second_kernel, ny, nx), in_specs=v...  5.45 us
    pallas_call x1, Pallas kernels, edge_powers(): pl.pallas_call(functools.partial(edge_kernel, ny, nx, devices), in_specs=...  4.91 us
    pallas_call x1, Pallas kernels, load(): pl.pallas_call(load_kernel, in_specs=hbm(7), out_specs=vmem(8), out_shape...  4.61 us
    ppermute x1, starting transfers between devices, shards(): ye = lax.ppermute(ye, 'gy', even_pairs(gy))  2.57 us
    pallas_call x1, Pallas kernels, clean_first(): pl.pallas_call(functools.partial(clean_first_kernel, ny, nx), in_specs=vm...  2.27 us
    pallas_call x1, Pallas kernels, partial_residual(): pl.pallas_call(functools.partial(partial_kernel, gx, gy), in_specs=vmem(9...  1.86 us
  transfers between devices with their start and end apart: 4, of which 0 were waited for; matrix products, arithmetic and copies ran while one was open for 0% of the time, Pallas kernels for 23%

profile of v4, /device:TPU:0, one launch (start us, length us, event | category | flops | bytes accessed | tf_op | source)
XLA Modules:
  0.0 53.1 jit_solution(15875280978887993295)
XLA Ops:
  0.6 1.7 %x_edges.1 = (f32[2,16,8,128]{3,2,1,0:T(8,128)S(1)}, f32[2,16,8,128]{3,2,1,0:T(8,128)S(1)}) custom-call(f32[8,64,16,128]{3,2,1,0:T(8,128)} %it_hbm.3, f32[64,16,128]{2,1,0:T(8,128)} %src_hbm.3, f32[64,16,128]{2,1,0:T(8,128)} %dg_hbm.3, f32[64,16,128]{2,1,0:T(8,128)} %fx_hbm.3, f32[64,16,128]{2,1,0:T(8,128)} %fy_hbm.3, f32[64,16,128]{2,1,0:T(8,128)} %fz_hbm.3, ...), custom_call_target="tpu_custom_call" | custom-call | tf_op jit(solution)/shard_map/x_edges/pallas_call | solution.py:127
  2.4 0.6 %collective-permute-start = (f32[2,16,8,128]{3,2,1,0:T(8,128)S(1)}, f32[2,16,8,128]{3,2,1,0:T(8,128)S(1)}, u32[]{:S(2)}, u32[]{:S(2)}) collective-permute-start(f32[2,16,8,128]{3,2,1,0:T(8,128)S(1)} %get-tuple-element.37), channel_id=1, source_target_pairs={{0,8},{8,0},{16,24},{24,16},{1,9},{9,1},{17,25},{25,17},{2,10},{10... | collective-permute-start | bytes 393224 | tf_op jit(solution)/shard_map/ppermute | solution.py:825
  2.9 0.7 %collective-permute-start.1 = (f32[2,16,8,128]{3,2,1,0:T(8,128)S(1)}, f32[2,16,8,128]{3,2,1,0:T(8,128)S(1)}, u32[]{:S(2)}, u32[]{:S(2)}) collective-permute-start(f32[2,16,8,128]{3,2,1,0:T(8,128)S(1)} %get-tuple-element.38), channel_id=1, source_target_pairs={{8,16},{16,8},{9,17},{17,9},{10,18},{18,10},{11,19},{19,11},{12,20... | collective-permute-start | bytes 393224 | tf_op jit(solution)/shard_map/ppermute | solution.py:824
  3.6 4.6 %load.1 = (f32[16,64,128]{2,1,0:T(8,128)S(1)}, f32[16,64,128]{2,1,0:T(8,128)S(1)}, f32[16,64,128]{2,1,0:T(8,128)S(1)}, f32[16,64,128]{2,1,0:T(8,128)S(1)}, f32[1...) custom-call(f32[8,64,16,128]{3,2,1,0:T(8,128)} %it_hbm.3, ...), custom_call_target="tpu_custom_call" | custom-call | flops 2000000 | bytes 16000000 | tf_op jit(solution)/shard_map/load/pallas_call | solution.py:196
  8.2 0.0 collective-permute-done.xe_ref
  8.2 0.0 collective-permute-done.1.xo_ref
  8.2 1.9 %partial_residual.1 = (f32[1280,128]{1,0:T(8,128)S(1)}, f32[1280,128]{1,0:T(8,128)S(1)}, f32[1280,128]{1,0:T(8,128)S(1)}, f32[1280,128]{1,0:T(8,128)S(1)}, f32[1...) custom-call(f32[16,64,128]{2,1,0:T(8,128)S(1)} %get-tuple-element.30.s_in, ...), custom_call_target="tpu_custom_call" | custom-call | tf_op jit(solution)/shard_map/partial_residual/pallas_call | solution.py:330
  10.1 2.6 %collective-permute-start.2 = (f32[488,128]{1,0:T(8,128)S(1)}, f32[488,128]{1,0:T(8,128)S(1)}, u32[]{:S(2)}, u32[]{:S(2)}) collective-permute-start(f32[488,128]{1,0:T(8,128)S(1)} %get-tuple-element.48), channel_id=1, source_target_pairs={{0,1},{1,0},{2,3},{3,2},{4,5},{5,4},{6,7},{7,6},{8,9},{9,8},{10,11... | collective-permute-start | bytes 749576 | tf_op jit(solution)/shard_map/ppermute | solution.py:828
  12.7 2.3 %clean_first.1 = (f32[8,960,128]{2,1,0:T(8,128)S(1)}, f32[488,128]{1,0:T(8,128)S(1)}) custom-call(f32[1280,128]{1,0:T(8,128)S(1)} %get-tuple-element.39.t_ref, f32[1280,128]{1,0:T(8,128)S(1)} %get-tuple-element.40.s_ref, f32[1280,128]{1,0:T(8,128)S(1)} %get-tuple-element.41.fx_ref, f32[1280,128]{1,0:T(8,128)S(1)} %get-tuple-element.42.fy_ref, ...), custom_call_target="tpu_custom_call" | custom-call | flops 20000000 | bytes 8000000 | tf_op jit(solution)/shard_map/clean_first/pallas_call | solution.py:466
  14.9 0.7 %collective-permute-start.3 = (f32[488,128]{1,0:T(8,128)S(1)}, f32[488,128]{1,0:T(8,128)S(1)}, u32[]{:S(2)}, u32[]{:S(2)}) collective-permute-start(f32[488,128]{1,0:T(8,128)S(1)} %get-tuple-element.49), channel_id=1, source_target_pairs={{1,2},{2,1},{3,4},{4,3},{5,6},{6,5},{9,10},{10,9},{11,12},{12,11},... | collective-permute-start | bytes 749576 | tf_op jit(solution)/shard_map/ppermute | solution.py:830
  15.6 5.4 %clean_second.1 = (f32[8,640,128]{2,1,0:T(8,128)S(1)}, f32[116,8,128]{2,1,0:T(8,128)S(1)}) custom-call(f32[1280,128]{1,0:T(8,128)S(1)} %get-tuple-element.39.t_ref, f32[1280,128]{1,0:T(8,128)S(1)} %get-tuple-element.41.fx_ref, f32[1280,128]{1,0:T(8,128)S(1)} %get-tuple-element.42.fy_ref, f32[1280,128]{1,0:T(8,128)S(1)} %get-tuple-element.43.dg_ref, ...), custom_call_target="tpu_custom_call" | custom-call | flops 40000000 | bytes 12000000 | tf_op jit(solution)/shard_map/clean_second/pallas_call | solution.py:480
  21.1 0.0 collective-permute-done.2.ye_ref
  21.1 0.0 collective-permute-done.3.yo_ref
  21.1 4.9 %edge_powers.1 = (f32[8,960,128]{2,1,0:T(8,128)S(1)}, f32[8,384,128]{2,1,0:T(8,128)S(1)}, f32[960,128]{1,0:T(8,128)S(1)}, f32[960,128]{1,0:T(8,128)}, f32[32,2,128]{2,1,0:T(2,128)S(1)}) custom-call(f32[1280,128]{1,0:T(8,128)S(1)} %get-tuple-element.39.t_ref, f32[1280,128]{1,0:T(8,128)S(1)} %get-tuple-element.40.s_ref, ...), custom_call_target="tpu_custom_call" | custom-call | tf_op jit(solution)/shard_map/edge_powers/pallas_call | solution.py:634
  26.0 16.7 %all_to_all.5.parts_ref = f32[32,2,128]{2,1,0:T(2,128)S(1)} all-to-all(f32[32,2,128]{2,1,0:T(2,128)S(1)} %get-tuple-element.50), channel_id=1, replica_groups=mesh['gx'=4,'gy'=8] {'gx','gy'}, dimensions={0} | all-to-all | bytes 65536 | tf_op jit(solution)/shard_map/all_to_all | solution.py:833
  42.7 10.4 %update.1 = (f32[8,1024,128]{2,1,0:T(8,128)}, f32[1024,128]{1,0:T(8,128)}) custom-call(f32[32,2,128]{2,1,0:T(2,128)S(1)} %all_to_all.5.parts_ref, f32[8,960,128]{2,1,0:T(8,128)S(1)} %get-tuple-element.46.p_out.pc_ref, f32[8,640,128]{2,1,0:T(8,128)S(1)} %get-tuple-element.51.qc_ref, f32[8,960,128]{2,1,0:T(8,128)S(1)} %get-tuple-element.52.pd_ref, ...), custom_call_target="tpu_custom_call" | custom-call | tf_op jit(solution)/shard_map/update/pallas_call | solution.py:800
Async XLA Ops:
  2.4 5.8 %collective-permute-start = (f32[2,16,8,128]{3,2,1,0:T(8,128)S(1)}, f32[2,16,8,128]{3,2,1,0:T(8,128)S(1)}, u32[]{:S(2)}, u32[]{:S(2)}) collective-permute-start(f32[2,16,8,128]{3,2,1,0:T(8,128)S(1)} %get-tuple-element.37), channel_id=1, source_target_pairs={{0,8},{8,0},{16,24},{24,16},{1,9},{9,1},{17,25},{25,17},{2,10},{10... | collective-permute-start | bytes 393224 | tf_op jit(solution)/shard_map/ppermute | solution.py:825
  2.9 5.3 %collective-permute-start.1 = (f32[2,16,8,128]{3,2,1,0:T(8,128)S(1)}, f32[2,16,8,128]{3,2,1,0:T(8,128)S(1)}, u32[]{:S(2)}, u32[]{:S(2)}) collective-permute-start(f32[2,16,8,128]{3,2,1,0:T(8,128)S(1)} %get-tuple-element.38), channel_id=1, source_target_pairs={{8,16},{16,8},{9,17},{17,9},{10,18},{18,10},{11,19},{19,11},{12,20... | collective-permute-start | bytes 393224 | tf_op jit(solution)/shard_map/ppermute | solution.py:824
  10.1 11.0 %collective-permute-start.2 = (f32[488,128]{1,0:T(8,128)S(1)}, f32[488,128]{1,0:T(8,128)S(1)}, u32[]{:S(2)}, u32[]{:S(2)}) collective-permute-start(f32[488,128]{1,0:T(8,128)S(1)} %get-tuple-element.48), channel_id=1, source_target_pairs={{0,1},{1,0},{2,3},{3,2},{4,5},{5,4},{6,7},{7,6},{8,9},{9,8},{10,11... | collective-permute-start | bytes 749576 | tf_op jit(solution)/shard_map/ppermute | solution.py:828
  14.9 6.1 %collective-permute-start.3 = (f32[488,128]{1,0:T(8,128)S(1)}, f32[488,128]{1,0:T(8,128)S(1)}, u32[]{:S(2)}, u32[]{:S(2)}) collective-permute-start(f32[488,128]{1,0:T(8,128)S(1)} %get-tuple-element.49), channel_id=1, source_target_pairs={{1,2},{2,1},{3,4},{4,3},{5,6},{6,5},{9,10},{10,9},{11,12},{12,11},... | collective-permute-start | bytes 749576 | tf_op jit(solution)/shard_map/ppermute | solution.py:830

commit v5 on v4

--- a/solution.py
+++ b/solution.py
@@ -673,8 +673,9 @@
     m = jnp.concatenate([dot(lhs, upper), dot(lhs, lower)], axis=0)
     row = iota(m.shape, 0)
     for i in range(2 * ENLARGE):
-        pivot = m[i : i + 1] / m[i : i + 1, i : i + 1]
-        m = jnp.where(row == i, pivot, m - m[:, i : i + 1] * pivot)
+        column = jnp.broadcast_to(m[:, i : i + 1], m.shape)
+        pivot = m[i : i + 1] / column[i : i + 1]
+        m = jnp.where(row == i, pivot, m - column * pivot)
     return m
 
 
@@ -733,18 +734,13 @@
     loop(ny * nx // 128, coefficients, unroll=2)
 
     def spots(c, visit):
-        def clean(i):
-            x = PAD + c * 8
+        x = PAD + c * 8
+        for i in range(ny - 6):
             visit(i + 3, pc_ref, (i + 1) * pitch + x, qc_ref, i * nx + c * 8, t_ref, (i + 3) * pitch + x)
-
-        loop(ny - 6, clean, unroll=2)
-
-        def edge(i):
-            at = (i + 2 + jnp.where(i >= 3, 2, 0)) * pitch + PAD + c * 8
-            y = i + jnp.where(i >= 3, ny - 6, 0)
+        for i in range(6):
+            at = (i + 2 + (2 if i >= 3 else 0)) * pitch + x
+            y = i + (ny - 6 if i >= 3 else 0)
             visit(y, pd_ref, at, qd_ref, i * nx + c * 8, rd_ref, at)
-
-        loop(6, edge, unroll=2)
 
     def place(c, y):
         return pl.ds(c * 8 * ny + y, 8, stride=ny)

time: 53.4 us -> 50.7 us (0.949)
  Pallas kernels: 31.2 us -> 28.5 us
    pallas_call x1, Pallas kernels: 10.4 us -> 7.67 us  [update(): pl.pallas_call(update_kernel, in_specs=vmem(9), out_specs=hbm(2), out_sha...]
  transfers between devices with their start and end apart: 4 -> 4, of which waited for: 0 -> 0; matrix products, arithmetic and copies ran while one was open for 0% -> 0% of each run, Pallas kernels for 23% -> 24%
where the time goes in v5:
time: 50.7 us; the launch traced here: 50.4 us
  Pallas kernels  28.5 us (56%)
  blocking collectives  16.7 us (33%)
  starting transfers between devices  4.45 us (9%)
  between operations  0.7 us (1%)
    all_to_all x1, blocking collectives, shards(): parts = lax.all_to_all(gram, ('gx', 'gy'), 0, 0, tiled=True)  16.7 us
    pallas_call x1, Pallas kernels, update(): pl.pallas_call(update_kernel, in_specs=vmem(9), out_specs=hbm(2), out_sha...  7.67 us
    pallas_call x1, Pallas kernels, clean_second(): pl.pallas_call(functools.partial(clean_second_kernel, ny, nx), in_specs=v...  5.45 us
    pallas_call x1, Pallas kernels, edge_powers(): pl.pallas_call(functools.partial(edge_kernel, ny, nx, devices), in_specs=...  4.91 us
    pallas_call x1, Pallas kernels, load(): pl.pallas_call(load_kernel, in_specs=hbm(7), out_specs=vmem(8), out_shape...  4.61 us
    ppermute x1, starting transfers between devices, shards(): ye = lax.ppermute(ye, 'gy', even_pairs(gy))  2.57 us
    pallas_call x1, Pallas kernels, clean_first(): pl.pallas_call(functools.partial(clean_first_kernel, ny, nx), in_specs=vm...  2.27 us
    pallas_call x1, Pallas kernels, partial_residual(): pl.pallas_call(functools.partial(partial_kernel, gx, gy), in_specs=vmem(9...  1.86 us
  transfers between devices with their start and end apart: 4, of which 0 were waited for; matrix products, arithmetic and copies ran while one was open for 0% of the time, Pallas kernels for 24%

profile of v5, /device:TPU:0, one launch (start us, length us, event | category | flops | bytes accessed | tf_op | source)
XLA Modules:
  0.0 50.4 jit_solution(10689058580725624378)
XLA Ops:
  0.6 1.7 %x_edges.1 = (f32[2,16,8,128]{3,2,1,0:T(8,128)S(1)}, f32[2,16,8,128]{3,2,1,0:T(8,128)S(1)}) custom-call(f32[8,64,16,128]{3,2,1,0:T(8,128)} %it_hbm.3, f32[64,16,128]{2,1,0:T(8,128)} %src_hbm.3, f32[64,16,128]{2,1,0:T(8,128)} %dg_hbm.3, f32[64,16,128]{2,1,0:T(8,128)} %fx_hbm.3, f32[64,16,128]{2,1,0:T(8,128)} %fy_hbm.3, f32[64,16,128]{2,1,0:T(8,128)} %fz_hbm.3, ...), custom_call_target="tpu_custom_call" | custom-call | tf_op jit(solution)/shard_map/x_edges/pallas_call | solution.py:127
  2.4 0.6 %collective-permute-start = (f32[2,16,8,128]{3,2,1,0:T(8,128)S(1)}, f32[2,16,8,128]{3,2,1,0:T(8,128)S(1)}, u32[]{:S(2)}, u32[]{:S(2)}) collective-permute-start(f32[2,16,8,128]{3,2,1,0:T(8,128)S(1)} %get-tuple-element.37), channel_id=1, source_target_pairs={{0,8},{8,0},{16,24},{24,16},{1,9},{9,1},{17,25},{25,17},{2,10},{10... | collective-permute-start | bytes 393224 | tf_op jit(solution)/shard_map/ppermute | solution.py:821
  2.9 0.7 %collective-permute-start.1 = (f32[2,16,8,128]{3,2,1,0:T(8,128)S(1)}, f32[2,16,8,128]{3,2,1,0:T(8,128)S(1)}, u32[]{:S(2)}, u32[]{:S(2)}) collective-permute-start(f32[2,16,8,128]{3,2,1,0:T(8,128)S(1)} %get-tuple-element.38), channel_id=1, source_target_pairs={{8,16},{16,8},{9,17},{17,9},{10,18},{18,10},{11,19},{19,11},{12,20... | collective-permute-start | bytes 393224 | tf_op jit(solution)/shard_map/ppermute | solution.py:820
  3.6 4.6 %load.1 = (f32[16,64,128]{2,1,0:T(8,128)S(1)}, f32[16,64,128]{2,1,0:T(8,128)S(1)}, f32[16,64,128]{2,1,0:T(8,128)S(1)}, f32[16,64,128]{2,1,0:T(8,128)S(1)}, f32[1...) custom-call(f32[8,64,16,128]{3,2,1,0:T(8,128)} %it_hbm.3, ...), custom_call_target="tpu_custom_call" | custom-call | flops 2000000 | bytes 16000000 | tf_op jit(solution)/shard_map/load/pallas_call | solution.py:196
  8.2 0.0 collective-permute-done.xe_ref
  8.2 0.0 collective-permute-done.1.xo_ref
  8.2 1.9 %partial_residual.1 = (f32[1280,128]{1,0:T(8,128)S(1)}, f32[1280,128]{1,0:T(8,128)S(1)}, f32[1280,128]{1,0:T(8,128)S(1)}, f32[1280,128]{1,0:T(8,128)S(1)}, f32[1...) custom-call(f32[16,64,128]{2,1,0:T(8,128)S(1)} %get-tuple-element.30.s_in, ...), custom_call_target="tpu_custom_call" | custom-call | tf_op jit(solution)/shard_map/partial_residual/pallas_call | solution.py:330
  10.1 2.6 %collective-permute-start.2 = (f32[488,128]{1,0:T(8,128)S(1)}, f32[488,128]{1,0:T(8,128)S(1)}, u32[]{:S(2)}, u32[]{:S(2)}) collective-permute-start(f32[488,128]{1,0:T(8,128)S(1)} %get-tuple-element.48), channel_id=1, source_target_pairs={{0,1},{1,0},{2,3},{3,2},{4,5},{5,4},{6,7},{7,6},{8,9},{9,8},{10,11... | collective-permute-start | bytes 749576 | tf_op jit(solution)/shard_map/ppermute | solution.py:824
  12.7 2.3 %clean_first.1 = (f32[8,960,128]{2,1,0:T(8,128)S(1)}, f32[488,128]{1,0:T(8,128)S(1)}) custom-call(f32[1280,128]{1,0:T(8,128)S(1)} %get-tuple-element.39.t_ref, f32[1280,128]{1,0:T(8,128)S(1)} %get-tuple-element.40.s_ref, f32[1280,128]{1,0:T(8,128)S(1)} %get-tuple-element.41.fx_ref, f32[1280,128]{1,0:T(8,128)S(1)} %get-tuple-element.42.fy_ref, ...), custom_call_target="tpu_custom_call" | custom-call | flops 20000000 | bytes 8000000 | tf_op jit(solution)/shard_map/clean_first/pallas_call | solution.py:466
  14.9 0.7 %collective-permute-start.3 = (f32[488,128]{1,0:T(8,128)S(1)}, f32[488,128]{1,0:T(8,128)S(1)}, u32[]{:S(2)}, u32[]{:S(2)}) collective-permute-start(f32[488,128]{1,0:T(8,128)S(1)} %get-tuple-element.49), channel_id=1, source_target_pairs={{1,2},{2,1},{3,4},{4,3},{5,6},{6,5},{9,10},{10,9},{11,12},{12,11},... | collective-permute-start | bytes 749576 | tf_op jit(solution)/shard_map/ppermute | solution.py:826
  15.6 5.4 %clean_second.1 = (f32[8,640,128]{2,1,0:T(8,128)S(1)}, f32[116,8,128]{2,1,0:T(8,128)S(1)}) custom-call(f32[1280,128]{1,0:T(8,128)S(1)} %get-tuple-element.39.t_ref, f32[1280,128]{1,0:T(8,128)S(1)} %get-tuple-element.41.fx_ref, f32[1280,128]{1,0:T(8,128)S(1)} %get-tuple-element.42.fy_ref, f32[1280,128]{1,0:T(8,128)S(1)} %get-tuple-element.43.dg_ref, ...), custom_call_target="tpu_custom_call" | custom-call | flops 40000000 | bytes 12000000 | tf_op jit(solution)/shard_map/clean_second/pallas_call | solution.py:480
  21.1 0.0 collective-permute-done.2.ye_ref
  21.1 0.0 collective-permute-done.3.yo_ref
  21.1 4.9 %edge_powers.1 = (f32[8,960,128]{2,1,0:T(8,128)S(1)}, f32[8,384,128]{2,1,0:T(8,128)S(1)}, f32[960,128]{1,0:T(8,128)S(1)}, f32[960,128]{1,0:T(8,128)}, f32[32,2,128]{2,1,0:T(2,128)S(1)}) custom-call(f32[1280,128]{1,0:T(8,128)S(1)} %get-tuple-element.39.t_ref, f32[1280,128]{1,0:T(8,128)S(1)} %get-tuple-element.40.s_ref, ...), custom_call_target="tpu_custom_call" | custom-call | tf_op jit(solution)/shard_map/edge_powers/pallas_call | solution.py:634
  26.0 16.7 %all_to_all.5.parts_ref = f32[32,2,128]{2,1,0:T(2,128)S(1)} all-to-all(f32[32,2,128]{2,1,0:T(2,128)S(1)} %get-tuple-element.50), channel_id=1, replica_groups=mesh['gx'=4,'gy'=8] {'gx','gy'}, dimensions={0} | all-to-all | bytes 65536 | tf_op jit(solution)/shard_map/all_to_all | solution.py:829
  42.7 7.7 %update.1 = (f32[8,1024,128]{2,1,0:T(8,128)}, f32[1024,128]{1,0:T(8,128)}) custom-call(f32[32,2,128]{2,1,0:T(2,128)S(1)} %all_to_all.5.parts_ref, f32[8,960,128]{2,1,0:T(8,128)S(1)} %get-tuple-element.46.p_out.pc_ref, f32[8,640,128]{2,1,0:T(8,128)S(1)} %get-tuple-element.51.qc_ref, f32[8,960,128]{2,1,0:T(8,128)S(1)} %get-tuple-element.52.pd_ref, ...), custom_call_target="tpu_custom_call" | custom-call | tf_op jit(solution)/shard_map/update/pallas_call | solution.py:796
Async XLA Ops:
  2.4 5.8 %collective-permute-start = (f32[2,16,8,128]{3,2,1,0:T(8,128)S(1)}, f32[2,16,8,128]{3,2,1,0:T(8,128)S(1)}, u32[]{:S(2)}, u32[]{:S(2)}) collective-permute-start(f32[2,16,8,128]{3,2,1,0:T(8,128)S(1)} %get-tuple-element.37), channel_id=1, source_target_pairs={{0,8},{8,0},{16,24},{24,16},{1,9},{9,1},{17,25},{25,17},{2,10},{10... | collective-permute-start | bytes 393224 | tf_op jit(solution)/shard_map/ppermute | solution.py:821
  2.9 5.3 %collective-permute-start.1 = (f32[2,16,8,128]{3,2,1,0:T(8,128)S(1)}, f32[2,16,8,128]{3,2,1,0:T(8,128)S(1)}, u32[]{:S(2)}, u32[]{:S(2)}) collective-permute-start(f32[2,16,8,128]{3,2,1,0:T(8,128)S(1)} %get-tuple-element.38), channel_id=1, source_target_pairs={{8,16},{16,8},{9,17},{17,9},{10,18},{18,10},{11,19},{19,11},{12,20... | collective-permute-start | bytes 393224 | tf_op jit(solution)/shard_map/ppermute | solution.py:820
  10.1 11.0 %collective-permute-start.2 = (f32[488,128]{1,0:T(8,128)S(1)}, f32[488,128]{1,0:T(8,128)S(1)}, u32[]{:S(2)}, u32[]{:S(2)}) collective-permute-start(f32[488,128]{1,0:T(8,128)S(1)} %get-tuple-element.48), channel_id=1, source_target_pairs={{0,1},{1,0},{2,3},{3,2},{4,5},{5,4},{6,7},{7,6},{8,9},{9,8},{10,11... | collective-permute-start | bytes 749576 | tf_op jit(solution)/shard_map/ppermute | solution.py:824
  14.9 6.1 %collective-permute-start.3 = (f32[488,128]{1,0:T(8,128)S(1)}, f32[488,128]{1,0:T(8,128)S(1)}, u32[]{:S(2)}, u32[]{:S(2)}) collective-permute-start(f32[488,128]{1,0:T(8,128)S(1)} %get-tuple-element.49), channel_id=1, source_target_pairs={{1,2},{2,1},{3,4},{4,3},{5,6},{6,5},{9,10},{10,9},{11,12},{12,11},... | collective-permute-start | bytes 749576 | tf_op jit(solution)/shard_map/ppermute | solution.py:826

commit v6 on v5

--- a/solution.py
+++ b/solution.py
@@ -378,8 +378,9 @@
 def clean_first_kernel(
     ny, nx,
     t_ref, s_ref, fx_ref, fy_ref, dg_ref, fz_ref, lb_ref,
-    p_out, yo_ref,
+    p_out, acc_out, yo_ref,
 ):
+    nz = t_ref.shape[-1]
     pitch = nx + 2 * PAD
 
     def first(i):
@@ -401,6 +402,16 @@
                 p_out[j, eight(i * pitch + r)] = values
 
     loop(ny - 4, first)
+
+    def p_dots(i, sums):
+        for r in range(PAD, PAD + nx, 8):
+            p = [p_out[j, eight(i * pitch + r)] for j in range(ENLARGE)]
+            sums = dot_pairs(sums, p, p)
+        return sums
+
+    sums = lax.fori_loop(0, ny - 4, p_dots, zeros_like_pairs(nz, len(PAIRS)))
+    for n, values in enumerate(sums):
+        acc_out[n] = values
     odd_y = lax.rem(lax.axis_index("gy"), 2) == 1
     pack_y_edge(ny, nx, yo_ref, odd_y, t_ref, s_ref, fy_ref, fx_ref, dg_ref, fz_ref, lb_ref)
 
@@ -439,12 +450,6 @@
             sums = dot_own(sums, t_ref[shifted], lb_ref[shifted], fields_at(p_out, row))
         return sums
 
-    def p_dots(i, sums):
-        for c in range(chunks):
-            p = fields_at(p_out, i * pitch + PAD + c * 8)
-            sums = dot_pairs(sums, p, p)
-        return sums
-
     def q_dots(i, sums):
         for c in range(chunks):
             p = fields_at(p_out, (i + 1) * pitch + PAD + c * 8)
@@ -452,9 +457,7 @@
         return sums
 
     slot = 0
-    for dots, layers, count in (
-        (own_dots, ny - 4, len(PAIRS) + ENLARGE), (p_dots, ny - 4, len(PAIRS)), (q_dots, ny - 6, len(PAIRS)),
-    ):
+    for dots, layers, count in ((own_dots, ny - 4, len(PAIRS) + ENLARGE), (q_dots, ny - 6, len(PAIRS))):
         sums = lax.fori_loop(0, layers, dots, zeros_like_pairs(nz, count))
         for values in sums:
             acc_out[slot] = values
@@ -466,8 +469,12 @@
     return pl.pallas_call(
         functools.partial(clean_first_kernel, ny, nx),
         in_specs=vmem(7),
-        out_specs=vmem(2),
-        out_shape=[array(ENLARGE, (ny - 4) * (nx + 2 * PAD), nz), array(blocks_of(nx)[1][-1], nz)],
+        out_specs=vmem(3),
+        out_shape=[
+            array(ENLARGE, (ny - 4) * (nx + 2 * PAD), nz),
+            array(len(PAIRS), 8, nz),
+            array(blocks_of(nx)[1][-1], nz),
+        ],
         compiler_params=params(),
         cost_estimate=pl.CostEstimate(flops=20_000_000, bytes_accessed=8_000_000, transcendentals=0),
         name="clean_first",
@@ -481,89 +488,87 @@
         functools.partial(clean_second_kernel, ny, nx),
         in_specs=vmem(7),
         out_specs=vmem(2),
-        out_shape=[array(ENLARGE, (ny - 6) * nx, nz), array(3 * len(PAIRS) + ENLARGE, 8, nz)],
+        out_shape=[array(ENLARGE, (ny - 6) * nx, nz), array(2 * len(PAIRS) + ENLARGE, 8, nz)],
         compiler_params=params(),
         cost_estimate=pl.CostEstimate(flops=40_000_000, bytes_accessed=12_000_000, transcendentals=0),
         name="clean_second",
     )(t, fx, fy, dg, fz, lb, pc)
 
 
-def edge_slot(y, ny):
-    return y + 2 if y < 4 else y - (ny - 4) + 6
+def side_of(phase):
+    odd = lax.rem(lax.axis_index("gy"), 2)
+    return odd if phase else 1 - odd
 
 
 def edge_kernel(
-    ny, nx, devices,
-    t_ref, s_ref, fx_ref, fy_ref, dg_ref, fz_ref, lb_ref, pc_ref, acc_ref, ye_ref, yo_ref,
-    p_out, q_out, r_out, lb_out, gram_out,
-    packs, fx, fy, dg, fz, rows_acc,
+    ny, nx, phase, devices,
+    t_ref, s_ref, fx_ref, fy_ref, dg_ref, fz_ref, lb_ref, pc_ref, acc_pp, acc_ref, pack,
+    p_out, q_out, r_out, *rest,
 ):
+    outs, (lb, fx, fy, dg, fz, rows_acc) = rest[:-6], rest[-6:]
     nz = t_ref.shape[-1]
     pitch = nx + 2 * PAD
     chunks = nx // 8
     wide, starts = blocks_of(nx)
     left = PAD - SENT
-    odd = lax.rem(lax.axis_index("gy"), 2)
-    packs[1 - odd] = ye_ref[...]
-    packs[odd] = yo_ref[...]
-
-    def packed(side, b):
-        return packs[side, starts[b] : starts[b + 1]]
-
-    for side in range(2):
+    side = side_of(phase)
+
+    def packed(b):
+        return pack[starts[b] : starts[b + 1]]
+
+    def setup(which):
+        first, skip = (0, 2) if which == 0 else (ny - 4, 0)
         for i in range(4):
-            source = ((side * (ny - 4)) + i) * pitch
-            dest = (side * 4 + i + 2) * pitch
-            for ref, out in ((t_ref, r_out), (lb_ref, lb_out), (fx_ref, fx), (fy_ref, fy), (dg_ref, dg), (fz_ref, fz)):
+            source, dest = (first + i) * pitch, (skip + i) * pitch
+            for ref, out in ((t_ref, r_out), (lb_ref, lb), (fx_ref, fx), (fy_ref, fy), (dg_ref, dg), (fz_ref, fz)):
                 out[dest : dest + pitch] = ref[source : source + pitch]
+        first, skip = (0, 4) if which == 0 else (ny - 6, 0)
         for i in range(2):
-            source = (side * (ny - 6) + i) * pitch
-            dest = (side * 2 + i + 4) * pitch
+            source, dest = (first + i) * pitch, (skip + i) * pitch
             p_out[:, dest : dest + pitch] = pc_ref[:, source : source + pitch]
-    for side in range(2):
-        inner, ghost, far = (0, -1, -2) if side == 0 else (ny - 1, ny, ny + 1)
-        at = lambda y, start=left, size=wide: pl.ds(edge_slot(y, ny) * pitch + start, size)
-        base = pl.ds(inner * pitch + left, wide)
-        face = packed(side, 2) if side == 0 else fy_ref[base]
-        r_out[at(ghost)] = packed(side, 0) + face * s_ref[base]
-        r_out[at(inner)] = t_ref[base] + face * packed(side, 1)
-        if side == 0:
+        inner, ghost, far = (2, 1, 0) if which == 0 else (3, 4, 5)
+        at = lambda slot, start=left, size=wide: pl.ds(slot * pitch + start, size)
+        base = pl.ds((0 if which == 0 else ny - 1) * pitch + left, wide)
+        face = packed(2) if which == 0 else fy_ref[base]
+        r_out[at(ghost)] = packed(0) + face * s_ref[base]
+        r_out[at(inner)] = t_ref[base] + face * packed(1)
+        if which == 0:
             fy[at(ghost)] = face
-        fy[at(far if side == 0 else ghost)] = jnp.ones((wide, nz), F32)
-        r_out[at(far, PAD, nx)] = packed(side, 4)
-        fx[at(ghost)] = packed(side, 3)
-        dg[at(ghost, PAD, nx)] = packed(side, 5)
-        fz[at(ghost, PAD, nx)] = packed(side, 6)
-        labels = packed(side, 7)
+        fy[at(far if which == 0 else ghost)] = jnp.ones((wide, nz), F32)
+        r_out[at(far, PAD, nx)] = packed(4)
+        fx[at(ghost)] = packed(3)
+        dg[at(ghost, PAD, nx)] = packed(5)
+        fz[at(ghost, PAD, nx)] = packed(6)
+        labels = packed(7)
         spot = iota((wide, nz), 0) == iota((wide, nz), 1)
-        for r, y in ((0, ghost), (1, far)):
+        for r, slot in ((0, ghost), (1, far)):
             column = jnp.sum(jnp.where(spot, labels[r : r + 1], 0.0), axis=1, keepdims=True)
-            lb_out[at(y)] = jnp.broadcast_to(column, (wide, nz))
+            lb[at(slot)] = jnp.broadcast_to(column, (wide, nz))
+
+    for which in range(2):
+        pl.when(side == which)(functools.partial(setup, which))
 
     def first(i):
-        base = (i + 1 + jnp.where(i >= 3, 4, 0)) * pitch
+        base = (i + 1 + side) * pitch
         for r in range(0, pitch, 8):
             at = base + r
             here, below, above = eight(at), eight(at - pitch), eight(at + pitch)
             value = r_out[here]
             parts = [
-                ((dg[here] - SHIFT) * value - along_z(fz[here], value), lb_out[here]),
-                (-fx[here] * r_out[near(at + 1)], lb_out[near(at + 1)]),
-                (-fx[near(at - 1)] * r_out[near(at - 1)], lb_out[near(at - 1)]),
-                (-fy[here] * r_out[above], lb_out[above]),
-                (-fy[below] * r_out[below], lb_out[below]),
+                ((dg[here] - SHIFT) * value - along_z(fz[here], value), lb[here]),
+                (-fx[here] * r_out[near(at + 1)], lb[near(at + 1)]),
+                (-fx[near(at - 1)] * r_out[near(at - 1)], lb[near(at - 1)]),
+                (-fy[here] * r_out[above], lb[above]),
+                (-fy[below] * r_out[below], lb[below]),
             ]
             for j, values in enumerate(spread(parts)):
                 p_out[j, here] = values
 
-    loop(6, first)
-
-    def q_slot(i):
-        return i + 2 + jnp.where(i >= 3, 2, 0)
+    loop(3, first)
 
     def second(i):
         for c in range(chunks):
-            at = q_slot(i) * pitch + PAD + c * 8
+            at = (i + 2 - side) * pitch + PAD + c * 8
             here, below, above = eight(at), eight(at - pitch), eight(at + pitch)
             d, z, fxp, fxm, fyp, fym = dg[here], fz[here], fx[here], fx[near(at - 1)], fy[here], fy[below]
             for j in range(ENLARGE):
@@ -572,84 +577,82 @@
                 q = q - fyp * p_out[j, above] - fym * p_out[j, below]
                 q_out[j, eight(i * nx + c * 8)] = q - along_z(z, p)
 
-    loop(6, second)
+    loop(3, second)
 
     def fields_at(ref, at):
         return [ref[j, eight(at)] for j in range(ENLARGE)]
 
     def own_dots(i, sums):
-        base = (i + 2 + jnp.where(i >= 2, 4, 0)) * pitch + PAD
         for c in range(chunks):
-            at = base + c * 8
-            sums = dot_own(sums, r_out[eight(at)], lb_out[eight(at)], fields_at(p_out, at))
+            at = (i + 2) * pitch + PAD + c * 8
+            sums = dot_own(sums, r_out[eight(at)], lb[eight(at)], fields_at(p_out, at))
         return sums
 
     def p_dots(i, sums):
-        base = (i + 2 + jnp.where(i >= 2, 4, 0)) * pitch + PAD
         for c in range(chunks):
-            p = fields_at(p_out, base + c * 8)
+            p = fields_at(p_out, (i + 2) * pitch + PAD + c * 8)
             sums = dot_pairs(sums, p, p)
         return sums
 
     def q_dots(i, sums):
-        base = q_slot(i) * pitch + PAD
         for c in range(chunks):
-            sums = dot_pairs(sums, fields_at(p_out, base + c * 8), fields_at(q_out, i * nx + c * 8))
+            p = fields_at(p_out, (i + 2 - side) * pitch + PAD + c * 8)
+            sums = dot_pairs(sums, p, fields_at(q_out, i * nx + c * 8))
         return sums
 
-    rows_acc[...] = jnp.zeros_like(rows_acc)
+    pairs = len(PAIRS)
     span = ENLARGE * ENLARGE
+    groups = (
+        (0, own_dots, 2, [(acc_ref, i) for i in range(pairs + ENLARGE)]),
+        (1, p_dots, 2, [(acc_pp, i) for i in range(pairs)]),
+        (2, q_dots, 3, [(acc_ref, pairs + ENLARGE + i) for i in range(pairs)]),
+    )
+    if phase:
+        rows_acc[...] = jnp.zeros_like(rows_acc)
 
     def put(slot, values):
         rows_acc[slot : slot + 1] = jnp.sum(values, axis=0, keepdims=True)
 
-    pairs = len(PAIRS)
-    begin = 0
-    for which, dots, layers, count in (
-        (0, own_dots, 4, pairs + ENLARGE), (1, p_dots, 4, pairs), (2, q_dots, 6, pairs),
-    ):
-        sums = tuple(acc_ref[begin + i] for i in range(count))
-        begin += count
+    for which, dots, layers, stored in groups:
+        sums = tuple(ref[i] for ref, i in stored)
         sums = lax.fori_loop(0, layers, dots, sums)
+        if not phase:
+            out = outs[0] if which == 1 else outs[1]
+            for (_, i), values in zip(stored, sums):
+                out[i] = values
+            continue
         for (j, k), values in zip(PAIRS, sums):
             put(which * span + j * ENLARGE + k, values)
             if j != k:
                 put(which * span + k * ENLARGE + j, values)
         for j, values in enumerate(sums[pairs:]):
             put(3 * span + j * ENLARGE + j, values)
-    ones = jnp.ones((8, nz), F32)
-    flat = lax.dot_general(
-        ones, rows_acc[...], (((1,), (1,)), ((), ())), precision=HIGHEST, preferred_element_type=F32
-    )
-    half = 2 * span
-    pair = jnp.where(iota((2, half), 0) == 0, flat[0:2, 0:half], flat[0:2, half : 2 * half])
-    for d in range(devices):
-        gram_out[d] = pair
-
-
-def edge_powers(ext, pc, acc, ye, yo, ny, nx, devices):
+    if phase:
+        ones = jnp.ones((8, nz), F32)
+        flat = lax.dot_general(
+            ones, rows_acc[...], (((1,), (1,)), ((), ())), precision=HIGHEST, preferred_element_type=F32
+        )
+        half = 2 * span
+        pair = jnp.where(iota((2, half), 0) == 0, flat[0:2, 0:half], flat[0:2, half : 2 * half])
+        for d in range(devices):
+            outs[0][d] = pair
+
+
+def edge_powers(phase, ext, pc, acc_pp, acc, pack, ny, nx, devices):
     nz = pc.shape[-1]
-    rows = 12 * (nx + 2 * PAD)
+    rows = 6 * (nx + 2 * PAD)
     half = 2 * ENLARGE * ENLARGE
+    result = [array(devices, 2, half)] if phase else [array(*acc_pp.shape), array(*acc.shape)]
     return pl.pallas_call(
-        functools.partial(edge_kernel, ny, nx, devices),
+        functools.partial(edge_kernel, ny, nx, phase, devices),
         in_specs=vmem(11),
-        out_specs=vmem(5),
-        out_shape=[
-            array(ENLARGE, rows, nz), array(ENLARGE, 6 * nx, nz), array(rows, nz), array(rows, nz),
-            array(devices, 2, half),
-        ],
-        scratch_shapes=[
-            pltpu.VMEM((2,) + ye.shape, F32),
-            pltpu.VMEM((rows, nz), F32),
-            pltpu.VMEM((rows, nz), F32),
-            pltpu.VMEM((rows, nz), F32),
-            pltpu.VMEM((rows, nz), F32),
-            pltpu.VMEM((2 * half, nz), F32),
-        ],
+        out_specs=vmem(3 + len(result)),
+        out_shape=[array(ENLARGE, rows, nz), array(ENLARGE, 3 * nx, nz), array(rows, nz)] + result,
+        scratch_shapes=[pltpu.VMEM((rows, nz), F32)] * 5 + [pltpu.VMEM((2 * half, nz), F32)],
         compiler_params=params(),
-        name="edge_powers",
-    )(*ext, pc, acc, ye, yo)
+        cost_estimate=pl.CostEstimate(flops=20_000_000, bytes_accessed=8_000_000, transcendentals=0),
+        name=f"edge_powers_{phase}",
+    )(*ext, pc, acc_pp, acc, pack)
 
 
 def solve_columns(parts):
@@ -672,15 +675,18 @@
     dot = functools.partial(jnp.dot, precision=HIGHEST, preferred_element_type=F32)
     m = jnp.concatenate([dot(lhs, upper), dot(lhs, lower)], axis=0)
     row = iota(m.shape, 0)
-    for i in range(2 * ENLARGE):
-        column = jnp.broadcast_to(m[:, i : i + 1], m.shape)
-        pivot = m[i : i + 1] / column[i : i + 1]
-        m = jnp.where(row == i, pivot, m - column * pivot)
-    return m
+    two = 2 * ENLARGE
+    columns = [jnp.broadcast_to(m[:, i : i + 1], m.shape) for i in range(two + ENLARGE)]
+    for i in range(two):
+        inverse = 1.0 / columns[i][i : i + 1]
+        for n in range(i + 1, two + ENLARGE):
+            scaled = jnp.broadcast_to(columns[n][i : i + 1] * inverse, m.shape)
+            columns[n] = jnp.where(row == i, scaled, columns[n] - columns[i] * scaled)
+    return columns[two:]
 
 
 def update_kernel(
-    parts_ref, pc_ref, qc_ref, pd_ref, qd_ref, t_ref, rd_ref, lb_ref, it_ref,
+    parts_ref, pc_ref, qc_ref, p0_ref, q0_ref, r0_ref, p1_ref, q1_ref, r1_ref, t_ref, lb_ref, it_ref,
     it_out, r_out,
     table, weights, onehot, own, work, r_work, sem_out, sem_r,
 ):
@@ -706,8 +712,7 @@
 
     loop(ny, mark)
 
-    m = solve_columns(parts_ref[...])
-    columns = [jnp.broadcast_to(m[:, two + j : two + j + 1], (two, nz)) for j in range(ENLARGE)]
+    columns = solve_columns(parts_ref[...])
     carried = columns[0]
     for column in columns[1:]:
         carried = carried + column
@@ -737,10 +742,15 @@
         x = PAD + c * 8
         for i in range(ny - 6):
             visit(i + 3, pc_ref, (i + 1) * pitch + x, qc_ref, i * nx + c * 8, t_ref, (i + 3) * pitch + x)
-        for i in range(6):
-            at = (i + 2 + (2 if i >= 3 else 0)) * pitch + x
-            y = i + (ny - 6 if i >= 3 else 0)
-            visit(y, pd_ref, at, qd_ref, i * nx + c * 8, rd_ref, at)
+        for phase, p_ref, q_ref, r_ref in ((0, p0_ref, q0_ref, r0_ref), (1, p1_ref, q1_ref, r1_ref)):
+            for side in range(2):
+
+                def visit_side(side=side, p_ref=p_ref, q_ref=q_ref, r_ref=r_ref):
+                    for i in range(3):
+                        at = (i + 2 - side) * pitch + x
+                        visit(i + side * (ny - 3), p_ref, at, q_ref, i * nx + c * 8, r_ref, at)
+
+                pl.when(side_of(phase) == side)(visit_side)
 
     def place(c, y):
         return pl.ds(c * 8 * ny + y, 8, stride=ny)
@@ -790,12 +800,12 @@
     loop(chunks, lambda c: copy_r(c).wait())
 
 
-def update(parts, pc, qc, pd, qd, t, rd, labels, held):
+def update(parts, pc, qc, edges, t, labels, held):
     _, ny, nx, nz = held.shape
     rows = nx * ny
     return pl.pallas_call(
         update_kernel,
-        in_specs=vmem(9),
+        in_specs=vmem(12),
         out_specs=hbm(2),
         out_shape=[array(ENLARGE, rows, nz), array(rows, nz)],
         scratch_shapes=[
@@ -810,7 +820,7 @@
         ],
         compiler_params=params(),
         name="update",
-    )(parts, pc, qc, pd, qd, t, rd, labels, held)
+    )(parts, pc, qc, *edges, t, labels, held)
 
 
 def shards(gx, gy, source, diagonal, face_x, face_y, face_z, iterates, labels):
@@ -822,12 +832,14 @@
     *fields, held = load(arrays)
     *ext, ye = partial_residual(fields, xe, xo, gx, gy)
     ye = lax.ppermute(ye, "gy", even_pairs(gy))
-    pc, yo = clean_first(ext, ny, nx)
+    pc, acc_pp, yo = clean_first(ext, ny, nx)
     yo = lax.ppermute(yo, "gy", odd_pairs(gy))
     qc, acc = clean_second(ext, pc, ny, nx)
-    pd, qd, rd, _, gram = edge_powers(ext, pc, acc, ye, yo, ny, nx, gx * gy)
+    p0, q0, r0, acc_pp, acc = edge_powers(0, ext, pc, acc_pp, acc, ye, ny, nx, gx * gy)
+    p1, q1, r1, gram = edge_powers(1, ext, pc, acc_pp, acc, yo, ny, nx, gx * gy)
     parts = lax.all_to_all(gram, ("gx", "gy"), 0, 0, tiled=True)
-    new_iterates, new_residual = update(parts, pc, qc, pd, qd, ext[0], rd, ext[-1], held)
+    edges = (p0, q0, r0, p1, q1, r1)
+    new_iterates, new_residual = update(parts, pc, qc, edges, ext[0], ext[-1], held)
     return new_iterates.reshape(iterates.shape), new_residual.reshape(source.shape)
 
 

time: 50.7 us -> 49.6 us (0.978)
  Pallas kernels: 28.5 us -> 27.6 us
    pallas_call x1, Pallas kernels: 5.45 us -> 4.4 us  [clean_second(): pl.pallas_call(functools.partial(clean_second_kernel, ny, nx), in_specs=v...]
    pallas_call x1, Pallas kernels: 2.27 us -> 3.31 us  [clean_first(): pl.pallas_call(functools.partial(clean_first_kernel, ny, nx), in_specs=vm...]
    pallas_call x2 -> x3, Pallas kernels: 12.6 us -> 11.7 us  [the longest x1 7.34 us: update(): pl.pallas_call(update_kernel, in_specs=vmem(12), out_specs=hbm(2), out_sh...]
  transfers between devices with their start and end apart: 4 -> 4, of which waited for: 0 -> 0; matrix products, arithmetic and copies ran while one was open for 0% -> 0% of each run, Pallas kernels for 24% -> 29%
where the time goes in v6:
time: 49.6 us; the launch traced here: 49.3 us
  Pallas kernels  27.6 us (56%)
  blocking collectives  16.4 us (33%)
  starting transfers between devices  4.45 us (9%)
  between operations  0.72 us (1%)
    all_to_all x1, blocking collectives, shards(): parts = lax.all_to_all(gram, ('gx', 'gy'), 0, 0, tiled=True)  16.4 us
    pallas_call x1, Pallas kernels, update(): pl.pallas_call(update_kernel, in_specs=vmem(12), out_specs=hbm(2), out_sh...  7.34 us
    pallas_call x1, Pallas kernels, load(): pl.pallas_call(load_kernel, in_specs=hbm(7), out_specs=vmem(8), out_shape...  4.61 us
    pallas_call x1, Pallas kernels, clean_second(): pl.pallas_call(functools.partial(clean_second_kernel, ny, nx), in_specs=v...  4.4 us
    pallas_call x2, Pallas kernels, edge_powers(): pl.pallas_call(functools.partial(edge_kernel, ny, nx, phase, devices), in...  4.38 us
    pallas_call x1, Pallas kernels, clean_first(): pl.pallas_call(functools.partial(clean_first_kernel, ny, nx), in_specs=vm...  3.31 us
    ppermute x1, starting transfers between devices, shards(): ye = lax.ppermute(ye, 'gy', even_pairs(gy))  2.57 us
    pallas_call x1, Pallas kernels, partial_residual(): pl.pallas_call(functools.partial(partial_kernel, gx, gy), in_specs=vmem(9...  1.86 us
  transfers between devices with their start and end apart: 4, of which 0 were waited for; matrix products, arithmetic and copies ran while one was open for 0% of the time, Pallas kernels for 29%

profile of v6, /device:TPU:0, one launch (start us, length us, event | category | flops | bytes accessed | tf_op | source)
XLA Modules:
  0.0 49.3 jit_solution(12826016156709660361)
XLA Ops:
  0.6 1.7 %x_edges.1 = (f32[2,16,8,128]{3,2,1,0:T(8,128)S(1)}, f32[2,16,8,128]{3,2,1,0:T(8,128)S(1)}) custom-call(f32[8,64,16,128]{3,2,1,0:T(8,128)} %it_hbm.3, f32[64,16,128]{2,1,0:T(8,128)} %src_hbm.3, f32[64,16,128]{2,1,0:T(8,128)} %dg_hbm.3, f32[64,16,128]{2,1,0:T(8,128)} %fx_hbm.3, f32[64,16,128]{2,1,0:T(8,128)} %fy_hbm.3, f32[64,16,128]{2,1,0:T(8,128)} %fz_hbm.3, ...), custom_call_target="tpu_custom_call" | custom-call | tf_op jit(solution)/shard_map/x_edges/pallas_call | solution.py:127
  2.4 0.6 %collective-permute-start = (f32[2,16,8,128]{3,2,1,0:T(8,128)S(1)}, f32[2,16,8,128]{3,2,1,0:T(8,128)S(1)}, u32[]{:S(2)}, u32[]{:S(2)}) collective-permute-start(f32[2,16,8,128]{3,2,1,0:T(8,128)S(1)} %get-tuple-element.43), channel_id=1, source_target_pairs={{0,8},{8,0},{16,24},{24,16},{1,9},{9,1},{17,25},{25,17},{2,10},{10... | collective-permute-start | bytes 393224 | tf_op jit(solution)/shard_map/ppermute | solution.py:831
  2.9 0.7 %collective-permute-start.1 = (f32[2,16,8,128]{3,2,1,0:T(8,128)S(1)}, f32[2,16,8,128]{3,2,1,0:T(8,128)S(1)}, u32[]{:S(2)}, u32[]{:S(2)}) collective-permute-start(f32[2,16,8,128]{3,2,1,0:T(8,128)S(1)} %get-tuple-element.44), channel_id=1, source_target_pairs={{8,16},{16,8},{9,17},{17,9},{10,18},{18,10},{11,19},{19,11},{12,20... | collective-permute-start | bytes 393224 | tf_op jit(solution)/shard_map/ppermute | solution.py:830
  3.6 4.6 %load.1 = (f32[16,64,128]{2,1,0:T(8,128)S(1)}, f32[16,64,128]{2,1,0:T(8,128)S(1)}, f32[16,64,128]{2,1,0:T(8,128)S(1)}, f32[16,64,128]{2,1,0:T(8,128)S(1)}, f32[1...) custom-call(f32[8,64,16,128]{3,2,1,0:T(8,128)} %it_hbm.3, ...), custom_call_target="tpu_custom_call" | custom-call | flops 2000000 | bytes 16000000 | tf_op jit(solution)/shard_map/load/pallas_call | solution.py:196
  8.2 0.0 collective-permute-done.xe_ref
  8.2 0.0 collective-permute-done.1.xo_ref
  8.2 1.9 %partial_residual.1 = (f32[1280,128]{1,0:T(8,128)S(1)}, f32[1280,128]{1,0:T(8,128)S(1)}, f32[1280,128]{1,0:T(8,128)S(1)}, f32[1280,128]{1,0:T(8,128)S(1)}, f32[1...) custom-call(f32[16,64,128]{2,1,0:T(8,128)S(1)} %get-tuple-element.36.s_in, ...), custom_call_target="tpu_custom_call" | custom-call | tf_op jit(solution)/shard_map/partial_residual/pallas_call | solution.py:330
  10.1 2.6 %collective-permute-start.2 = (f32[488,128]{1,0:T(8,128)S(1)}, f32[488,128]{1,0:T(8,128)S(1)}, u32[]{:S(2)}, u32[]{:S(2)}) collective-permute-start(f32[488,128]{1,0:T(8,128)S(1)} %get-tuple-element.55), channel_id=1, source_target_pairs={{0,1},{1,0},{2,3},{3,2},{4,5},{5,4},{6,7},{7,6},{8,9},{9,8},{10,11... | collective-permute-start | bytes 749576 | tf_op jit(solution)/shard_map/ppermute | solution.py:834
  12.7 3.3 %clean_first.1 = (f32[8,960,128]{2,1,0:T(8,128)S(1)}, f32[36,8,128]{2,1,0:T(8,128)S(1)}, f32[488,128]{1,0:T(8,128)S(1)}) custom-call(f32[1280,128]{1,0:T(8,128)S(1)} %get-tuple-element.45.t_ref, f32[1280,128]{1,0:T(8,128)S(1)} %get-tuple-element.46.s_ref, f32[1280,128]{1,0:T(8,128)S(1)} %get-tuple-element.47.fx_ref, ...), custom_call_target="tpu_custom_call" | custom-call | flops 20000000 | bytes 8000000 | tf_op jit(solution)/shard_map/clean_first/pallas_call | solution.py:469
  16.0 0.7 %collective-permute-start.3 = (f32[488,128]{1,0:T(8,128)S(1)}, f32[488,128]{1,0:T(8,128)S(1)}, u32[]{:S(2)}, u32[]{:S(2)}) collective-permute-start(f32[488,128]{1,0:T(8,128)S(1)} %get-tuple-element.58), channel_id=1, source_target_pairs={{1,2},{2,1},{3,4},{4,3},{5,6},{6,5},{9,10},{10,9},{11,12},{12,11},... | collective-permute-start | bytes 749576 | tf_op jit(solution)/shard_map/ppermute | solution.py:836
  16.7 4.4 %clean_second.1 = (f32[8,640,128]{2,1,0:T(8,128)S(1)}, f32[80,8,128]{2,1,0:T(8,128)S(1)}) custom-call(f32[1280,128]{1,0:T(8,128)S(1)} %get-tuple-element.45.t_ref, f32[1280,128]{1,0:T(8,128)S(1)} %get-tuple-element.47.fx_ref, f32[1280,128]{1,0:T(8,128)S(1)} %get-tuple-element.48.fy_ref, f32[1280,128]{1,0:T(8,128)S(1)} %get-tuple-element.49.dg_ref, ...), custom_call_target="tpu_custom_call" | custom-call | flops 40000000 | bytes 12000000 | tf_op jit(solution)/shard_map/clean_second/pallas_call | solution.py:487
  21.1 0.0 collective-permute-done.2.pack
  21.1 2.0 %edge_powers_0.1 = (f32[8,480,128]{2,1,0:T(8,128)S(1)}, f32[8,192,128]{2,1,0:T(8,128)S(1)}, f32[480,128]{1,0:T(8,128)S(1)}, f32[36,8,128]{2,1,0:T(8,128)S(1)}, f32[80,8,128]{2,1,0:T(8,128)S(1)}) custom-call(f32[1280,128]{1,0:T(8,128)S(1)} %get-tuple-element.45.t_ref, f32[1280,128]{1,0:T(8,128)S(1)} %get-tuple-element.46.s_ref, ...), custom_call_target="tpu_custom_call" | custom-call | flops 20000000 | bytes 8000000 | tf_op jit(solution)/shard_map/edge_powers_0/pallas_call | solution.py:646
  23.1 0.0 collective-permute-done.3.pack
  23.1 2.4 %edge_powers_1.1 = (f32[8,480,128]{2,1,0:T(8,128)S(1)}, f32[8,192,128]{2,1,0:T(8,128)S(1)}, f32[480,128]{1,0:T(8,128)S(1)}, f32[32,2,128]{2,1,0:T(2,128)S(1)}) custom-call(f32[1280,128]{1,0:T(8,128)S(1)} %get-tuple-element.45.t_ref, f32[1280,128]{1,0:T(8,128)S(1)} %get-tuple-element.46.s_ref, f32[1280,128]{1,0:T(8,128)S(1)} %get-tuple-element.47.fx_ref, ...), custom_call_target="tpu_custom_call" | custom-call | flops 20000000 | bytes 8000000 | tf_op jit(solution)/shard_map/edge_powers_1/pallas_call | solution.py:646
  25.5 16.4 %all_to_all.5.parts_ref = f32[32,2,128]{2,1,0:T(2,128)S(1)} all-to-all(f32[32,2,128]{2,1,0:T(2,128)S(1)} %get-tuple-element.59), channel_id=1, replica_groups=mesh['gx'=4,'gy'=8] {'gx','gy'}, dimensions={0} | all-to-all | bytes 65536 | tf_op jit(solution)/shard_map/all_to_all | solution.py:840
  41.9 7.3 %update.1 = (f32[8,1024,128]{2,1,0:T(8,128)}, f32[1024,128]{1,0:T(8,128)}) custom-call(f32[32,2,128]{2,1,0:T(2,128)S(1)} %all_to_all.5.parts_ref, f32[8,960,128]{2,1,0:T(8,128)S(1)} %get-tuple-element.52.p_out.pc_ref, f32[8,640,128]{2,1,0:T(8,128)S(1)} %get-tuple-element.60.qc_ref, f32[8,480,128]{2,1,0:T(8,128)S(1)} %get-tuple-element.61.p0_ref, ...), custom_call_target="tpu_custom_call" | custom-call | tf_op jit(solution)/shard_map/update/pallas_call | solution.py:806
Async XLA Ops:
  2.4 5.8 %collective-permute-start = (f32[2,16,8,128]{3,2,1,0:T(8,128)S(1)}, f32[2,16,8,128]{3,2,1,0:T(8,128)S(1)}, u32[]{:S(2)}, u32[]{:S(2)}) collective-permute-start(f32[2,16,8,128]{3,2,1,0:T(8,128)S(1)} %get-tuple-element.43), channel_id=1, source_target_pairs={{0,8},{8,0},{16,24},{24,16},{1,9},{9,1},{17,25},{25,17},{2,10},{10... | collective-permute-start | bytes 393224 | tf_op jit(solution)/shard_map/ppermute | solution.py:831
  2.9 5.3 %collective-permute-start.1 = (f32[2,16,8,128]{3,2,1,0:T(8,128)S(1)}, f32[2,16,8,128]{3,2,1,0:T(8,128)S(1)}, u32[]{:S(2)}, u32[]{:S(2)}) collective-permute-start(f32[2,16,8,128]{3,2,1,0:T(8,128)S(1)} %get-tuple-element.44), channel_id=1, source_target_pairs={{8,16},{16,8},{9,17},{17,9},{10,18},{18,10},{11,19},{19,11},{12,20... | collective-permute-start | bytes 393224 | tf_op jit(solution)/shard_map/ppermute | solution.py:830
  10.1 11.0 %collective-permute-start.2 = (f32[488,128]{1,0:T(8,128)S(1)}, f32[488,128]{1,0:T(8,128)S(1)}, u32[]{:S(2)}, u32[]{:S(2)}) collective-permute-start(f32[488,128]{1,0:T(8,128)S(1)} %get-tuple-element.55), channel_id=1, source_target_pairs={{0,1},{1,0},{2,3},{3,2},{4,5},{5,4},{6,7},{7,6},{8,9},{9,8},{10,11... | collective-permute-start | bytes 749576 | tf_op jit(solution)/shard_map/ppermute | solution.py:834
  16.0 7.1 %collective-permute-start.3 = (f32[488,128]{1,0:T(8,128)S(1)}, f32[488,128]{1,0:T(8,128)S(1)}, u32[]{:S(2)}, u32[]{:S(2)}) collective-permute-start(f32[488,128]{1,0:T(8,128)S(1)} %get-tuple-element.58), channel_id=1, source_target_pairs={{1,2},{2,1},{3,4},{4,3},{5,6},{6,5},{9,10},{10,9},{11,12},{12,11},... | collective-permute-start | bytes 749576 | tf_op jit(solution)/shard_map/ppermute | solution.py:836

commit v7 on v6

--- a/solution.py
+++ b/solution.py
@@ -142,28 +142,95 @@
     )(*arrays)
 
 
+def partial_layers(ny, pitch, rows, t, s, src_at, dg, fx, fy, fz):
+    nz = t.shape[-1]
+
+    def layer(y, down=True, up=True):
+        base = y * pitch
+        for r in rows:
+            at = base + r
+            here = eight(at)
+            value, face, fzs = s[here], fx[here], fz[here]
+            last = -1 if r == 0 else (1 if r == pitch - 8 else 0)
+            total = dg[here] * value - face * edge_near(s, at, 1, last)
+            total = total - edge_near(fx, at, -1, last) * edge_near(s, at, -1, last)
+            if up:
+                total = total - fy[here] * s[eight(at + pitch)]
+            if down:
+                total = total - fy[eight(at - pitch)] * s[eight(at - pitch)]
+            total = total - fzs * pltpu.roll(value, nz - 1, 1) - pltpu.roll(fzs * value, 1, 1)
+            t[here] = src_at(y, r) - total
+
+    layer(0, down=False)
+    layer(ny - 1, up=False)
+    loop(ny - 2, lambda i: layer(i + 1))
+
+
+def inside_rows(nx):
+    return range(PAD + 8, PAD + nx - 8, 8)
+
+
+def deep_rows(nx):
+    return range(PAD + 16, PAD + nx - 16, 8)
+
+
+def first_power(ny, pitch, rows, p_out, t, fx, fy, dg, fz, lb):
+    def layer(i):
+        base = (i + 2) * pitch
+        for r in rows:
+            at = base + r
+            last = -1 if r == 0 else (1 if r == pitch - 8 else 0)
+            here, below, above = eight(at), eight(at - pitch), eight(at + pitch)
+            value = t[here]
+            parts = [
+                ((dg[here] - SHIFT) * value - along_z(fz[here], value), lb[here]),
+                (-fx[here] * edge_near(t, at, 1, last), edge_near(lb, at, 1, last)),
+                (-edge_near(fx, at, -1, last) * edge_near(t, at, -1, last), edge_near(lb, at, -1, last)),
+                (-fy[here] * t[above], lb[above]),
+                (-fy[below] * t[below], lb[below]),
+            ]
+            for j, values in enumerate(spread(parts)):
+                p_out[j, eight(i * pitch + r)] = values
+
+    loop(ny - 4, layer)
+
+
 def load_kernel(
-    it_hbm, src_hbm, dg_hbm, fx_hbm, fy_hbm, fz_hbm, label_hbm,
-    s_out, src_out, dg_out, fx_out, fy_out, fz_out, lb_out, work,
-    label_ref, sem_it, sem_field, sem_label,
+    gx, gy,
+    it_ref, src_in, dg_in, fx_in, fy_in, fz_in, label_hbm,
+    t_out, s_out, fx_out, fy_out, dg_out, fz_out, lb_out, src_out, p_out,
+    label_ref, sem_label,
 ):
-    ny, nx, nz = s_out.shape
-    pairs = list(zip((src_hbm, dg_hbm, fx_hbm, fy_hbm, fz_hbm), (src_out, dg_out, fx_out, fy_out, fz_out)))
+    _, nx, ny, nz = it_ref.shape
+    pitch = nx + 2 * PAD
     label_copy = pltpu.make_async_copy(label_hbm, label_ref, sem_label)
-
-    def copy_it(y):
-        return pltpu.make_async_copy(it_hbm.at[:, :, y], work.at[:, y], sem_it.at[y])
-
-    def copy_field(f, y):
-        return pltpu.make_async_copy(pairs[f][0].at[:, y], pairs[f][1].at[y], sem_field.at[f, y])
-
-    def start(y):
-        copy_it(y).start()
-        for f in range(len(pairs)):
-            copy_field(f, y).start()
-
     label_copy.start()
-    loop(ny, start)
+
+    last_x = lax.axis_index("gx") == gx - 1
+    last_y = lax.axis_index("gy") == gy - 1
+    top = jnp.logical_and(last_y, iota((8, nz), 0) == 7)
+    end = iota((8, nz), 1) == nz - 1
+
+    def add(c):
+        for x in range(8):
+            for y in range(0, ny, 8):
+                place = pl.ds(y * pitch + PAD + c * 8 + x, 8, stride=pitch)
+                at = (c * 8 + x, slice(y, y + 8))
+                total = it_ref[(0,) + at]
+                for j in range(1, ENLARGE):
+                    total = total + it_ref[(j,) + at]
+                s_out[place, :] = total
+                src_out[place, :] = src_in[at]
+                dg_out[place, :] = dg_in[at]
+                face = fx_in[at]
+                if x == 7:
+                    face = jnp.where(jnp.logical_and(last_x, c == nx // 8 - 1), 0.0, face)
+                fx_out[place, :] = face
+                face = fy_in[at]
+                fy_out[place, :] = jnp.where(top, 0.0, face) if y == ny - 8 else face
+                fz_out[place, :] = jnp.where(end, 0.0, fz_in[at])
+
+    loop(nx // 8, add)
     label_copy.wait()
 
     spot = iota((nx, nx), 0) == iota((nx, nx), 1)
@@ -171,43 +238,28 @@
     labels = label_ref[...].astype(F32)
     for y in range(ny):
         row = jnp.where(spot, labels[y : y + 1], 0.0).astype(jnp.bfloat16)
-        lb_out[y] = jnp.dot(row, ones, preferred_element_type=F32)
-
-    def add(y):
-        copy_it(y).wait()
-        for r in range(0, nx, 8):
-            total = work[0, y, r : r + 8]
-            for j in range(1, ENLARGE):
-                total = total + work[j, y, r : r + 8]
-            s_out[y, r : r + 8] = total
-
-    loop(ny, add)
-
-    def finish(y):
-        for f in range(len(pairs)):
-            copy_field(f, y).wait()
-
-    loop(ny, finish)
-
-
-def load(arrays):
+        lb_out[y * pitch + PAD : y * pitch + PAD + nx] = jnp.dot(row, ones, preferred_element_type=F32)
+
+    src_at = lambda y, r: src_out[eight(y * pitch + r)]
+    partial_layers(ny, pitch, inside_rows(nx), t_out, s_out, src_at, dg_out, fx_out, fy_out, fz_out)
+    first_power(ny, pitch, deep_rows(nx), p_out, t_out, fx_out, fy_out, dg_out, fz_out, lb_out)
+
+
+def load(arrays, labels, gx, gy):
     _, nx, ny, nz = arrays[0].shape
-    field = array(ny, nx, nz)
     return pl.pallas_call(
-        load_kernel,
-        in_specs=hbm(7),
-        out_specs=vmem(8),
-        out_shape=[field] * 7 + [array(ENLARGE, ny, nx, nz)],
+        functools.partial(load_kernel, gx, gy),
+        in_specs=vmem(6) + hbm(1),
+        out_specs=vmem(9),
+        out_shape=[array(ny * (nx + 2 * PAD), nz)] * 8 + [array(ENLARGE, (ny - 4) * (nx + 2 * PAD), nz)],
         scratch_shapes=[
             pltpu.VMEM((ny, nx), jnp.int32),
-            pltpu.SemaphoreType.DMA((ny,)),
-            pltpu.SemaphoreType.DMA((5, ny)),
             pltpu.SemaphoreType.DMA,
         ],
         compiler_params=params(),
-        cost_estimate=pl.CostEstimate(flops=2_000_000, bytes_accessed=16_000_000, transcendentals=0),
+        cost_estimate=pl.CostEstimate(flops=4_000_000, bytes_accessed=16_000_000, transcendentals=0),
         name="load",
-    )(*arrays)
+    )(*arrays, labels)
 
 
 def blocks_of(nx):
@@ -250,89 +302,55 @@
 
 
 def partial_kernel(
-    gx, gy,
-    s_in, src_in, dg_in, fx_in, fy_in, fz_in, lb_in, xe_ref, xo_ref,
+    gy, nx, ny,
+    t_in, s_in, fx_in, fy_in, dg_in, fz_in, lb_in, src_ref, xe_ref, xo_ref,
     t_out, s_out, fx_out, fy_out, dg_out, fz_out, lb_out, ye_ref,
-    src_ext,
+    src_ghost,
 ):
-    ny, nx, nz = s_in.shape
+    nz = t_in.shape[-1]
     pitch = nx + 2 * PAD
-    lane = iota((8, nz), 1)
+    end = iota((8, nz), 1) == nz - 1
     even_x = lax.rem(lax.axis_index("gx"), 2) == 0
-    last_x = lax.axis_index("gx") == gx - 1
     last_y = lax.axis_index("gy") == gy - 1
-    last_row = jnp.logical_and(iota((8, nz), 0) == 7, last_x)
+    roll = lambda v, n: pltpu.roll(v, n, 0)
 
     def fill(y):
         top = jnp.logical_and(last_y, y == ny - 1)
-        fy_of = lambda v: jnp.where(top, 0.0, v)
-        fz_of = lambda v: jnp.where(lane == nz - 1, 0.0, v)
-        base = y * pitch
-        roll = lambda v, n: pltpu.roll(v, n, 0)
         for at, is_low in ((0, True), (PAD + nx, False)):
             one, two = [
                 jnp.where(even_x == is_low, xo_ref[part, y], xe_ref[part, y]) for part in range(2)
             ]
-            here = eight(base + at)
+            here = eight(y * pitch + at)
             s_out[here] = one
             fx_out[here] = roll(one, 3 if is_low else 5)
             lb_out[here] = roll(one, 6 if is_low else 2)
-            src_ext[here] = two
+            src_ghost[0 if is_low else 1, y] = two
             dg_out[here] = roll(two, 6)
-            fy_out[here] = fy_of(roll(two, 4))
-            fz_out[here] = fz_of(roll(two, 2))
-        for r in range(0, nx, 8):
-            here = eight(base + PAD + r)
-            span = slice(r, r + 8)
-            s_out[here] = s_in[y, span]
-            face = fx_in[y, span]
-            fx_out[here] = jnp.where(last_row, 0.0, face) if r == nx - 8 else face
-            lb_out[here] = lb_in[y, span]
-            src_ext[here] = src_in[y, span]
-            dg_out[here] = dg_in[y, span]
-            fy_out[here] = fy_of(fy_in[y, span])
-            fz_out[here] = fz_of(fz_in[y, span])
-
-    loop(ny, fill)
-
-    def layer(y, down=True, up=True):
-        base = y * pitch
-        for r in range(0, pitch, 8):
-            at = base + r
-            here = eight(at)
-            s, fx, fz = s_out[here], fx_out[here], fz_out[here]
-            if r == 0:
-                sm, fxm = pltpu.roll(s, 1, 0), pltpu.roll(fx, 1, 0)
-            else:
-                sm, fxm = s_out[near(at - 1)], fx_out[near(at - 1)]
-            sp = pltpu.roll(s, 7, 0) if r == pitch - 8 else s_out[near(at + 1)]
-            total = dg_out[here] * s - fx * sp - fxm * sm
-            if up:
-                total = total - fy_out[here] * s_out[eight(at + pitch)]
-            if down:
-                total = total - fy_out[eight(at - pitch)] * s_out[eight(at - pitch)]
-            total = total - fz * pltpu.roll(s, nz - 1, 1) - pltpu.roll(fz * s, 1, 1)
-            t_out[here] = src_ext[here] - total
-
-    layer(0, down=False)
-    layer(ny - 1, up=False)
-    loop(ny - 2, lambda i: layer(i + 1))
-
+            fy_out[here] = jnp.where(top, 0.0, roll(two, 4))
+            fz_out[here] = jnp.where(end, 0.0, roll(two, 2))
+
+    loop(ny, fill, unroll=2)
+
+    def src_at(y, r):
+        if r == 0 or r == pitch - 8:
+            return src_ghost[0 if r == 0 else 1, y]
+        return src_ref[eight(y * pitch + r)]
+
+    rows = [r for r in range(0, pitch, 8) if r not in inside_rows(nx)]
+    partial_layers(ny, pitch, rows, t_out, s_out, src_at, dg_out, fx_out, fy_out, fz_out)
     even_y = lax.rem(lax.axis_index("gy"), 2) == 0
     pack_y_edge(ny, nx, ye_ref, even_y, t_out, s_out, fy_out, fx_out, dg_out, fz_out, lb_out)
 
 
-def partial_residual(fields, xe, xo, gx, gy):
-    ny, nx, nz = fields[0].shape
-    rows = ny * (nx + 2 * PAD)
-    ext = array(rows, nz)
-    pack = array(blocks_of(nx)[1][-1], nz)
+def partial_residual(fields, xe, xo, gy, nx, ny):
+    nz = xe.shape[-1]
     return pl.pallas_call(
-        functools.partial(partial_kernel, gx, gy),
-        in_specs=vmem(9),
+        functools.partial(partial_kernel, gy, nx, ny),
+        in_specs=vmem(10),
         out_specs=vmem(8),
-        out_shape=[ext] * 7 + [pack],
-        scratch_shapes=[pltpu.VMEM((rows, nz), F32)],
+        out_shape=[array(*a.shape) for a in fields[:7]] + [array(blocks_of(nx)[1][-1], nz)],
+        input_output_aliases={i: i for i in range(7)},
+        scratch_shapes=[pltpu.VMEM((2, ny, 8, nz), F32)],
         compiler_params=params(),
         name="partial_residual",
     )(*fields, xe, xo)
@@ -377,31 +395,14 @@
 
 def clean_first_kernel(
     ny, nx,
-    t_ref, s_ref, fx_ref, fy_ref, dg_ref, fz_ref, lb_ref,
+    t_ref, s_ref, fx_ref, fy_ref, dg_ref, fz_ref, lb_ref, p_in,
     p_out, acc_out, yo_ref,
 ):
     nz = t_ref.shape[-1]
     pitch = nx + 2 * PAD
 
-    def first(i):
-        layer = (i + 2) * pitch
-        for r in range(0, pitch, 8):
-            at = layer + r
-            last = -1 if r == 0 else (1 if r == pitch - 8 else 0)
-            here = eight(at)
-            value = t_ref[here]
-            below, above = eight(at - pitch), eight(at + pitch)
-            parts = [
-                ((dg_ref[here] - SHIFT) * value - along_z(fz_ref[here], value), lb_ref[here]),
-                (-fx_ref[here] * edge_near(t_ref, at, 1, last), edge_near(lb_ref, at, 1, last)),
-                (-edge_near(fx_ref, at, -1, last) * edge_near(t_ref, at, -1, last), edge_near(lb_ref, at, -1, last)),
-                (-fy_ref[here] * t_ref[above], lb_ref[above]),
-                (-fy_ref[below] * t_ref[below], lb_ref[below]),
-            ]
-            for j, values in enumerate(spread(parts)):
-                p_out[j, eight(i * pitch + r)] = values
-
-    loop(ny - 4, first)
+    rows = [r for r in range(0, pitch, 8) if r not in deep_rows(nx)]
+    first_power(ny, pitch, rows, p_out, t_ref, fx_ref, fy_ref, dg_ref, fz_ref, lb_ref)
 
     def p_dots(i, sums):
         for r in range(PAD, PAD + nx, 8):
@@ -464,21 +465,22 @@
             slot += 1
 
 
-def clean_first(ext, ny, nx):
+def clean_first(ext, inner, ny, nx):
     nz = ext[0].shape[-1]
     return pl.pallas_call(
         functools.partial(clean_first_kernel, ny, nx),
-        in_specs=vmem(7),
+        in_specs=vmem(8),
         out_specs=vmem(3),
         out_shape=[
             array(ENLARGE, (ny - 4) * (nx + 2 * PAD), nz),
             array(len(PAIRS), 8, nz),
             array(blocks_of(nx)[1][-1], nz),
         ],
+        input_output_aliases={7: 0},
         compiler_params=params(),
         cost_estimate=pl.CostEstimate(flops=20_000_000, bytes_accessed=8_000_000, transcendentals=0),
         name="clean_first",
-    )(*ext)
+    )(*ext, inner)
 
 
 def clean_second(ext, pc, ny, nx):
@@ -686,15 +688,20 @@
 
 
 def update_kernel(
-    parts_ref, pc_ref, qc_ref, p0_ref, q0_ref, r0_ref, p1_ref, q1_ref, r1_ref, t_ref, lb_ref, it_ref,
-    it_out, r_out,
-    table, weights, onehot, own, work, r_work, sem_out, sem_r,
+    parts_ref, pc_ref, qc_ref, p0_ref, q0_ref, r0_ref, p1_ref, q1_ref, r1_ref, t_ref, lb_ref, it_hbm,
+    it_out, r_out, it_ref,
+    table, weights, onehot, own, work, r_work, sem_in, sem_out, sem_r,
 ):
     _, ny, nx, nz = it_ref.shape
     pitch = nx + 2 * PAD
     two = 2 * ENLARGE
     square = ENLARGE * ENLARGE
     chunks = nx // 8
+
+    def copy_in(y):
+        return pltpu.make_async_copy(it_hbm.at[:, :, y], it_ref.at[:, y], sem_in.at[y])
+
+    loop(ny, lambda y: copy_in(y).start())
 
     def copy_out(half, c):
         span, rows = pl.ds(half * 4, 4), pl.ds(pl.multiple_of(c * 8 * ny, 8 * ny), 8 * ny)
@@ -792,35 +799,38 @@
 
         loop(chunks, block)
 
+    residuals()
+    loop(ny, lambda y: copy_in(y).wait())
     updates(0)
     updates(1)
-    residuals()
     for half in range(2):
         loop(chunks, lambda c, half=half: copy_out(half, c).wait())
     loop(chunks, lambda c: copy_r(c).wait())
 
 
-def update(parts, pc, qc, edges, t, labels, held):
-    _, ny, nx, nz = held.shape
+def update(parts, pc, qc, edges, t, labels, iterates):
+    _, nx, ny, nz = iterates.shape
     rows = nx * ny
     return pl.pallas_call(
         update_kernel,
-        in_specs=vmem(12),
+        in_specs=vmem(11) + hbm(1),
         out_specs=hbm(2),
         out_shape=[array(ENLARGE, rows, nz), array(rows, nz)],
         scratch_shapes=[
+            pltpu.VMEM((ENLARGE, ny, nx, nz), F32),
             pltpu.VMEM((ENLARGE * ENLARGE + 2 * ENLARGE, 8, nz), F32),
             pltpu.VMEM((nz, (ENLARGE + 1) * nz), F32),
             pltpu.VMEM((rows, nz), jnp.bfloat16),
             pltpu.VMEM((rows, (ENLARGE + 1) * nz), F32),
             pltpu.VMEM((ENLARGE, rows, nz), F32),
             pltpu.VMEM((rows, nz), F32),
+            pltpu.SemaphoreType.DMA((ny,)),
             pltpu.SemaphoreType.DMA((2, nx // 8)),
             pltpu.SemaphoreType.DMA((nx // 8,)),
         ],
         compiler_params=params(),
         name="update",
-    )(parts, pc, qc, *edges, t, labels, held)
+    )(parts, pc, qc, *edges, t, labels, iterates)
 
 
 def shards(gx, gy, source, diagonal, face_x, face_y, face_z, iterates, labels):
@@ -829,17 +839,18 @@
     xe, xo = x_edges(arrays)
     xo = lax.ppermute(xo, "gx", odd_pairs(gx))
     xe = lax.ppermute(xe, "gx", even_pairs(gx))
-    *fields, held = load(arrays)
-    *ext, ye = partial_residual(fields, xe, xo, gx, gy)
+    direct = [iterates, source, diagonal, face_x, face_y, face_z]
+    *fields, inner = load(direct, arrays[6], gx, gy)
+    *ext, ye = partial_residual(fields, xe, xo, gy, nx, ny)
     ye = lax.ppermute(ye, "gy", even_pairs(gy))
-    pc, acc_pp, yo = clean_first(ext, ny, nx)
+    pc, acc_pp, yo = clean_first(ext, inner, ny, nx)
     yo = lax.ppermute(yo, "gy", odd_pairs(gy))
     qc, acc = clean_second(ext, pc, ny, nx)
     p0, q0, r0, acc_pp, acc = edge_powers(0, ext, pc, acc_pp, acc, ye, ny, nx, gx * gy)
     p1, q1, r1, gram = edge_powers(1, ext, pc, acc_pp, acc, yo, ny, nx, gx * gy)
     parts = lax.all_to_all(gram, ("gx", "gy"), 0, 0, tiled=True)
     edges = (p0, q0, r0, p1, q1, r1)
-    new_iterates, new_residual = update(parts, pc, qc, edges, ext[0], ext[-1], held)
+    new_iterates, new_residual = update(parts, pc, qc, edges, ext[0], ext[-1], arrays[0])
     return new_iterates.reshape(iterates.shape), new_residual.reshape(source.shape)
 
 

time: 49.6 us -> 48 us (0.968)
  Pallas kernels: 27.6 us -> 26 us
  blocking collectives: 16.4 us -> 15.9 us
    pallas_call x3, Pallas kernels: 13.8 us -> 12.9 us  [the longest x1 7.7 us: update(): pl.pallas_call(update_kernel, in_specs=vmem(11) + hbm(1), out_specs=hbm(2...]
    pallas_call x1, Pallas kernels: 3.31 us -> 2.5 us  [clean_first(): pl.pallas_call(functools.partial(clean_first_kernel, ny, nx), in_specs=vm...]
    all_to_all x1, blocking collectives: 16.4 us -> 15.9 us  [shards(): parts = lax.all_to_all(gram, ('gx', 'gy'), 0, 0, tiled=True)]
  transfers between devices with their start and end apart: 4 -> 4, of which waited for: 0 -> 0; matrix products, arithmetic and copies ran while one was open for 0% -> 0% of each run, Pallas kernels for 29% -> 27%
where the time goes in v7:
time: 48 us; the launch traced here: 47.8 us
  Pallas kernels  26 us (54%)
  blocking collectives  15.9 us (33%)
  starting transfers between devices  4.92 us (10%)
  between operations  0.81 us (2%)
    all_to_all x1, blocking collectives, shards(): parts = lax.all_to_all(gram, ('gx', 'gy'), 0, 0, tiled=True)  15.9 us
    pallas_call x1, Pallas kernels, update(): pl.pallas_call(update_kernel, in_specs=vmem(11) + hbm(1), out_specs=hbm(2...  7.7 us
    pallas_call x1, Pallas kernels, clean_second(): pl.pallas_call(functools.partial(clean_second_kernel, ny, nx), in_specs=v...  4.43 us
    pallas_call x2, Pallas kernels, edge_powers(): pl.pallas_call(functools.partial(edge_kernel, ny, nx, phase, devices), in...  4.35 us
    pallas_call x1, Pallas kernels, load(): pl.pallas_call(functools.partial(load_kernel, gx, gy), in_specs=vmem(6) +...  3.85 us
    ppermute x1, starting transfers between devices, shards(): ye = lax.ppermute(ye, 'gy', even_pairs(gy))  3.03 us
    pallas_call x1, Pallas kernels, clean_first(): pl.pallas_call(functools.partial(clean_first_kernel, ny, nx), in_specs=vm...  2.5 us
    pallas_call x1, Pallas kernels, x_edges(): pl.pallas_call(edges_kernel, in_specs=hbm(7), out_specs=vmem(2), out_shap...  1.8 us
  transfers between devices with their start and end apart: 4, of which 0 were waited for; matrix products, arithmetic and copies ran while one was open for 0% of the time, Pallas kernels for 27%

profile of v7, /device:TPU:0, one launch (start us, length us, event | category | flops | bytes accessed | tf_op | source)
XLA Modules:
  0.0 47.8 jit_solution(5434806375103283736)
XLA Ops:
  0.6 0.0 copy-start
  0.6 0.0 copy-start.5
  0.7 0.0 copy-start.4
  0.7 0.0 copy-start.3
  0.7 0.0 copy-start.2
  0.7 0.0 copy-start.1
  0.7 1.8 %x_edges.1 = (f32[2,16,8,128]{3,2,1,0:T(8,128)S(1)}, f32[2,16,8,128]{3,2,1,0:T(8,128)S(1)}) custom-call(f32[8,64,16,128]{3,2,1,0:T(8,128)} %it_hbm.3, f32[64,16,128]{2,1,0:T(8,128)} %src_hbm.1, f32[64,16,128]{2,1,0:T(8,128)} %dg_hbm.1, f32[64,16,128]{2,1,0:T(8,128)} %fx_hbm.1, f32[64,16,128]{2,1,0:T(8,128)} %fy_hbm.1, f32[64,16,128]{2,1,0:T(8,128)} %fz_hbm.1, ...), custom_call_target="tpu_custom_call" | custom-call | tf_op jit(solution)/shard_map/x_edges/pallas_call | solution.py:127
  2.5 0.6 %collective-permute-start = (f32[2,16,8,128]{3,2,1,0:T(8,128)S(1)}, f32[2,16,8,128]{3,2,1,0:T(8,128)S(1)}, u32[]{:S(2)}, u32[]{:S(2)}) collective-permute-start(f32[2,16,8,128]{3,2,1,0:T(8,128)S(1)} %get-tuple-element.45), channel_id=1, source_target_pairs={{0,8},{8,0},{16,24},{24,16},{1,9},{9,1},{17,25},{25,17},{2,10},{10... | collective-permute-start | bytes 393224 | tf_op jit(solution)/shard_map/ppermute | solution.py:841
  3.1 0.7 %collective-permute-start.1 = (f32[2,16,8,128]{3,2,1,0:T(8,128)S(1)}, f32[2,16,8,128]{3,2,1,0:T(8,128)S(1)}, u32[]{:S(2)}, u32[]{:S(2)}) collective-permute-start(f32[2,16,8,128]{3,2,1,0:T(8,128)S(1)} %get-tuple-element.46), channel_id=1, source_target_pairs={{8,16},{16,8},{9,17},{17,9},{10,18},{18,10},{11,19},{19,11},{12,20... | collective-permute-start | bytes 393224 | tf_op jit(solution)/shard_map/ppermute | solution.py:840
  3.8 0.1 copy-done.1
  3.9 3.9 %load.1 = (f32[1280,128]{1,0:T(8,128)S(1)}, f32[1280,128]{1,0:T(8,128)S(1)}, f32[1280,128]{1,0:T(8,128)S(1)}, f32[1280,128]{1,0:T(8,128)S(1)}, f32[1280,128]{1,0...) custom-call(f32[8,64,16,128]{3,2,1,0:T(8,128)S(1)} %copy-done, ...), custom_call_target="tpu_custom_call" | custom-call | flops 4000000 | bytes 16000000 | tf_op jit(solution)/shard_map/load/pallas_call | solution.py:250
  7.7 0.0 collective-permute-done.xe_ref
  7.7 0.0 collective-permute-done.1.xo_ref
  7.7 1.4 %partial_residual.1 = (f32[1280,128]{1,0:T(8,128)S(1)}, f32[1280,128]{1,0:T(8,128)S(1)}, f32[1280,128]{1,0:T(8,128)S(1)}, f32[1280,128]{1,0:T(8,128)S(1)}, f32[1...) custom-call(f32[1280,128]{1,0:T(8,128)S(1)} %get-tuple-element.37.t_, ...), custom_call_target="tpu_custom_call", output_to_operand_aliasing={{0}: (0, {}), {1}: (1, {}), {2}: (2, {}), {3}: (3, {}), {4}... | custom-call | tf_op jit(solution)/shard_map/partial_residual/pallas_call | solution.py:347
  9.1 3.0 %collective-permute-start.2 = (f32[488,128]{1,0:T(8,128)S(1)}, f32[488,128]{1,0:T(8,128)S(1)}, u32[]{:S(2)}, u32[]{:S(2)}) collective-permute-start(f32[488,128]{1,0:T(8,128)S(1)} %get-tuple-element.58), channel_id=1, source_target_pairs={{0,1},{1,0},{2,3},{3,2},{4,5},{5,4},{6,7},{7,6},{8,9},{9,8},{10,11... | collective-permute-start | bytes 749576 | tf_op jit(solution)/shard_map/ppermute | solution.py:845
  12.2 2.5 %clean_first.1 = (f32[8,960,128]{2,1,0:T(8,128)S(1)}, f32[36,8,128]{2,1,0:T(8,128)S(1)}, f32[488,128]{1,0:T(8,128)S(1)}) custom-call(f32[1280,128]{1,0:T(8,128)S(1)} %get-tuple-element.47.t_ref, f32[1280,128]{1,0:T(8,128)S(1)} %get-tuple-element.48.s_ref, f32[1280,128]{1,0:T(8,128)S(1)} %get-tuple-element.49.fx_ref, ...), custom_call_target="tpu_custom_call", output_to_operand_aliasing={{0}: (7, {})} | custom-call | flops 20000000 | bytes 8000000 | tf_op jit(solution)/shard_map/clean_first/pallas_call | solution.py:470
  14.7 0.7 %collective-permute-start.3 = (f32[488,128]{1,0:T(8,128)S(1)}, f32[488,128]{1,0:T(8,128)S(1)}, u32[]{:S(2)}, u32[]{:S(2)}) collective-permute-start(f32[488,128]{1,0:T(8,128)S(1)} %get-tuple-element.61), channel_id=1, source_target_pairs={{1,2},{2,1},{3,4},{4,3},{5,6},{6,5},{9,10},{10,9},{11,12},{12,11},... | collective-permute-start | bytes 749576 | tf_op jit(solution)/shard_map/ppermute | solution.py:847
  15.3 4.4 %clean_second.1 = (f32[8,640,128]{2,1,0:T(8,128)S(1)}, f32[80,8,128]{2,1,0:T(8,128)S(1)}) custom-call(f32[1280,128]{1,0:T(8,128)S(1)} %get-tuple-element.47.t_ref, f32[1280,128]{1,0:T(8,128)S(1)} %get-tuple-element.49.fx_ref, f32[1280,128]{1,0:T(8,128)S(1)} %get-tuple-element.50.fy_ref, f32[1280,128]{1,0:T(8,128)S(1)} %get-tuple-element.51.dg_ref, ...), custom_call_target="tpu_custom_call" | custom-call | flops 40000000 | bytes 12000000 | tf_op jit(solution)/shard_map/clean_second/pallas_call | solution.py:489
  19.8 0.0 collective-permute-done.2.pack
  19.8 2.0 %edge_powers_0.1 = (f32[8,480,128]{2,1,0:T(8,128)S(1)}, f32[8,192,128]{2,1,0:T(8,128)S(1)}, f32[480,128]{1,0:T(8,128)S(1)}, f32[36,8,128]{2,1,0:T(8,128)S(1)}, f32[80,8,128]{2,1,0:T(8,128)S(1)}) custom-call(f32[1280,128]{1,0:T(8,128)S(1)} %get-tuple-element.47.t_ref, f32[1280,128]{1,0:T(8,128)S(1)} %get-tuple-element.48.s_ref, ...), custom_call_target="tpu_custom_call" | custom-call | flops 20000000 | bytes 8000000 | tf_op jit(solution)/shard_map/edge_powers_0/pallas_call | solution.py:648
  21.8 0.0 collective-permute-done.3.pack
  21.8 2.3 %edge_powers_1.1 = (f32[8,480,128]{2,1,0:T(8,128)S(1)}, f32[8,192,128]{2,1,0:T(8,128)S(1)}, f32[480,128]{1,0:T(8,128)S(1)}, f32[32,2,128]{2,1,0:T(2,128)S(1)}) custom-call(f32[1280,128]{1,0:T(8,128)S(1)} %get-tuple-element.47.t_ref, f32[1280,128]{1,0:T(8,128)S(1)} %get-tuple-element.48.s_ref, f32[1280,128]{1,0:T(8,128)S(1)} %get-tuple-element.49.fx_ref, ...), custom_call_target="tpu_custom_call" | custom-call | flops 20000000 | bytes 8000000 | tf_op jit(solution)/shard_map/edge_powers_1/pallas_call | solution.py:648
  24.2 15.9 %all_to_all.5.parts_ref = f32[32,2,128]{2,1,0:T(2,128)S(1)} all-to-all(f32[32,2,128]{2,1,0:T(2,128)S(1)} %get-tuple-element.62), channel_id=1, replica_groups=mesh['gx'=4,'gy'=8] {'gx','gy'}, dimensions={0} | all-to-all | bytes 65536 | tf_op jit(solution)/shard_map/all_to_all | solution.py:851
  40.1 7.7 %update.1 = (f32[8,1024,128]{2,1,0:T(8,128)}, f32[1024,128]{1,0:T(8,128)}) custom-call(f32[32,2,128]{2,1,0:T(2,128)S(1)} %all_to_all.5.parts_ref, f32[8,960,128]{2,1,0:T(8,128)S(1)} %get-tuple-element.55.p_out.pc_ref, f32[8,640,128]{2,1,0:T(8,128)S(1)} %get-tuple-element.63.qc_ref, f32[8,480,128]{2,1,0:T(8,128)S(1)} %get-tuple-element.64.p0_ref, ...), custom_call_target="tpu_custom_call" | custom-call | tf_op jit(solution)/shard_map/update/pallas_call | solution.py:814
  (5 shorter events, 0.0 us)
Async XLA Ops:
  0.6 3.1 %copy-start = (f32[8,64,16,128]{3,2,1,0:T(8,128)S(1)}, f32[8,64,16,128]{3,2,1,0:T(8,128)}, u32[]{:S(2)}) copy-start(f32[8,64,16,128]{3,2,1,0:T(8,128)} %it_hbm.3) | copy-start | bytes 12582916
  0.6 3.1 %copy-start.5 = (f32[64,16,128]{2,1,0:T(8,128)S(1)}, f32[64,16,128]{2,1,0:T(8,128)}, u32[]{:S(2)}) copy-start(f32[64,16,128]{2,1,0:T(8,128)} %fz_hbm.1) | copy-start | bytes 1572868
  0.7 3.1 %copy-start.4 = (f32[64,16,128]{2,1,0:T(8,128)S(1)}, f32[64,16,128]{2,1,0:T(8,128)}, u32[]{:S(2)}) copy-start(f32[64,16,128]{2,1,0:T(8,128)} %fy_hbm.1) | copy-start | bytes 1572868
  0.7 3.1 %copy-start.3 = (f32[64,16,128]{2,1,0:T(8,128)S(1)}, f32[64,16,128]{2,1,0:T(8,128)}, u32[]{:S(2)}) copy-start(f32[64,16,128]{2,1,0:T(8,128)} %fx_hbm.1) | copy-start | bytes 1572868
  0.7 3.1 %copy-start.2 = (f32[64,16,128]{2,1,0:T(8,128)S(1)}, f32[64,16,128]{2,1,0:T(8,128)}, u32[]{:S(2)}) copy-start(f32[64,16,128]{2,1,0:T(8,128)} %dg_hbm.1) | copy-start | bytes 1572868
  0.7 3.2 %copy-start.1 = (f32[64,16,128]{2,1,0:T(8,128)S(1)}, f32[64,16,128]{2,1,0:T(8,128)}, u32[]{:S(2)}) copy-start(f32[64,16,128]{2,1,0:T(8,128)} %src_hbm.1) | copy-start | bytes 1572868
  2.5 5.2 %collective-permute-start = (f32[2,16,8,128]{3,2,1,0:T(8,128)S(1)}, f32[2,16,8,128]{3,2,1,0:T(8,128)S(1)}, u32[]{:S(2)}, u32[]{:S(2)}) collective-permute-start(f32[2,16,8,128]{3,2,1,0:T(8,128)S(1)} %get-tuple-element.45), channel_id=1, source_target_pairs={{0,8},{8,0},{16,24},{24,16},{1,9},{9,1},{17,25},{25,17},{2,10},{10... | collective-permute-start | bytes 393224 | tf_op jit(solution)/shard_map/ppermute | solution.py:841
  3.1 4.7 %collective-permute-start.1 = (f32[2,16,8,128]{3,2,1,0:T(8,128)S(1)}, f32[2,16,8,128]{3,2,1,0:T(8,128)S(1)}, u32[]{:S(2)}, u32[]{:S(2)}) collective-permute-start(f32[2,16,8,128]{3,2,1,0:T(8,128)S(1)} %get-tuple-element.46), channel_id=1, source_target_pairs={{8,16},{16,8},{9,17},{17,9},{10,18},{18,10},{11,19},{19,11},{12,20... | collective-permute-start | bytes 393224 | tf_op jit(solution)/shard_map/ppermute | solution.py:840
  9.1 10.7 %collective-permute-start.2 = (f32[488,128]{1,0:T(8,128)S(1)}, f32[488,128]{1,0:T(8,128)S(1)}, u32[]{:S(2)}, u32[]{:S(2)}) collective-permute-start(f32[488,128]{1,0:T(8,128)S(1)} %get-tuple-element.58), channel_id=1, source_target_pairs={{0,1},{1,0},{2,3},{3,2},{4,5},{5,4},{6,7},{7,6},{8,9},{9,8},{10,11... | collective-permute-start | bytes 749576 | tf_op jit(solution)/shard_map/ppermute | solution.py:845
  14.7 7.2 %collective-permute-start.3 = (f32[488,128]{1,0:T(8,128)S(1)}, f32[488,128]{1,0:T(8,128)S(1)}, u32[]{:S(2)}, u32[]{:S(2)}) collective-permute-start(f32[488,128]{1,0:T(8,128)S(1)} %get-tuple-element.61), channel_id=1, source_target_pairs={{1,2},{2,1},{3,4},{4,3},{5,6},{6,5},{9,10},{10,9},{11,12},{12,11},... | collective-permute-start | bytes 749576 | tf_op jit(solution)/shard_map/ppermute | solution.py:847

commit v8 on v7

--- a/solution.py
+++ b/solution.py
@@ -745,24 +745,20 @@
 
     loop(ny * nx // 128, coefficients, unroll=2)
 
-    def spots(c, visit):
+    def spots(c, odd, visit):
         x = PAD + c * 8
         for i in range(ny - 6):
             visit(i + 3, pc_ref, (i + 1) * pitch + x, qc_ref, i * nx + c * 8, t_ref, (i + 3) * pitch + x)
         for phase, p_ref, q_ref, r_ref in ((0, p0_ref, q0_ref, r0_ref), (1, p1_ref, q1_ref, r1_ref)):
-            for side in range(2):
-
-                def visit_side(side=side, p_ref=p_ref, q_ref=q_ref, r_ref=r_ref):
-                    for i in range(3):
-                        at = (i + 2 - side) * pitch + x
-                        visit(i + side * (ny - 3), p_ref, at, q_ref, i * nx + c * 8, r_ref, at)
-
-                pl.when(side_of(phase) == side)(visit_side)
+            side = odd if phase else 1 - odd
+            for i in range(3):
+                at = (i + 2 - side) * pitch + x
+                visit(i + side * (ny - 3), p_ref, at, q_ref, i * nx + c * 8, r_ref, at)
 
     def place(c, y):
         return pl.ds(c * 8 * ny + y, 8, stride=ny)
 
-    def updates(half):
+    def updates(odd, half):
         js = range(half * 4, half * 4 + 4)
         scales = [[table[j * ENLARGE + k] for k in range(ENLARGE)] for j in js]
 
@@ -777,12 +773,12 @@
                 for j, t in zip(js, totals):
                     work[j, place(c, y), :] = t
 
-            spots(c, visit)
+            spots(c, odd, visit)
             copy_out(half, c).start()
 
         loop(chunks, block)
 
-    def residuals():
+    def residuals(odd):
         scales = [table[square + k] for k in range(two)]
 
         def block(c):
@@ -794,15 +790,19 @@
                     total = total - scales[ENLARGE + k] * q_ref[k, eight(q_at)]
                 r_work[place(c, y), :] = total
 
-            spots(c, visit)
+            spots(c, odd, visit)
             copy_r(c).start()
 
         loop(chunks, block)
 
-    residuals()
-    loop(ny, lambda y: copy_in(y).wait())
-    updates(0)
-    updates(1)
+    def run(odd):
+        residuals(odd)
+        loop(ny, lambda y: copy_in(y).wait())
+        updates(odd, 0)
+        updates(odd, 1)
+
+    for odd in range(2):
+        pl.when(side_of(1) == odd)(functools.partial(run, odd))
     for half in range(2):
         loop(chunks, lambda c, half=half: copy_out(half, c).wait())
     loop(chunks, lambda c: copy_r(c).wait())

time: 48 us -> 47.2 us (0.983)
  Pallas kernels: 26 us -> 25.2 us
    pallas_call x1, Pallas kernels: 7.7 us -> 6.89 us  [update(): pl.pallas_call(update_kernel, in_specs=vmem(11) + hbm(1), out_specs=hbm(2...]
where the time goes in v8:
time: 47.2 us; the launch traced here: 47 us
  Pallas kernels  25.2 us (53%)
  blocking collectives  15.9 us (34%)
  starting transfers between devices  4.92 us (10%)
  between operations  0.81 us (2%)
    all_to_all x1, blocking collectives, shards(): parts = lax.all_to_all(gram, ('gx', 'gy'), 0, 0, tiled=True)  15.9 us
    pallas_call x1, Pallas kernels, update(): pl.pallas_call(update_kernel, in_specs=vmem(11) + hbm(1), out_specs=hbm(2...  6.89 us
    pallas_call x1, Pallas kernels, clean_second(): pl.pallas_call(functools.partial(clean_second_kernel, ny, nx), in_specs=v...  4.43 us
    pallas_call x2, Pallas kernels, edge_powers(): pl.pallas_call(functools.partial(edge_kernel, ny, nx, phase, devices), in...  4.35 us
    pallas_call x1, Pallas kernels, load(): pl.pallas_call(functools.partial(load_kernel, gx, gy), in_specs=vmem(6) +...  3.85 us
    ppermute x1, starting transfers between devices, shards(): ye = lax.ppermute(ye, 'gy', even_pairs(gy))  3.03 us
    pallas_call x1, Pallas kernels, clean_first(): pl.pallas_call(functools.partial(clean_first_kernel, ny, nx), in_specs=vm...  2.5 us
    pallas_call x1, Pallas kernels, x_edges(): pl.pallas_call(edges_kernel, in_specs=hbm(7), out_specs=vmem(2), out_shap...  1.8 us
  transfers between devices with their start and end apart: 4, of which 0 were waited for; matrix products, arithmetic and copies ran while one was open for 0% of the time, Pallas kernels for 27%

profile of v8, /device:TPU:0, one launch (start us, length us, event | category | flops | bytes accessed | tf_op | source)
XLA Modules:
  0.0 47.0 jit_solution(2583868684269310580)
XLA Ops:
  0.6 0.0 copy-start
  0.6 0.0 copy-start.5
  0.7 0.0 copy-start.4
  0.7 0.0 copy-start.3
  0.7 0.0 copy-start.2
  0.7 0.0 copy-start.1
  0.7 1.8 %x_edges.1 = (f32[2,16,8,128]{3,2,1,0:T(8,128)S(1)}, f32[2,16,8,128]{3,2,1,0:T(8,128)S(1)}) custom-call(f32[8,64,16,128]{3,2,1,0:T(8,128)} %it_hbm.3, f32[64,16,128]{2,1,0:T(8,128)} %src_hbm.1, f32[64,16,128]{2,1,0:T(8,128)} %dg_hbm.1, f32[64,16,128]{2,1,0:T(8,128)} %fx_hbm.1, f32[64,16,128]{2,1,0:T(8,128)} %fy_hbm.1, f32[64,16,128]{2,1,0:T(8,128)} %fz_hbm.1, ...), custom_call_target="tpu_custom_call" | custom-call | tf_op jit(solution)/shard_map/x_edges/pallas_call | solution.py:127
  2.5 0.6 %collective-permute-start = (f32[2,16,8,128]{3,2,1,0:T(8,128)S(1)}, f32[2,16,8,128]{3,2,1,0:T(8,128)S(1)}, u32[]{:S(2)}, u32[]{:S(2)}) collective-permute-start(f32[2,16,8,128]{3,2,1,0:T(8,128)S(1)} %get-tuple-element.45), channel_id=1, source_target_pairs={{0,8},{8,0},{16,24},{24,16},{1,9},{9,1},{17,25},{25,17},{2,10},{10... | collective-permute-start | bytes 393224 | tf_op jit(solution)/shard_map/ppermute | solution.py:841
  3.1 0.7 %collective-permute-start.1 = (f32[2,16,8,128]{3,2,1,0:T(8,128)S(1)}, f32[2,16,8,128]{3,2,1,0:T(8,128)S(1)}, u32[]{:S(2)}, u32[]{:S(2)}) collective-permute-start(f32[2,16,8,128]{3,2,1,0:T(8,128)S(1)} %get-tuple-element.46), channel_id=1, source_target_pairs={{8,16},{16,8},{9,17},{17,9},{10,18},{18,10},{11,19},{19,11},{12,20... | collective-permute-start | bytes 393224 | tf_op jit(solution)/shard_map/ppermute | solution.py:840
  3.8 0.1 copy-done.1
  3.9 3.9 %load.1 = (f32[1280,128]{1,0:T(8,128)S(1)}, f32[1280,128]{1,0:T(8,128)S(1)}, f32[1280,128]{1,0:T(8,128)S(1)}, f32[1280,128]{1,0:T(8,128)S(1)}, f32[1280,128]{1,0...) custom-call(f32[8,64,16,128]{3,2,1,0:T(8,128)S(1)} %copy-done, ...), custom_call_target="tpu_custom_call" | custom-call | flops 4000000 | bytes 16000000 | tf_op jit(solution)/shard_map/load/pallas_call | solution.py:250
  7.7 0.0 collective-permute-done.xe_ref
  7.7 0.0 collective-permute-done.1.xo_ref
  7.7 1.4 %partial_residual.1 = (f32[1280,128]{1,0:T(8,128)S(1)}, f32[1280,128]{1,0:T(8,128)S(1)}, f32[1280,128]{1,0:T(8,128)S(1)}, f32[1280,128]{1,0:T(8,128)S(1)}, f32[1...) custom-call(f32[1280,128]{1,0:T(8,128)S(1)} %get-tuple-element.37.t_, ...), custom_call_target="tpu_custom_call", output_to_operand_aliasing={{0}: (0, {}), {1}: (1, {}), {2}: (2, {}), {3}: (3, {}), {4}... | custom-call | tf_op jit(solution)/shard_map/partial_residual/pallas_call | solution.py:347
  9.1 3.0 %collective-permute-start.2 = (f32[488,128]{1,0:T(8,128)S(1)}, f32[488,128]{1,0:T(8,128)S(1)}, u32[]{:S(2)}, u32[]{:S(2)}) collective-permute-start(f32[488,128]{1,0:T(8,128)S(1)} %get-tuple-element.58), channel_id=1, source_target_pairs={{0,1},{1,0},{2,3},{3,2},{4,5},{5,4},{6,7},{7,6},{8,9},{9,8},{10,11... | collective-permute-start | bytes 749576 | tf_op jit(solution)/shard_map/ppermute | solution.py:845
  12.2 2.5 %clean_first.1 = (f32[8,960,128]{2,1,0:T(8,128)S(1)}, f32[36,8,128]{2,1,0:T(8,128)S(1)}, f32[488,128]{1,0:T(8,128)S(1)}) custom-call(f32[1280,128]{1,0:T(8,128)S(1)} %get-tuple-element.47.t_ref, f32[1280,128]{1,0:T(8,128)S(1)} %get-tuple-element.48.s_ref, f32[1280,128]{1,0:T(8,128)S(1)} %get-tuple-element.49.fx_ref, ...), custom_call_target="tpu_custom_call", output_to_operand_aliasing={{0}: (7, {})} | custom-call | flops 20000000 | bytes 8000000 | tf_op jit(solution)/shard_map/clean_first/pallas_call | solution.py:470
  14.7 0.7 %collective-permute-start.3 = (f32[488,128]{1,0:T(8,128)S(1)}, f32[488,128]{1,0:T(8,128)S(1)}, u32[]{:S(2)}, u32[]{:S(2)}) collective-permute-start(f32[488,128]{1,0:T(8,128)S(1)} %get-tuple-element.61), channel_id=1, source_target_pairs={{1,2},{2,1},{3,4},{4,3},{5,6},{6,5},{9,10},{10,9},{11,12},{12,11},... | collective-permute-start | bytes 749576 | tf_op jit(solution)/shard_map/ppermute | solution.py:847
  15.3 4.4 %clean_second.1 = (f32[8,640,128]{2,1,0:T(8,128)S(1)}, f32[80,8,128]{2,1,0:T(8,128)S(1)}) custom-call(f32[1280,128]{1,0:T(8,128)S(1)} %get-tuple-element.47.t_ref, f32[1280,128]{1,0:T(8,128)S(1)} %get-tuple-element.49.fx_ref, f32[1280,128]{1,0:T(8,128)S(1)} %get-tuple-element.50.fy_ref, f32[1280,128]{1,0:T(8,128)S(1)} %get-tuple-element.51.dg_ref, ...), custom_call_target="tpu_custom_call" | custom-call | flops 40000000 | bytes 12000000 | tf_op jit(solution)/shard_map/clean_second/pallas_call | solution.py:489
  19.8 0.0 collective-permute-done.2.pack
  19.8 2.0 %edge_powers_0.1 = (f32[8,480,128]{2,1,0:T(8,128)S(1)}, f32[8,192,128]{2,1,0:T(8,128)S(1)}, f32[480,128]{1,0:T(8,128)S(1)}, f32[36,8,128]{2,1,0:T(8,128)S(1)}, f32[80,8,128]{2,1,0:T(8,128)S(1)}) custom-call(f32[1280,128]{1,0:T(8,128)S(1)} %get-tuple-element.47.t_ref, f32[1280,128]{1,0:T(8,128)S(1)} %get-tuple-element.48.s_ref, ...), custom_call_target="tpu_custom_call" | custom-call | flops 20000000 | bytes 8000000 | tf_op jit(solution)/shard_map/edge_powers_0/pallas_call | solution.py:648
  21.8 0.0 collective-permute-done.3.pack
  21.8 2.3 %edge_powers_1.1 = (f32[8,480,128]{2,1,0:T(8,128)S(1)}, f32[8,192,128]{2,1,0:T(8,128)S(1)}, f32[480,128]{1,0:T(8,128)S(1)}, f32[32,2,128]{2,1,0:T(2,128)S(1)}) custom-call(f32[1280,128]{1,0:T(8,128)S(1)} %get-tuple-element.47.t_ref, f32[1280,128]{1,0:T(8,128)S(1)} %get-tuple-element.48.s_ref, f32[1280,128]{1,0:T(8,128)S(1)} %get-tuple-element.49.fx_ref, ...), custom_call_target="tpu_custom_call" | custom-call | flops 20000000 | bytes 8000000 | tf_op jit(solution)/shard_map/edge_powers_1/pallas_call | solution.py:648
  24.2 15.9 %all_to_all.5.parts_ref = f32[32,2,128]{2,1,0:T(2,128)S(1)} all-to-all(f32[32,2,128]{2,1,0:T(2,128)S(1)} %get-tuple-element.62), channel_id=1, replica_groups=mesh['gx'=4,'gy'=8] {'gx','gy'}, dimensions={0} | all-to-all | bytes 65536 | tf_op jit(solution)/shard_map/all_to_all | solution.py:851
  40.1 6.9 %update.1 = (f32[8,1024,128]{2,1,0:T(8,128)}, f32[1024,128]{1,0:T(8,128)}) custom-call(f32[32,2,128]{2,1,0:T(2,128)S(1)} %all_to_all.5.parts_ref, f32[8,960,128]{2,1,0:T(8,128)S(1)} %get-tuple-element.55.p_out.pc_ref, f32[8,640,128]{2,1,0:T(8,128)S(1)} %get-tuple-element.63.qc_ref, f32[8,480,128]{2,1,0:T(8,128)S(1)} %get-tuple-element.64.p0_ref, ...), custom_call_target="tpu_custom_call" | custom-call | tf_op jit(solution)/shard_map/update/pallas_call | solution.py:814
  (5 shorter events, 0.0 us)
Async XLA Ops:
  0.6 3.1 %copy-start = (f32[8,64,16,128]{3,2,1,0:T(8,128)S(1)}, f32[8,64,16,128]{3,2,1,0:T(8,128)}, u32[]{:S(2)}) copy-start(f32[8,64,16,128]{3,2,1,0:T(8,128)} %it_hbm.3) | copy-start | bytes 12582916
  0.6 3.1 %copy-start.5 = (f32[64,16,128]{2,1,0:T(8,128)S(1)}, f32[64,16,128]{2,1,0:T(8,128)}, u32[]{:S(2)}) copy-start(f32[64,16,128]{2,1,0:T(8,128)} %fz_hbm.1) | copy-start | bytes 1572868
  0.7 3.1 %copy-start.4 = (f32[64,16,128]{2,1,0:T(8,128)S(1)}, f32[64,16,128]{2,1,0:T(8,128)}, u32[]{:S(2)}) copy-start(f32[64,16,128]{2,1,0:T(8,128)} %fy_hbm.1) | copy-start | bytes 1572868
  0.7 3.1 %copy-start.3 = (f32[64,16,128]{2,1,0:T(8,128)S(1)}, f32[64,16,128]{2,1,0:T(8,128)}, u32[]{:S(2)}) copy-start(f32[64,16,128]{2,1,0:T(8,128)} %fx_hbm.1) | copy-start | bytes 1572868
  0.7 3.1 %copy-start.2 = (f32[64,16,128]{2,1,0:T(8,128)S(1)}, f32[64,16,128]{2,1,0:T(8,128)}, u32[]{:S(2)}) copy-start(f32[64,16,128]{2,1,0:T(8,128)} %dg_hbm.1) | copy-start | bytes 1572868
  0.7 3.2 %copy-start.1 = (f32[64,16,128]{2,1,0:T(8,128)S(1)}, f32[64,16,128]{2,1,0:T(8,128)}, u32[]{:S(2)}) copy-start(f32[64,16,128]{2,1,0:T(8,128)} %src_hbm.1) | copy-start | bytes 1572868
  2.5 5.2 %collective-permute-start = (f32[2,16,8,128]{3,2,1,0:T(8,128)S(1)}, f32[2,16,8,128]{3,2,1,0:T(8,128)S(1)}, u32[]{:S(2)}, u32[]{:S(2)}) collective-permute-start(f32[2,16,8,128]{3,2,1,0:T(8,128)S(1)} %get-tuple-element.45), channel_id=1, source_target_pairs={{0,8},{8,0},{16,24},{24,16},{1,9},{9,1},{17,25},{25,17},{2,10},{10... | collective-permute-start | bytes 393224 | tf_op jit(solution)/shard_map/ppermute | solution.py:841
  3.1 4.7 %collective-permute-start.1 = (f32[2,16,8,128]{3,2,1,0:T(8,128)S(1)}, f32[2,16,8,128]{3,2,1,0:T(8,128)S(1)}, u32[]{:S(2)}, u32[]{:S(2)}) collective-permute-start(f32[2,16,8,128]{3,2,1,0:T(8,128)S(1)} %get-tuple-element.46), channel_id=1, source_target_pairs={{8,16},{16,8},{9,17},{17,9},{10,18},{18,10},{11,19},{19,11},{12,20... | collective-permute-start | bytes 393224 | tf_op jit(solution)/shard_map/ppermute | solution.py:840
  9.1 10.7 %collective-permute-start.2 = (f32[488,128]{1,0:T(8,128)S(1)}, f32[488,128]{1,0:T(8,128)S(1)}, u32[]{:S(2)}, u32[]{:S(2)}) collective-permute-start(f32[488,128]{1,0:T(8,128)S(1)} %get-tuple-element.58), channel_id=1, source_target_pairs={{0,1},{1,0},{2,3},{3,2},{4,5},{5,4},{6,7},{7,6},{8,9},{9,8},{10,11... | collective-permute-start | bytes 749576 | tf_op jit(solution)/shard_map/ppermute | solution.py:845
  14.7 7.2 %collective-permute-start.3 = (f32[488,128]{1,0:T(8,128)S(1)}, f32[488,128]{1,0:T(8,128)S(1)}, u32[]{:S(2)}, u32[]{:S(2)}) collective-permute-start(f32[488,128]{1,0:T(8,128)S(1)} %get-tuple-element.61), channel_id=1, source_target_pairs={{1,2},{2,1},{3,4},{4,3},{5,6},{6,5},{9,10},{10,9},{11,12},{12,11},... | collective-permute-start | bytes 749576 | tf_op jit(solution)/shard_map/ppermute | solution.py:847
